TPU v7x, 512 devices: a whole 4x8x8 slice. The times are simulated.
512 devices in a mesh: lat: 32 (over x_hi, z, core), lon: 16 (over y, x_lo).
Axes of the slice: x: 4 (x_hi: 2, x_lo: 2; x = x_hi * 2 + x_lo), y: 8, z: 8, core: 2. Of those that a mesh axis runs over, the one named last changes fastest.
Arguments:
- nodes: bfloat16 [32, 16, 128, 512], P('lat', 'lon'), may hold values from -6 to 6
- top_nodes: bfloat16 [1024, 512], P('lat'), may hold values from -6 to 6
- cotangent: bfloat16 [32, 16, 128, 512], P('lat', 'lon'), may hold values from -3 to 3
- w_src: bfloat16 [512, 512], replicated, may hold values from -0.25 to 0.25
- w_dst: bfloat16 [512, 512], replicated, may hold values from -0.25 to 0.25
- w_msg: bfloat16 [512, 512], replicated, may hold values from -0.25 to 0.25
- w_top: bfloat16 [512, 512], replicated, may hold values from -0.25 to 0.25
- src_code: int32 [32, 16, 1024], P('lat', 'lon'), may hold values from 0 to 8
- src_node: int32 [32, 16, 1024], P('lat', 'lon'), may hold values from 0 to 127
- dst_node: int32 [32, 16, 1024], P('lat', 'lon'), may hold values from 0 to 127
- edge_count: int32 [32, 16], P('lat', 'lon'), may hold values from 256 to 1024, as said below
- parent: int32 [32, 16, 128], P('lat', 'lon'), may hold values from 0 to 1023, as said below
Outputs:
- updated: bfloat16 [32, 16, 128, 512], P('lat', 'lon')
- weight_grads: bfloat16 [4, 512, 512], replicated
- d_top: bfloat16 [1024, 512], P(('lat', 'lon'))
Inputs may be any that keep to these rules, and one draw needn't show every extreme that they name: `edge_count`: some block has all 1024 slots live. Top-level nodes come in bands of 32, one band for the one block row. Node n of block (i, j) lies at longitude position p = j * 128 + n, and c = p * 32 // 2048 is the band column above it. Its parent is (i) * 32 + k for a column k of 0 to 31 with |k - c| <= 2.
All inputs are finite; a program needn't handle non-finite values.
Results may differ from a plain program's by a relative error of at most 0.006.
Values may be sent and summed in bfloat16 or wider, within the bound.
No kernel may reach another device: no remote copies, remote signals or barrier semaphores. Data moves between devices by JAX's collectives and lax.ppermute only.
A program may use at most 64 MiB of HBM per device.

v0:
```python
import math

import jax
import jax.numpy as jnp
from jax import lax
from jax.sharding import PartitionSpec as P


def extended_2(block, sides, width):
    for axis, dim in sides:
        count = lax.axis_size(axis)
        forward = [(i, i + 1) for i in range(count - 1)]
        backward = [(target, source) for source, target in forward]
        low = lax.ppermute(
            lax.slice_in_dim(block, block.shape[dim] - width, None, axis=dim), axis, forward
        )
        high = lax.ppermute(lax.slice_in_dim(block, 0, width, axis=dim), axis, backward)
        block = jnp.concatenate([low, block, high], axis=dim)
    return block


def silu_slope(values):
    sigmoid_v = jax.nn.sigmoid(values)
    return sigmoid_v * (1.0 + values * (1.0 - sigmoid_v))


def contract_rows(left_mat, right_mat):
    return lax.dot_general(
        left_mat, right_mat, (((0,), (0,)), ((), ())), preferred_element_type=jnp.float32
    )


def shards(
    nodes,
    top_nodes,
    cotangent,
    w_src,
    w_dst,
    w_msg,
    w_top,
    src_code,
    src_node,
    dst_node,
    edge_count,
    parent,
):
    block_rows, block_cols, block_size, features = nodes.shape
    block_count = block_rows * block_cols
    slot_count = src_code.shape[-1]
    ext_cols = block_cols + 2
    top_local = top_nodes.shape[0]
    owner_rows = top_local // lax.axis_size("lon")
    lon_index = lax.axis_index("lon")
    band_start = lax.axis_index("lat") * top_local
    parents = parent.reshape(-1)
    band_ids = parents - band_start
    window_ids = band_ids - (lon_index - 1) * owner_rows
    top_table = jnp.dot(top_nodes, w_top, preferred_element_type=jnp.float32).astype(jnp.bfloat16)
    table_rows = jnp.take(top_table, band_ids, axis=0)
    extended = extended_2(nodes, (("lat", 0), ("lon", 1)), 1)
    ext_flat = extended.reshape(-1, features)
    src_proj = jnp.dot(ext_flat, w_src, preferred_element_type=jnp.float32)
    local_rows = nodes.reshape(-1, features)
    dst_proj = jnp.dot(local_rows, w_dst, preferred_element_type=jnp.float32)
    block_row = lax.iota(jnp.int32, block_rows)[:, None, None]
    block_col = lax.iota(jnp.int32, block_cols)[None, :, None]
    src_idx = (
        ((block_row + src_code // 3) * ext_cols + block_col + src_code % 3) * block_size + src_node
    ).reshape(-1)
    dst_idx = ((block_row * block_cols + block_col) * block_size + dst_node).reshape(-1)
    live_slot = lax.iota(jnp.int32, slot_count)[None, None, :] < edge_count[:, :, None]
    node_ids = lax.iota(jnp.int32, block_size)[None, :, None]
    one_hot = ((dst_node == node_ids) & live_slot).astype(jnp.bfloat16)
    pre_act = jnp.take(src_proj, src_idx, axis=0) + jnp.take(dst_proj, dst_idx, axis=0)
    hidden = jax.nn.silu(pre_act).astype(jnp.bfloat16)
    msg_pre = jnp.dot(hidden, w_msg, preferred_element_type=jnp.float32)
    message = jax.nn.silu(msg_pre).astype(jnp.bfloat16)
    inflow = jnp.einsum(
        "bne,bed->bnd",
        one_hot,
        message.reshape(block_count, slot_count, features),
        preferred_element_type=jnp.float32,
    ).reshape(-1, features)
    node_pre = inflow + table_rows.astype(jnp.float32)
    updated = (
        (local_rows.astype(jnp.float32) + jax.nn.silu(node_pre))
        .astype(jnp.bfloat16)
        .reshape(nodes.shape)
    )
    node_grad = (cotangent.reshape(-1, features).astype(jnp.float32) * silu_slope(node_pre)).astype(
        jnp.bfloat16
    )
    msg_grad = jnp.einsum(
        "bne,bnd->bed",
        one_hot,
        node_grad.reshape(block_count, block_size, features),
        preferred_element_type=jnp.float32,
    ).reshape(-1, features)
    pre_grad = (msg_grad * silu_slope(msg_pre)).astype(jnp.bfloat16)
    grad_msg = contract_rows(hidden, pre_grad)
    hidden_grad = lax.dot_general(
        pre_grad, w_msg, (((1,), (1,)), ((), ())), preferred_element_type=jnp.float32
    )
    act_grad = (hidden_grad * silu_slope(pre_act)).astype(jnp.bfloat16)
    dst_grad = (
        jnp.einsum(
            "bne,bed->bnd",
            one_hot,
            act_grad.reshape(block_count, slot_count, features),
            preferred_element_type=jnp.float32,
        )
        .astype(jnp.bfloat16)
        .reshape(-1, features)
    )
    grad_dst = contract_rows(local_rows, dst_grad)
    grad_src = contract_rows(jnp.take(ext_flat, src_idx, axis=0), act_grad)
    window_cols = lax.iota(jnp.int32, 3 * owner_rows)
    picks = (window_ids[:, None] == window_cols[None, :]).astype(jnp.bfloat16)
    window_sum = contract_rows(picks, node_grad)
    rims = jnp.concatenate([window_sum[:owner_rows], window_sum[2 * owner_rows :]], axis=0)
    rim_parts = extended_2(rims, (("lon", 0),), owner_rows)
    table_sum = (
        window_sum[owner_rows : 2 * owner_rows]
        + rim_parts[:owner_rows]
        + rim_parts[3 * owner_rows :]
    )
    table_grad = table_sum.astype(jnp.bfloat16)
    top_mine = lax.dynamic_slice_in_dim(top_nodes, lon_index * owner_rows, owner_rows, 0)
    d_top = lax.dot_general(
        table_grad, w_top, (((1,), (1,)), ((), ())), preferred_element_type=jnp.float32
    ).astype(jnp.bfloat16)
    grad_top = contract_rows(top_mine, table_grad)
    summed = lax.psum((grad_src, grad_dst, grad_msg, grad_top), ("lat", "lon"))
    nodes_total = block_count * block_size * lax.axis_size("lat") * lax.axis_size("lon")
    grad_scale = 8.0 / math.sqrt(nodes_total)
    weight_grads = (jnp.stack(summed) * grad_scale).astype(jnp.bfloat16)
    return (updated, weight_grads, d_top)


def solution(mesh):
    placed = (
        P("lat", "lon", None, None),
        P("lat", None),
        P("lat", "lon", None, None),
        P(),
        P(),
        P(),
        P(),
        P("lat", "lon", None),
        P("lat", "lon", None),
        P("lat", "lon", None),
        P("lat", "lon"),
        P("lat", "lon", None),
    )
    return jax.shard_map(
        shards,
        mesh=mesh,
        in_specs=placed,
        out_specs=(P("lat", "lon", None, None), P(), P(("lat", "lon"), None)),
        check_vma=False,
    )
```

profile of v0, /device:TPU:1, one launch (start us, length us, event | category | flops | bytes accessed | tf_op | source)
XLA Modules:
  0.0 387.7 jit_solution(804594889232757917)
XLA Ops:
  7.2 0.0 copy-start
  7.2 0.0 all-reduce.3.cloned.1.call-start
  7.2 8.9 %collective-permute-start.1 = (bf16[1,1,128,512]{3,2,1,0:T(8,128)(2,1)}, bf16[1,1,128,512]{3,2,1,0:T(8,128)(2,1)S(1)}, u32[]{:S(2)}, u32[]{:S(2)}) collective-permute-start(bf16[1,1,128,512]{3,2,1,0:T(8,128)(2,1)} %param.12), channel_id=1, source_target_pairs={{16,0},{32,16},{48,32},{64,48},{80,64},{96,80},{112,96},{128,112},... | collective-permute-start | bytes 393224 | tf_op jit(solution)/shard_map/ppermute | solution.py:17
  16.2 1.9 collective-permute-start
  18.1 0.7 compare_select_fusion
  18.8 0.7 compare_select_fusion.1
  19.5 1.3 fusion.20
  20.9 0.7 fusion.28
  21.6 1.2 convolution_convert_fusion.1
  22.8 1.3 compare_and_fusion.2
  24.7 1.5 gather_fusion.2
  26.2 4.9 %gather_fusion.1 = f32[1024,512]{1,0:T(8,128)} fusion(f32[128,512]{1,0:T(8,128)S(1)} %fusion.20, s32[1024]{0:T(1024)S(1)} %get-tuple-element.14), kind=kCustom, calls=%fused_computation.1 | custom fusion | bytes 4198400 | tf_op jit(solution)/shard_map/jit(_take)/gather | solution.py:74
  31.1 0.6 iota_compare_fusion.3
  31.7 0.0 collective-permute-done.1
  31.7 1.3 collective-permute-start.3
  33.0 4.0 %collective-permute-start.2 = (bf16[3,1,128,512]{3,2,1,0:T(8,128)(2,1)S(1)}, bf16[3,1,128,512]{3,2,1,0:T(8,128)(2,1)S(1)}, u32[]{:S(2)}, u32[]{:S(2)}) collective-permute-start(bf16[3,1,128,512]{3,2,1,0:T(8,128)(2,1)S(1)} %constant_dynamic-update-slice_fusion), channel_id=1, source_target_pairs={{0,1},{1,2},{2,3},{3,4},{4,5},{5,6},{6,7},{7,8},{8,9},{9,10},{10,1... | collective-permute-start | bytes 1179656 | tf_op jit(solution)/shard_map/ppermute | solution.py:14
  37.1 0.5 bitcast_subtract_fusion
  37.6 6.2 %collective-permute-done.3 = bf16[3,1,128,512]{3,2,1,0:T(8,128)(2,1)S(1)} collective-permute-done((bf16[3,1,128,512]{3,2,1,0:T(8,128)(2,1)S(1)}, bf16[3,1,128,512]{3,2,1,0:T(8,128)(2,1)S(1)}, u32[]{:S(2)}, u32[]{:S(2)}) %collective-permute-start.3) | collective-permute-done | bytes 393248 | tf_op jit(solution)/shard_map/ppermute | solution.py:17
  43.8 4.8 %collective-permute-done.2 = bf16[3,1,128,512]{3,2,1,0:T(8,128)(2,1)S(1)} collective-permute-done((bf16[3,1,128,512]{3,2,1,0:T(8,128)(2,1)S(1)}, bf16[3,1,128,512]{3,2,1,0:T(8,128)(2,1)S(1)}, u32[]{:S(2)}, u32[]{:S(2)}) %collective-permute-start.2) | collective-permute-done | bytes 393248 | tf_op jit(solution)/shard_map/ppermute | solution.py:14
  48.6 0.1 pad_maximum_fusion
  48.7 1.0 copy-done.1
  49.8 5.1 %gather_fusion.3 = bf16[1024,512]{1,0:T(8,128)(2,1)} fusion(bf16[1152,512]{1,0:T(8,128)(2,1)S(1)} %bitcast.58, s32[1024]{0:T(1024)S(1)} %broadcast_clamp_fusion.1), kind=kCustom, calls=%fused_computation.3 | custom fusion | bytes 2101248 | tf_op jit(solution)/shard_map/jit(_take)/gather | solution.py:116
  54.8 2.0 fusion.33
  56.9 4.9 %gather_fusion = f32[1024,512]{1,0:T(8,128)} fusion(f32[1152,512]{1,0:T(8,128)S(1)} %fusion.33, s32[1024]{0:T(1024)S(1)} %broadcast_clamp_fusion.1), kind=kCustom, calls=%fused_computation | custom fusion | bytes 4198400 | tf_op jit(solution)/shard_map/jit(_take)/gather | solution.py:74
  61.8 2.6 multiply_convert_fusion.3
  64.4 0.0 copy-start.8
  64.4 0.0 copy-start.11
  64.5 0.7 fusion.34
  65.2 0.2 copy-done.8
  65.3 1.5 fusion.10
  66.8 0.1 fusion.9
  66.9 0.0 copy-start.2
  66.9 0.9 multiply_convert_fusion.1
  67.9 0.7 copy-done.2
  68.5 0.6 copy-done.3
  69.1 1.6 multiply_convert_fusion
  70.8 1.7 convolution_bitcast_fusion.1
  72.5 0.2 fusion.22
  72.8 4.1 %collective-permute-start.4 = (f32[2,512]{1,0:T(2,128)S(1)}, f32[2,512]{1,0:T(2,128)S(1)}, u32[]{:S(2)}, u32[]{:S(2)}) collective-permute-start(f32[2,512]{1,0:T(2,128)S(1)} %get-tuple-element.9), channel_id=1, source_target_pairs={{0,1},{1,2},{2,3},{3,4},{4,5},{5,6},{6,7},{7,8},{8,9},{9,10},{10,1... | collective-permute-start | bytes 12296 | tf_op jit(solution)/shard_map/ppermute | solution.py:14
  76.9 1.3 collective-permute-start.5
  78.2 1.8 convolution_bitcast_fusion.3
  80.0 1.6 convolution_bitcast_fusion.2
  81.6 2.0 convolution_bitcast_fusion
  83.6 0.0 all-reduce.3.cloned.1.call-update
  83.7 1.0 copy-done.4
  84.7 0.8 convolution_convert_fusion.2
  85.5 291.3 %all-reduce.3.cloned.1.call-done = (f32[1,512,512]{2,1,0:T(8,128)}, f32[1,512,512]{2,1,0:T(8,128)}, f32[1,512,512]{2,1,0:T(8,128)}, f32[1,512,512]{2,1,0:T(8,128)}) async-done(((f32[1,512,512]{2,1,0:T(8,128)}, f32[1,512,512]{2,1,0:T(8,128)}, f32[1,512,512]{2,1,0:T(8,128)}, f32[1,512,512]{2,1,0:T(8,128)}), (f32[1,512,512]{2,1,0:T(8,128)}, f32[1,512,512]{2,1,0:T(8,128)}, f32[1,512,512]{2,1,0:T(8,128)}, ...) | async-done | bytes 4194320 | tf_op jit(solution)/shard_map/psum | solution.py:133
  376.8 4.1 %fusion = bf16[4,512,512]{2,1,0:T(8,128)(2,1)} fusion(f32[1,512,512]{2,1,0:T(8,128)} %get-tuple-element.3, f32[1,512,512]{2,1,0:T(8,128)} %get-tuple-element.4, f32[1,512,512]{2,1,0:T(8,128)} %get-tuple-element.5, f32[1,512,512]{2,1,0:T(8,128)} %get-tuple-element.6), kind=kLoop, calls=%fused_computation.5 | loop fusion | flops 5242880 | bytes 6291456 | tf_op jit(solution)/shard_map/convert_element_type | solution.py:136
  (32 shorter events, 0.1 us)
Async XLA Ops:
  7.2 57.2 %copy-start = (bf16[512,512]{1,0:T(8,128)(2,1)S(1)}, bf16[512,512]{1,0:T(8,128)(2,1)}, u32[]{:S(2)}) copy-start(bf16[512,512]{1,0:T(8,128)(2,1)} %param.17) | copy-start | bytes 1572868
  7.2 369.6 %all-reduce.3.cloned.1.call-start = ((), (), s32[]{:S(2)}) async-start(), calls=%async_computation | async-start | bytes 8388608 | tf_op jit(solution)/shard_map/psum | solution.py:133
  7.2 24.5 %collective-permute-start.1 = (bf16[1,1,128,512]{3,2,1,0:T(8,128)(2,1)}, bf16[1,1,128,512]{3,2,1,0:T(8,128)(2,1)S(1)}, u32[]{:S(2)}, u32[]{:S(2)}) collective-permute-start(bf16[1,1,128,512]{3,2,1,0:T(8,128)(2,1)} %param.12), channel_id=1, source_target_pairs={{16,0},{32,16},{48,32},{64,48},{80,64},{96,80},{112,96},{128,112},... | collective-permute-start | bytes 393224 | tf_op jit(solution)/shard_map/ppermute | solution.py:17
  16.2 15.5 %collective-permute-start = (bf16[1,1,128,512]{3,2,1,0:T(8,128)(2,1)}, bf16[1,1,128,512]{3,2,1,0:T(8,128)(2,1)S(1)}, u32[]{:S(2)}, u32[]{:S(2)}) collective-permute-start(bf16[1,1,128,512]{3,2,1,0:T(8,128)(2,1)} %param.12), channel_id=1, source_target_pairs={{0,16},{16,32},{32,48},{48,64},{64,80},{80,96},{96,112},{112,128},... | collective-permute-start | bytes 393224 | tf_op jit(solution)/shard_map/ppermute | solution.py:14
  26.2 5.5 %copy-start.5 = (bf16[1,1,128,512]{3,2,1,0:T(8,128)(2,1)S(1)}, bf16[1,1,128,512]{3,2,1,0:T(8,128)(2,1)}, u32[]{:S(2)}) copy-start(bf16[1,1,128,512]{3,2,1,0:T(8,128)(2,1)} %param.12) | copy-start | bytes 393220
  26.2 10.8 %copy-start.12 = (s32[1,1,128]{2,1,0:T(1,128)S(1)}, s32[1,1,128]{2,1,0:T(1,128)}, u32[]{:S(2)}) copy-start(s32[1,1,128]{2,1,0:T(1,128)} %param.23) | copy-start | bytes 1540
  26.2 11.4 %copy-start.10 = (s32[1,1,1024]{2,1,0:T(1,128)S(1)}, s32[1,1,1024]{2,1,0:T(1,128)}, u32[]{:S(2)}) copy-start(s32[1,1,1024]{2,1,0:T(1,128)} %param.21) | copy-start | bytes 12292
  31.7 12.1 %collective-permute-start.3 = (bf16[3,1,128,512]{3,2,1,0:T(8,128)(2,1)S(1)}, bf16[3,1,128,512]{3,2,1,0:T(8,128)(2,1)S(1)}, u32[]{:S(2)}, u32[]{:S(2)}) collective-permute-start(bf16[3,1,128,512]{3,2,1,0:T(8,128)(2,1)S(1)} %constant_dynamic-update-slice_fusion), channel_id=1, source_target_pairs={{1,0},{2,1},{3,2},{4,3},{5,4},{6,5},{7,6},{8,7},{9,8},{10,9},{11,1... | collective-permute-start | bytes 1179656 | tf_op jit(solution)/shard_map/ppermute | solution.py:17
  33.0 15.6 %collective-permute-start.2 = (bf16[3,1,128,512]{3,2,1,0:T(8,128)(2,1)S(1)}, bf16[3,1,128,512]{3,2,1,0:T(8,128)(2,1)S(1)}, u32[]{:S(2)}, u32[]{:S(2)}) collective-permute-start(bf16[3,1,128,512]{3,2,1,0:T(8,128)(2,1)S(1)} %constant_dynamic-update-slice_fusion), channel_id=1, source_target_pairs={{0,1},{1,2},{2,3},{3,4},{4,5},{5,6},{6,7},{7,8},{8,9},{9,10},{10,1... | collective-permute-start | bytes 1179656 | tf_op jit(solution)/shard_map/ppermute | solution.py:14
  48.7 1.0 copy-start.1
  49.8 5.1 %copy-start.7 = (bf16[512,512]{1,0:T(8,128)(2,1)S(1)}, bf16[512,512]{1,0:T(8,128)(2,1)}, u32[]{:S(2)}) copy-start(bf16[512,512]{1,0:T(8,128)(2,1)} %param.15) | copy-start | bytes 1572868
  64.4 0.9 copy-start.8
  64.4 0.9 copy-start.11
  64.4 0.9 copy-start.14
  65.3 1.5 copy-start.9
  66.9 1.6 copy-start.2
  66.9 2.2 copy-start.3
  70.8 1.8 copy-start.13
  70.8 7.4 %copy-start.6 = (bf16[1024,512]{1,0:T(8,128)(2,1)S(1)}, bf16[1024,512]{1,0:T(8,128)(2,1)}, u32[]{:S(2)}) copy-start(bf16[1024,512]{1,0:T(8,128)(2,1)} %gather_fusion.3) | copy-start | bytes 3145732
  72.8 8.8 %collective-permute-start.4 = (f32[2,512]{1,0:T(2,128)S(1)}, f32[2,512]{1,0:T(2,128)S(1)}, u32[]{:S(2)}, u32[]{:S(2)}) collective-permute-start(f32[2,512]{1,0:T(2,128)S(1)} %get-tuple-element.9), channel_id=1, source_target_pairs={{0,1},{1,2},{2,3},{3,4},{4,5},{5,6},{6,7},{7,8},{8,9},{9,10},{10,1... | collective-permute-start | bytes 12296 | tf_op jit(solution)/shard_map/ppermute | solution.py:14
  76.9 4.7 %collective-permute-start.5 = (f32[2,512]{1,0:T(2,128)S(1)}, f32[2,512]{1,0:T(2,128)S(1)}, u32[]{:S(2)}, u32[]{:S(2)}) collective-permute-start(f32[2,512]{1,0:T(2,128)S(1)} %get-tuple-element.10), channel_id=1, source_target_pairs={{1,0},{2,1},{3,2},{4,3},{5,4},{6,5},{7,6},{8,7},{9,8},{10,9},{11,1... | collective-permute-start | bytes 12296 | tf_op jit(solution)/shard_map/ppermute | solution.py:17
  83.6 1.0 copy-start.4
Sparse Core Ops, SparseCore 0:
  83.8 292.9 all-reduce.2
where the time goes:
time: 389 us; the launch traced here: 388 us
  waiting for transfers between devices  302 us (78%)
  starting transfers between devices  21.6 us (6%)
  local copies, waits for them, and re-layouts  19.9 us (5%)
  matrix products  17.5 us (4%)
  between operations  14.9 us (4%)
  other arithmetic  11.4 us (3%)
    psum x1, waiting for transfers between devices, shards(): summed = lax.psum((grad_src, grad_dst, grad_msg, grad_top), ('lat', 'lon'))  291 us
    ppermute x3, starting transfers between devices, extended_2(): lax.ppermute(lax.slice_in_dim(block, 0, width, axis=dim), axis, backward)  11.5 us
    ppermute x3, starting transfers between devices, extended_2(): lax.ppermute(lax.slice_in_dim(block, block.shape[dim] - width, None, axis...  10 us
  transfers between devices with their start and end apart: 7, of which 3 were waited for; matrix products, arithmetic and copies ran while one was open for 5% of the time, Pallas kernels for 0%

commit v1 on v0

--- a/solution.py
+++ b/solution.py
@@ -3,7 +3,11 @@
 import jax
 import jax.numpy as jnp
 from jax import lax
+from jax.sharding import Mesh
 from jax.sharding import PartitionSpec as P
+
+LAT = ("x_hi", "z_hi", "z_lo", "core")
+LON = ("y_hi", "y_lo", "x_lo")
 
 
 def extended_2(block, sides, width):
@@ -30,6 +34,28 @@
     )
 
 
+NEAR = ("x_hi", "z_lo", "y_lo", "x_lo")
+FAR = ("z_hi", "y_hi")
+
+
+def all_sum(stack, scale):
+    part = stack.astype(jnp.bfloat16)
+    for axes in (("core",), NEAR, FAR):
+        count = lax.axis_size(axes)
+        part = lax.all_to_all(part, axes, 0, 0, tiled=True)
+        part = jnp.sum(
+            part.reshape(count, -1, part.shape[-1]).astype(jnp.float32), axis=0
+        )
+        if axes != FAR:
+            part = part.astype(jnp.bfloat16)
+    part = (part * scale).astype(jnp.bfloat16)
+    for axes in (FAR, NEAR, ("core",)):
+        count = lax.axis_size(axes)
+        copies = jnp.broadcast_to(part[None], (count,) + part.shape).reshape(-1, part.shape[-1])
+        part = lax.all_to_all(copies, axes, 0, 0, tiled=True)
+    return part
+
+
 def shards(
     nodes,
     top_nodes,
@@ -49,15 +75,15 @@
     slot_count = src_code.shape[-1]
     ext_cols = block_cols + 2
     top_local = top_nodes.shape[0]
-    owner_rows = top_local // lax.axis_size("lon")
-    lon_index = lax.axis_index("lon")
-    band_start = lax.axis_index("lat") * top_local
+    owner_rows = top_local // lax.axis_size(LON)
+    lon_index = lax.axis_index(LON)
+    band_start = lax.axis_index(LAT) * top_local
     parents = parent.reshape(-1)
     band_ids = parents - band_start
     window_ids = band_ids - (lon_index - 1) * owner_rows
     top_table = jnp.dot(top_nodes, w_top, preferred_element_type=jnp.float32).astype(jnp.bfloat16)
     table_rows = jnp.take(top_table, band_ids, axis=0)
-    extended = extended_2(nodes, (("lat", 0), ("lon", 1)), 1)
+    extended = extended_2(nodes, ((LAT, 0), (LON, 1)), 1)
     ext_flat = extended.reshape(-1, features)
     src_proj = jnp.dot(ext_flat, w_src, preferred_element_type=jnp.float32)
     local_rows = nodes.reshape(-1, features)
@@ -118,7 +144,7 @@
     picks = (window_ids[:, None] == window_cols[None, :]).astype(jnp.bfloat16)
     window_sum = contract_rows(picks, node_grad)
     rims = jnp.concatenate([window_sum[:owner_rows], window_sum[2 * owner_rows :]], axis=0)
-    rim_parts = extended_2(rims, (("lon", 0),), owner_rows)
+    rim_parts = extended_2(rims, ((LON, 0),), owner_rows)
     table_sum = (
         window_sum[owner_rows : 2 * owner_rows]
         + rim_parts[:owner_rows]
@@ -130,32 +156,42 @@
         table_grad, w_top, (((1,), (1,)), ((), ())), preferred_element_type=jnp.float32
     ).astype(jnp.bfloat16)
     grad_top = contract_rows(top_mine, table_grad)
-    summed = lax.psum((grad_src, grad_dst, grad_msg, grad_top), ("lat", "lon"))
-    nodes_total = block_count * block_size * lax.axis_size("lat") * lax.axis_size("lon")
+    nodes_total = block_count * block_size * lax.axis_size(LAT) * lax.axis_size(LON)
     grad_scale = 8.0 / math.sqrt(nodes_total)
-    weight_grads = (jnp.stack(summed) * grad_scale).astype(jnp.bfloat16)
+    stack = jnp.stack([grad_src, grad_dst, grad_msg, grad_top])
+    lanes = 128
+    tiles = features // lanes
+    by_lane_tile = stack.reshape(4 * features, tiles, lanes).transpose(1, 0, 2).reshape(-1, lanes)
+    summed = all_sum(by_lane_tile, grad_scale)
+    weight_grads = (
+        summed.reshape(tiles, 4, features, lanes).transpose(1, 2, 0, 3).reshape(4, features, features)
+    )
     return (updated, weight_grads, d_top)
 
 
 def solution(mesh):
+    fine = Mesh(
+        mesh.devices.reshape(2, 4, 2, 2, 4, 2, 2),
+        ("x_hi", "z_hi", "z_lo", "core", "y_hi", "y_lo", "x_lo"),
+    )
     placed = (
-        P("lat", "lon", None, None),
-        P("lat", None),
-        P("lat", "lon", None, None),
+        P(LAT, LON, None, None),
+        P(LAT, None),
+        P(LAT, LON, None, None),
         P(),
         P(),
         P(),
         P(),
-        P("lat", "lon", None),
-        P("lat", "lon", None),
-        P("lat", "lon", None),
-        P("lat", "lon"),
-        P("lat", "lon", None),
+        P(LAT, LON, None),
+        P(LAT, LON, None),
+        P(LAT, LON, None),
+        P(LAT, LON),
+        P(LAT, LON, None),
     )
     return jax.shard_map(
         shards,
-        mesh=mesh,
+        mesh=fine,
         in_specs=placed,
-        out_specs=(P("lat", "lon", None, None), P(), P(("lat", "lon"), None)),
+        out_specs=(P(LAT, LON, None, None), P(), P(LAT + LON, None)),
         check_vma=False,
     )

time: 389 us -> 185 us (0.48)
  waiting for transfers between devices: 302 us -> 24.1 us
  blocking collectives: 0 us -> 79.1 us
  between operations: 14.9 us -> 1.65 us
  local copies, waits for them, and re-layouts: 19.9 us -> 29.8 us
    psum x1 -> x0, waiting for transfers between devices: 291 us -> none  [shards(): summed = lax.psum((grad_src, grad_dst, grad_msg, grad_top), ('lat', 'lon'))]
    all_to_all x0 -> x5, blocking collectives: none -> 79.1 us  [the longest x3 54.8 us: all_sum(): part = lax.all_to_all(part, axes, 0, 0, tiled=True)]
    all_to_all x0 -> x1, waiting for transfers between devices: none -> 11.8 us  [all_sum(): part = lax.all_to_all(copies, axes, 0, 0, tiled=True)]
    convert_element_type x1, other arithmetic: 4.07 us -> 0.01 us  [all_sum(): part = (part * scale).astype(jnp.bfloat16)]
  transfers between devices with their start and end apart: 7 -> 7, of which waited for: 3 -> 4; matrix products, arithmetic and copies ran while one was open for 5% -> 8% of each run, Pallas kernels for 0% -> 0%
where the time goes in v1:
time: 185 us; the launch traced here: 184 us
  blocking collectives  79.1 us (43%)
  local copies, waits for them, and re-layouts  29.8 us (16%)
  starting transfers between devices  25.2 us (14%)
  waiting for transfers between devices  24.1 us (13%)
  matrix products  15.3 us (8%)
  other arithmetic  8.97 us (5%)
    all_to_all x3, blocking collectives, all_sum(): part = lax.all_to_all(part, axes, 0, 0, tiled=True)  54.8 us
    all_to_all x2, blocking collectives, all_sum(): part = lax.all_to_all(copies, axes, 0, 0, tiled=True)  24.2 us
    all_to_all x1, waiting for transfers between devices, all_sum(): part = lax.all_to_all(copies, axes, 0, 0, tiled=True)  11.8 us
    ppermute x3, starting transfers between devices, extended_2(): lax.ppermute(lax.slice_in_dim(block, 0, width, axis=dim), axis, backward)  11.5 us
    ppermute x3, starting transfers between devices, extended_2(): lax.ppermute(lax.slice_in_dim(block, block.shape[dim] - width, None, axis...  10 us
    ppermute x3, waiting for transfers between devices, extended_2(): lax.ppermute(lax.slice_in_dim(block, 0, width, axis=dim), axis, backward)  7.51 us
    unnamed x23, local copies, waits for them, and re-layouts  6.52 us
    gather x1, local copies, waits for them, and re-layouts, shards(): grad_src = contract_rows(jnp.take(ext_flat, src_idx, axis=0), act_grad)  5.06 us
  transfers between devices with their start and end apart: 7, of which 4 were waited for; matrix products, arithmetic and copies ran while one was open for 8% of the time, Pallas kernels for 0%

profile of v1, /device:TPU:1, one launch (start us, length us, event | category | flops | bytes accessed | tf_op | source)
XLA Modules:
  0.0 184.1 jit_solution(15758382152739934268)
XLA Ops:
  0.6 8.9 %collective-permute-start.1 = (bf16[1,1,128,512]{3,2,1,0:T(8,128)(2,1)}, bf16[1,1,128,512]{3,2,1,0:T(8,128)(2,1)S(1)}, u32[]{:S(2)}, u32[]{:S(2)}) collective-permute-start(bf16[1,1,128,512]{3,2,1,0:T(8,128)(2,1)} %param.12), channel_id=1, source_target_pairs={{16,0},{32,16},{48,32},{64,48},{80,64},{96,80},{112,96},{128,112},... | collective-permute-start | bytes 393224 | tf_op jit(solution)/shard_map/ppermute | solution.py:21
  9.6 1.9 %collective-permute-start = (bf16[1,1,128,512]{3,2,1,0:T(8,128)(2,1)}, bf16[1,1,128,512]{3,2,1,0:T(8,128)(2,1)S(1)}, u32[]{:S(2)}, u32[]{:S(2)}) collective-permute-start(bf16[1,1,128,512]{3,2,1,0:T(8,128)(2,1)} %param.12), channel_id=1, source_target_pairs={{0,16},{16,32},{32,48},{48,64},{64,80},{80,96},{96,112},{112,128},... | collective-permute-start | bytes 393224 | tf_op jit(solution)/shard_map/ppermute | solution.py:18
  11.5 0.7 compare_select_fusion
  12.2 0.7 compare_select_fusion.1
  13.0 1.3 fusion.23
  14.3 0.7 fusion.31
  15.0 1.2 convolution_convert_fusion.5
  16.2 0.7 compare_and_fusion.2
  17.6 0.8 gather_fusion.2
  18.5 4.9 %gather_fusion.1 = f32[1024,512]{1,0:T(8,128)} fusion(f32[128,512]{1,0:T(8,128)S(1)} %fusion.23, s32[1024]{0:T(1024)S(1)} %get-tuple-element.16), kind=kCustom, calls=%fused_computation.1 | custom fusion | bytes 4198400 | tf_op jit(solution)/shard_map/jit(_take)/gather | solution.py:100
  23.4 1.3 collective-permute-start.3
  24.7 4.0 %collective-permute-start.2 = (bf16[3,1,128,512]{3,2,1,0:T(8,128)(2,1)S(1)}, bf16[3,1,128,512]{3,2,1,0:T(8,128)(2,1)S(1)}, u32[]{:S(2)}, u32[]{:S(2)}) collective-permute-start(bf16[3,1,128,512]{3,2,1,0:T(8,128)(2,1)S(1)} %constant_dynamic-update-slice_fusion), channel_id=1, source_target_pairs={{0,1},{1,2},{2,3},{3,4},{4,5},{5,6},{6,7},{7,8},{8,9},{9,10},{10,1... | collective-permute-start | bytes 1179656 | tf_op jit(solution)/shard_map/ppermute | solution.py:18
  28.8 6.7 %collective-permute-done.3 = bf16[3,1,128,512]{3,2,1,0:T(8,128)(2,1)S(1)} collective-permute-done((bf16[3,1,128,512]{3,2,1,0:T(8,128)(2,1)S(1)}, bf16[3,1,128,512]{3,2,1,0:T(8,128)(2,1)S(1)}, u32[]{:S(2)}, u32[]{:S(2)}) %collective-permute-start.3) | collective-permute-done | bytes 393248 | tf_op jit(solution)/shard_map/ppermute | solution.py:21
  35.5 4.8 %collective-permute-done.2 = bf16[3,1,128,512]{3,2,1,0:T(8,128)(2,1)S(1)} collective-permute-done((bf16[3,1,128,512]{3,2,1,0:T(8,128)(2,1)S(1)}, bf16[3,1,128,512]{3,2,1,0:T(8,128)(2,1)S(1)}, u32[]{:S(2)}, u32[]{:S(2)}) %collective-permute-start.2) | collective-permute-done | bytes 393248 | tf_op jit(solution)/shard_map/ppermute | solution.py:18
  40.4 1.0 copy-done.1
  41.5 5.1 %gather_fusion.3 = bf16[1024,512]{1,0:T(8,128)(2,1)} fusion(bf16[1152,512]{1,0:T(8,128)(2,1)S(1)} %bitcast.69, s32[1024]{0:T(1024)S(1)} %broadcast_clamp_fusion.1), kind=kCustom, calls=%fused_computation.3 | custom fusion | bytes 2101248 | tf_op jit(solution)/shard_map/jit(_take)/gather | solution.py:142
  46.5 2.2 %fusion.36 = f32[1152,512]{1,0:T(8,128)S(1)} fusion(bf16[1152,512]{1,0:T(8,128)(2,1)} %bitcast.70, bf16[512,512]{1,0:T(8,128)(2,1)} %param.15), kind=kOutput, calls=%fused_computation.80 | convolution fusion | flops 603979776 | bytes 4063232 | tf_op jit(solution)/shard_map/dot_general | solution.py:88
  48.7 4.9 %gather_fusion = f32[1024,512]{1,0:T(8,128)} fusion(f32[1152,512]{1,0:T(8,128)S(1)} %fusion.36, s32[1024]{0:T(1024)S(1)} %broadcast_clamp_fusion.1), kind=kCustom, calls=%fused_computation | custom fusion | bytes 4198400 | tf_op jit(solution)/shard_map/jit(_take)/gather | solution.py:100
  53.6 2.6 %multiply_convert_fusion.3 = bf16[1024,512]{1,0:T(8,128)(2,1)S(1)} fusion(f32[1024,512]{1,0:T(8,128)} %gather_fusion.1, pred[1024]{0:T(1024)(128)(4,1)S(1)} %get-tuple-element.17, f32[1024,512]{1,0:T(8,128)} %gather_fusion, pred[1024]{0:T(1024)(128)(4,1)S(1)} %get-tuple-element.18), kind=kLoop, calls=%fused_computation.9 | loop fusion | flops 4194304 | bytes 5244928 | tf_op jit(solution)/shard_map/convert_element_type | solution.py:101
  56.3 0.7 fusion.37
  57.0 1.5 fusion.13
  58.6 0.9 multiply_convert_fusion.1
  59.5 0.7 copy-done.2
  60.2 0.6 copy-done.3
  60.8 1.6 multiply_convert_fusion
  62.4 1.5 fusion.1
  64.0 0.2 fusion.25
  64.2 4.1 %collective-permute-start.4 = (f32[2,512]{1,0:T(2,128)S(1)}, f32[2,512]{1,0:T(2,128)S(1)}, u32[]{:S(2)}, u32[]{:S(2)}) collective-permute-start(f32[2,512]{1,0:T(2,128)S(1)} %get-tuple-element.11), channel_id=1, source_target_pairs={{0,1},{1,2},{2,3},{3,4},{4,5},{5,6},{6,7},{7,8},{8,9},{9,10},{10,1... | collective-permute-start | bytes 12296 | tf_op jit(solution)/shard_map/ppermute | solution.py:18
  68.3 1.3 collective-permute-start.5
  69.6 1.6 fusion
  71.3 0.6 fusion.3
  71.9 0.8 collective-permute-done.5
  72.7 1.0 fusion.2
  73.8 1.5 pad_maximum_fusion
  75.2 2.0 %convert_element_type.93 = bf16[2048,4,128]{2,1,0:T(4,128)(2,1)} reshape(bf16[4,512,512]{2,1,0:T(8,128)(2,1)S(1)} %pad_maximum_fusion) | data formatting | bytes 4194304 | tf_op jit(solution)/shard_map/convert_element_type | solution.py:42
  77.2 1.9 %copy.23 = bf16[2048,4,128]{2,0,1:T(8,128)(2,1)S(1)} copy(bf16[2048,4,128]{2,1,0:T(4,128)(2,1)} %convert_element_type.93) | data formatting | bytes 4194304 | tf_op jit(solution)/shard_map/convert_element_type | solution.py:42
  79.1 7.0 %all_to_all.42 = bf16[2,4096,128]{2,1,0:T(8,128)(2,1)S(1)} all-to-all(bf16[2,4096,128]{2,1,0:T(8,128)(2,1)S(1)} %bitcast.71), channel_id=1, replica_groups=mesh['x_hi'=2,'z_hi'=4,'z_lo'=2,'core'=2,'y_hi'=4,'y_lo'=2,'x_lo'=2] {'c..., dimensions={0} | all-to-all | bytes 4194304 | tf_op jit(solution)/shard_map/all_to_all | solution.py:45
  86.1 1.6 reduce_sum.33
  87.7 22.6 %all_to_all.43 = bf16[16,256,128]{2,1,0:T(8,128)(2,1)S(1)} all-to-all(bf16[16,256,128]{2,1,0:T(8,128)(2,1)} %bitcast.75), channel_id=1, replica_groups=mesh['x_hi'=2,'z_hi'=4,'z_lo'=2,'core'=2,'y_hi'=4,'y_lo'=2,'x_lo'=2] {'x..., dimensions={0} | all-to-all | bytes 2097152 | tf_op jit(solution)/shard_map/all_to_all | solution.py:45
  110.5 25.2 %all_to_all.44 = bf16[16,16,128]{2,1,0:T(8,128)(2,1)S(1)} all-to-all(bf16[16,16,128]{2,1,0:T(8,128)(2,1)S(1)} %bitcast.76), channel_id=1, replica_groups=mesh['x_hi'=2,'z_hi'=4,'z_lo'=2,'core'=2,'y_hi'=4,'y_lo'=2,'x_lo'=2] {'z..., dimensions={0} | all-to-all | bytes 131072 | tf_op jit(solution)/shard_map/all_to_all | solution.py:45
  135.8 13.9 %all_to_all.45 = bf16[16,16,128]{2,1,0:T(8,128)(2,1)S(1)} all-to-all(bf16[16,16,128]{2,1,0:T(8,128)(2,1)S(1)} %broadcast_in_dim.69), channel_id=1, replica_groups=mesh['x_hi'=2,'z_hi'=4,'z_lo'=2,'core'=2,'y_hi'=4,'y_lo'=2,'x_lo'=2] {'z..., dimensions={0} | all-to-all | bytes 131072 | tf_op jit(solution)/shard_map/all_to_all | solution.py:55
  149.7 1.2 broadcast_in_dim.71
  150.9 3.7 %all-to-all-start.4 = ((bf16[16,256,128]{2,1,0:T(8,128)(2,1)}), bf16[16,256,128]{2,1,0:T(8,128)(2,1)S(1)}, u32[]{:S(2)}, u32[]{:S(2)}) async-start(bf16[16,256,128]{2,1,0:T(8,128)(2,1)} %broadcast_in_dim.71), calls=%async_computation.4 | async-start | bytes 2097152 | tf_op jit(solution)/shard_map/all_to_all | solution.py:55
  154.6 0.8 convolution_convert_fusion.6
  155.4 11.8 %all-to-all-done.4 = bf16[16,256,128]{2,1,0:T(8,128)(2,1)S(1)} async-done(((bf16[16,256,128]{2,1,0:T(8,128)(2,1)}), bf16[16,256,128]{2,1,0:T(8,128)(2,1)S(1)}, u32[]{:S(2)}, u32[]{:S(2)}) %all-to-all-start.4) | async-done | bytes 1048608 | tf_op jit(solution)/shard_map/all_to_all | solution.py:55
  167.3 10.3 %all_to_all.46 = bf16[2,4096,128]{2,1,0:T(8,128)(2,1)S(1)} all-to-all(bf16[2,4096,128]{2,1,0:T(8,128)(2,1)S(1)} %broadcast_in_dim.73), channel_id=1, replica_groups=mesh['x_hi'=2,'z_hi'=4,'z_lo'=2,'core'=2,'y_hi'=4,'y_lo'=2,'x_lo'=2] {'c..., dimensions={0} | all-to-all | bytes 4194304 | tf_op jit(solution)/shard_map/all_to_all | solution.py:55
  177.6 2.3 %copy.24 = bf16[4,512,4,128]{1,3,2,0:T(8,128)(2,1)} copy(bf16[4,512,4,128]{3,1,0,2:T(8,128)(2,1)S(1)} %bitcast.72) | data formatting | bytes 4194304 | tf_op jit(solution)/shard_map/transpose | solution.py:167
  180.0 4.1 %copy.25 = bf16[4,512,512]{2,1,0:T(8,128)(2,1)} copy(bf16[4,512,512]{1,2,0:T(8,128)(2,1)} %bitcast.73) | data formatting | bytes 4194304
  (37 shorter events, 0.7 us)
Async XLA Ops:
  0.6 55.6 %copy-start = (bf16[512,512]{1,0:T(8,128)(2,1)S(1)}, bf16[512,512]{1,0:T(8,128)(2,1)}, u32[]{:S(2)}) copy-start(bf16[512,512]{1,0:T(8,128)(2,1)} %param.17) | copy-start | bytes 1572868
  0.6 22.8 %collective-permute-start.1 = (bf16[1,1,128,512]{3,2,1,0:T(8,128)(2,1)}, bf16[1,1,128,512]{3,2,1,0:T(8,128)(2,1)S(1)}, u32[]{:S(2)}, u32[]{:S(2)}) collective-permute-start(bf16[1,1,128,512]{3,2,1,0:T(8,128)(2,1)} %param.12), channel_id=1, source_target_pairs={{16,0},{32,16},{48,32},{64,48},{80,64},{96,80},{112,96},{128,112},... | collective-permute-start | bytes 393224 | tf_op jit(solution)/shard_map/ppermute | solution.py:21
  9.6 13.8 %collective-permute-start = (bf16[1,1,128,512]{3,2,1,0:T(8,128)(2,1)}, bf16[1,1,128,512]{3,2,1,0:T(8,128)(2,1)S(1)}, u32[]{:S(2)}, u32[]{:S(2)}) collective-permute-start(bf16[1,1,128,512]{3,2,1,0:T(8,128)(2,1)} %param.12), channel_id=1, source_target_pairs={{0,16},{16,32},{32,48},{48,64},{64,80},{80,96},{96,112},{112,128},... | collective-permute-start | bytes 393224 | tf_op jit(solution)/shard_map/ppermute | solution.py:18
  18.4 4.9 %copy-start.5 = (bf16[1,1,128,512]{3,2,1,0:T(8,128)(2,1)S(1)}, bf16[1,1,128,512]{3,2,1,0:T(8,128)(2,1)}, u32[]{:S(2)}) copy-start(bf16[1,1,128,512]{3,2,1,0:T(8,128)(2,1)} %param.12) | copy-start | bytes 393220
  18.4 10.3 %copy-start.9 = (s32[1,1,128]{2,1,0:T(1,128)S(1)}, s32[1,1,128]{2,1,0:T(1,128)}, u32[]{:S(2)}) copy-start(s32[1,1,128]{2,1,0:T(1,128)} %param.23) | copy-start | bytes 1540
  18.5 10.3 %copy-start.8 = (s32[1,1,1024]{2,1,0:T(1,128)S(1)}, s32[1,1,1024]{2,1,0:T(1,128)}, u32[]{:S(2)}) copy-start(s32[1,1,1024]{2,1,0:T(1,128)} %param.21) | copy-start | bytes 12292
  23.4 12.1 %collective-permute-start.3 = (bf16[3,1,128,512]{3,2,1,0:T(8,128)(2,1)S(1)}, bf16[3,1,128,512]{3,2,1,0:T(8,128)(2,1)S(1)}, u32[]{:S(2)}, u32[]{:S(2)}) collective-permute-start(bf16[3,1,128,512]{3,2,1,0:T(8,128)(2,1)S(1)} %constant_dynamic-update-slice_fusion), channel_id=1, source_target_pairs={{1,0},{2,1},{3,2},{4,3},{5,4},{6,5},{7,6},{8,7},{9,8},{10,9},{11,1... | collective-permute-start | bytes 1179656 | tf_op jit(solution)/shard_map/ppermute | solution.py:21
  24.7 15.6 %collective-permute-start.2 = (bf16[3,1,128,512]{3,2,1,0:T(8,128)(2,1)S(1)}, bf16[3,1,128,512]{3,2,1,0:T(8,128)(2,1)S(1)}, u32[]{:S(2)}, u32[]{:S(2)}) collective-permute-start(bf16[3,1,128,512]{3,2,1,0:T(8,128)(2,1)S(1)} %constant_dynamic-update-slice_fusion), channel_id=1, source_target_pairs={{0,1},{1,2},{2,3},{3,4},{4,5},{5,6},{6,7},{7,8},{8,9},{9,10},{10,1... | collective-permute-start | bytes 1179656 | tf_op jit(solution)/shard_map/ppermute | solution.py:18
  40.4 1.0 copy-start.1
  57.0 1.5 copy-start.7
  58.6 1.6 copy-start.2
  58.6 2.2 %copy-start.3 = (f32[1024,512]{1,0:T(8,128)S(1)}, f32[1024,512]{1,0:T(8,128)}, u32[]{:S(2)}) copy-start(f32[1024,512]{1,0:T(8,128)} %gather_fusion) | copy-start | bytes 6291460
  62.4 7.2 %copy-start.6 = (bf16[1024,512]{1,0:T(8,128)(2,1)S(1)}, bf16[1024,512]{1,0:T(8,128)(2,1)}, u32[]{:S(2)}) copy-start(bf16[1024,512]{1,0:T(8,128)(2,1)} %gather_fusion.3) | copy-start | bytes 3145732
  64.2 7.7 %collective-permute-start.4 = (f32[2,512]{1,0:T(2,128)S(1)}, f32[2,512]{1,0:T(2,128)S(1)}, u32[]{:S(2)}, u32[]{:S(2)}) collective-permute-start(f32[2,512]{1,0:T(2,128)S(1)} %get-tuple-element.11), channel_id=1, source_target_pairs={{0,1},{1,2},{2,3},{3,4},{4,5},{5,6},{6,7},{7,8},{8,9},{9,10},{10,1... | collective-permute-start | bytes 12296 | tf_op jit(solution)/shard_map/ppermute | solution.py:18
  68.3 4.4 %collective-permute-start.5 = (f32[2,512]{1,0:T(2,128)S(1)}, f32[2,512]{1,0:T(2,128)S(1)}, u32[]{:S(2)}, u32[]{:S(2)}) collective-permute-start(f32[2,512]{1,0:T(2,128)S(1)} %get-tuple-element.12), channel_id=1, source_target_pairs={{1,0},{2,1},{3,2},{4,3},{5,4},{6,5},{7,6},{8,7},{9,8},{10,9},{11,1... | collective-permute-start | bytes 12296 | tf_op jit(solution)/shard_map/ppermute | solution.py:21
  110.3 44.2 %copy-start.4 = (bf16[512,512]{1,0:T(8,128)(2,1)S(1)}, bf16[512,512]{1,0:T(8,128)(2,1)}, u32[]{:S(2)}) copy-start(bf16[512,512]{1,0:T(8,128)(2,1)} %param.18) | copy-start | bytes 1572868
  150.9 16.3 %all-to-all-start.4 = ((bf16[16,256,128]{2,1,0:T(8,128)(2,1)}), bf16[16,256,128]{2,1,0:T(8,128)(2,1)S(1)}, u32[]{:S(2)}, u32[]{:S(2)}) async-start(bf16[16,256,128]{2,1,0:T(8,128)(2,1)} %broadcast_in_dim.71), calls=%async_computation.4 | async-start | bytes 2097152 | tf_op jit(solution)/shard_map/all_to_all | solution.py:55

commit v2 on v1

v2 whole, which is shorter than its diff:
```python
import math

import jax
import jax.numpy as jnp
from jax import lax
from jax.experimental import pallas as pl
from jax.experimental.pallas import tpu as pltpu
from jax.sharding import Mesh
from jax.sharding import PartitionSpec as P

LAT = ("x_hi", "z_hi", "z_lo", "core")
LON = ("y_hi", "y_lo", "x_lo")
NEAR = ("x_hi", "z_lo", "y_lo", "x_lo")
FAR = ("z_hi", "y_hi")
CORE = ("core",)
LANES = 128
CHUNK = 256
BF16 = jnp.bfloat16
F32 = jnp.float32


def exchange(part, axes):
    return lax.all_to_all(part, axes, 0, 0, tiled=True)


def reduce_stage(part, axes):
    got = exchange(part, axes)
    count = lax.axis_size(axes)
    return jnp.sum(got.reshape(count, -1, got.shape[-1]).astype(F32), axis=0)


def gather_stage(part, axes):
    count = lax.axis_size(axes)
    copies = jnp.broadcast_to(part[None], (count,) + part.shape)
    return exchange(copies.reshape(-1, part.shape[-1]), axes)


def all_sum(part, scale):
    features = part.shape[-1]
    tiles = features // LANES
    part = reduce_stage(part, CORE).astype(BF16)
    part = reduce_stage(part, NEAR).astype(BF16)
    rows = part.shape[0]
    part = part.reshape(rows, tiles, LANES).transpose(1, 0, 2).reshape(-1, LANES)
    part = (reduce_stage(part, FAR) * scale).astype(BF16)
    part = gather_stage(part, FAR)
    part = part.reshape(tiles, rows, LANES).transpose(1, 0, 2).reshape(rows, features)
    part = gather_stage(part, NEAR)
    return gather_stage(part, CORE)


def both_ways(block, axis):
    count = lax.axis_size(axis)
    forward = [(i, i + 1) for i in range(count - 1)]
    backward = [(target, source) for source, target in forward]
    return lax.ppermute(block, axis, forward), lax.ppermute(block, axis, backward)


def silu_parts(values):
    sigmoid_v = jax.nn.sigmoid(values)
    return values * sigmoid_v, sigmoid_v * (1.0 + values * (1.0 - sigmoid_v))


def mm(left, right):
    return lax.dot_general(left, right, (((1,), (0,)), ((), ())), preferred_element_type=F32)


def mm_rows(left, right):
    return lax.dot_general(left, right, (((0,), (0,)), ((), ())), preferred_element_type=F32)


def mm_cols(left, right):
    return lax.dot_general(left, right, (((1,), (1,)), ((), ())), preferred_element_type=F32)


def column(row):
    return jnp.transpose(jnp.broadcast_to(row, (8, row.shape[-1])))[:, :1]


def one_hot_cols(ids_column, width):
    lane_ids = lax.broadcasted_iota(jnp.int32, (ids_column.shape[0], width), 1)
    return (ids_column == lane_ids).astype(F32).astype(BF16)


def one_hot_rows(ids_row, height):
    row_ids = lax.broadcasted_iota(jnp.int32, (height, ids_row.shape[-1]), 0)
    return (ids_row == row_ids).astype(F32).astype(BF16)


def block_kernel(
    low_ref,
    mid_ref,
    high_ref,
    nodes_ref,
    top_ref,
    cot_ref,
    w_src_ref,
    w_dst_ref,
    w_msg_ref,
    w_top_ref,
    src_ref,
    dst_ref,
    band_ref,
    updated_ref,
    grads_ref,
    window_ref,
    ext,
    picked,
    hidden,
    pre_grad,
    act_grad,
    act_slope,
    msg_slope,
    dst_cols,
):
    slots = src_ref.shape[-1]
    block, features = nodes_ref.shape
    third = low_ref.shape[0]
    ext[0:third, :] = low_ref[...]
    ext[third : 2 * third, :] = mid_ref[...]
    ext[2 * third :, :] = high_ref[...]
    nodes = nodes_ref[...]
    src_col = column(src_ref[...])
    dst_col = column(dst_ref[...])
    dst_rows = one_hot_rows(dst_ref[...], block)
    inflow = jnp.zeros((block, features), F32)
    for start in range(0, slots, CHUNK):
        span = slice(start, start + CHUNK)
        gathered = mm(one_hot_cols(src_col[span], ext.shape[0]), ext[...]).astype(BF16)
        picked[span, :] = gathered
        at_dst = one_hot_cols(dst_col[span], block)
        dst_cols[span, :] = at_dst
        local = mm(at_dst, nodes).astype(BF16)
        pre_act = mm(gathered, w_src_ref[...]) + mm(local, w_dst_ref[...])
        value, slope = silu_parts(pre_act)
        act_slope[span, :] = slope
        hid = value.astype(BF16)
        hidden[span, :] = hid
        value, slope = silu_parts(mm(hid, w_msg_ref[...]))
        msg_slope[span, :] = slope
        inflow = inflow + mm(dst_rows[:, span], value.astype(BF16))
    top_count = top_ref.shape[0]
    top_nodes = top_ref[...]
    top_table = mm(top_nodes, w_top_ref[...]).astype(BF16)
    band_col = column(band_ref[...])
    node_pre = inflow + mm(one_hot_cols(band_col, top_count), top_table)
    value, slope = silu_parts(node_pre)
    updated_ref[...] = (nodes.astype(F32) + value).astype(BF16)
    node_grad = (cot_ref[...].astype(F32) * slope).astype(BF16)
    window = mm(one_hot_rows(band_ref[...], top_count), node_grad)
    window_ref[...] = window
    grads_ref[3] = mm_rows(top_nodes, window.astype(BF16)).astype(BF16)
    dst_grad = jnp.zeros((block, features), F32)
    for start in range(0, slots, CHUNK):
        span = slice(start, start + CHUNK)
        msg_grad = mm(dst_cols[span, :], node_grad)
        grad = (msg_grad * msg_slope[span, :]).astype(BF16)
        pre_grad[span, :] = grad
        grad = (mm_cols(grad, w_msg_ref[...]) * act_slope[span, :]).astype(BF16)
        act_grad[span, :] = grad
        dst_grad = dst_grad + mm(dst_rows[:, span], grad)
    grads_ref[0] = mm_rows(picked[...], act_grad[...]).astype(BF16)
    grads_ref[1] = mm_rows(nodes, dst_grad.astype(BF16)).astype(BF16)
    grads_ref[2] = mm_rows(hidden[...], pre_grad[...]).astype(BF16)


def block_round(*args):
    nodes, top_nodes = args[3], args[4]
    slots = args[10].shape[-1]
    block, features = nodes.shape
    ext_rows = 3 * args[0].shape[0]
    return pl.pallas_call(
        block_kernel,
        out_shape=(
            jax.ShapeDtypeStruct((block, features), BF16),
            jax.ShapeDtypeStruct((4, features, features), BF16),
            jax.ShapeDtypeStruct((top_nodes.shape[0], features), F32),
        ),
        scratch_shapes=[
            pltpu.VMEM((ext_rows, features), BF16),
            pltpu.VMEM((slots, features), BF16),
            pltpu.VMEM((slots, features), BF16),
            pltpu.VMEM((slots, features), BF16),
            pltpu.VMEM((slots, features), BF16),
            pltpu.VMEM((slots, features), F32),
            pltpu.VMEM((slots, features), F32),
            pltpu.VMEM((slots, block), BF16),
        ],
        compiler_params=pltpu.CompilerParams(vmem_limit_bytes=48 << 20),
        name="block_round",
    )(*args)


def shards(
    nodes,
    top_nodes,
    cotangent,
    w_src,
    w_dst,
    w_msg,
    w_top,
    src_code,
    src_node,
    dst_node,
    edge_count,
    parent,
):
    block_size, features = nodes.shape[2:]
    slots = src_code.shape[-1]
    top_local = top_nodes.shape[0]
    owner_rows = top_local // lax.axis_size(LON)
    lon_index = lax.axis_index(LON)
    band_start = lax.axis_index(LAT) * top_local
    own = nodes.reshape(block_size, features)
    west, east = both_ways(own, LON)
    mid = jnp.concatenate([west, own, east], axis=0)
    low, high = both_ways(mid, LAT)
    src_idx = (src_code * block_size + src_node).reshape(1, slots)
    live_slot = lax.broadcasted_iota(jnp.int32, (1, slots), 1) < edge_count
    dst_idx = jnp.where(live_slot, dst_node.reshape(1, slots), block_size)
    band_ids = parent.reshape(1, block_size) - band_start
    updated, grads, window = block_round(
        low,
        mid,
        high,
        own,
        top_nodes,
        cotangent.reshape(block_size, features),
        w_src,
        w_dst,
        w_msg,
        w_top,
        src_idx,
        dst_idx,
        band_ids,
    )
    nodes_total = block_size * lax.axis_size(LAT) * lax.axis_size(LON)
    grad_scale = 8.0 / math.sqrt(nodes_total)
    weight_grads = all_sum(grads.reshape(-1, features), grad_scale)
    padded = jnp.pad(window, ((owner_rows, owner_rows), (0, 0)))
    triple = lax.dynamic_slice_in_dim(padded, lon_index * owner_rows, 3 * owner_rows, 0)
    count = lax.axis_size(LON)
    forward = [(i, i + 1) for i in range(count - 1)]
    backward = [(target, source) for source, target in forward]
    from_left = lax.ppermute(triple[2 * owner_rows :], LON, forward)
    from_right = lax.ppermute(triple[:owner_rows], LON, backward)
    table_grad = (triple[owner_rows : 2 * owner_rows] + from_left + from_right).astype(BF16)
    d_top = lax.dot_general(
        table_grad, w_top, (((1,), (1,)), ((), ())), preferred_element_type=F32
    ).astype(BF16)
    return (
        updated.reshape(nodes.shape),
        weight_grads.reshape(4, features, features),
        d_top,
    )


def solution(mesh):
    lat_count, lon_count = mesh.shape["lat"], mesh.shape["lon"]
    fine = Mesh(
        mesh.devices.reshape(2, lat_count // 8, 2, 2, lon_count // 4, 2, 2),
        LAT + LON,
    )
    placed = (
        P(LAT, LON, None, None),
        P(LAT, None),
        P(LAT, LON, None, None),
        P(),
        P(),
        P(),
        P(),
        P(LAT, LON, None),
        P(LAT, LON, None),
        P(LAT, LON, None),
        P(LAT, LON),
        P(LAT, LON, None),
    )
    return jax.shard_map(
        shards,
        mesh=fine,
        in_specs=placed,
        out_specs=(P(LAT, LON, None, None), P(), P(LAT + LON, None)),
        check_vma=False,
    )
```

time: 185 us -> 141 us (0.76)
  local copies, waits for them, and re-layouts: 29.8 us -> 9.34 us
  matrix products: 15.3 us -> 0.83 us
  Pallas kernels: 0 us -> 8.92 us
  waiting for transfers between devices: 24.1 us -> 15.7 us
  other arithmetic: 8.97 us -> 4.25 us
  starting transfers between devices: 25.2 us -> 21.9 us
    gather x4 -> x0, local copies, waits for them, and re-layouts: 15.7 us -> none  [the longest x1 5.06 us: shards(): grad_src = contract_rows(jnp.take(ext_flat, src_idx, axis=0), act_grad)]
    dot_general x12 -> x0, matrix products: 14.5 us -> none  [the longest x5 5.02 us: contract_rows(): lax.dot_general(left_mat, right_mat, (((0,), (0,)), ((), ())), preferred_...]
    all_to_all x1, waiting for transfers between devices: 11.8 us -> 0.39 us  [exchange(): return lax.all_to_all(part, axes, 0, 0, tiled=True)]
    pallas_call x0 -> x1, Pallas kernels: none -> 8.92 us  [block_round(): pl.pallas_call(block_kernel, out_shape=(jax.ShapeDtypeStruct((block, feat...]
    convert_element_type x2 -> x0, local copies, waits for them, and re-layouts: 3.89 us -> none  [all_sum(): part = stack.astype(jnp.bfloat16)]
    ppermute x6, starting transfers between devices: 21.5 us -> 18.3 us  [the longest x2 9.94 us: both_ways(): lax.ppermute(block, axis, forward)]
    ppermute x6, waiting for transfers between devices: 12.3 us -> 15.4 us  [the longest x2 7.66 us: both_ways(): lax.ppermute(block, axis, backward)]
    convert_element_type x4 -> x1, other arithmetic: 2.75 us -> 0.01 us  [all_sum(): part = (reduce_stage(part, FAR) * scale).astype(BF16)]
  transfers between devices with their start and end apart: 7 -> 7, of which waited for: 4 -> 5; matrix products, arithmetic and copies ran while one was open for 8% -> 2% of each run, Pallas kernels for 0% -> 0%
where the time goes in v2:
time: 141 us; the launch traced here: 140 us
  blocking collectives  77.7 us (55%)
  starting transfers between devices  21.9 us (16%)
  waiting for transfers between devices  15.7 us (11%)
  local copies, waits for them, and re-layouts  9.34 us (7%)
  Pallas kernels  8.92 us (6%)
  other arithmetic  4.25 us (3%)
  between operations  1.46 us (1%)
    all_to_all x5, blocking collectives, exchange(): return lax.all_to_all(part, axes, 0, 0, tiled=True)  77.7 us
    ppermute x2, starting transfers between devices, both_ways(): lax.ppermute(block, axis, forward)  9.94 us
    pallas_call x1, Pallas kernels, block_round(): pl.pallas_call(block_kernel, out_shape=(jax.ShapeDtypeStruct((block, feat...  8.92 us
    unnamed x17, local copies, waits for them, and re-layouts  8.05 us
    ppermute x2, waiting for transfers between devices, both_ways(): lax.ppermute(block, axis, backward)  7.66 us
    ppermute x1, waiting for transfers between devices, shards(): from_right = lax.ppermute(triple[:owner_rows], LON, backward)  6.97 us
    ppermute x2, starting transfers between devices, both_ways(): lax.ppermute(block, axis, backward)  3.9 us
    all_to_all x1, starting transfers between devices, exchange(): return lax.all_to_all(part, axes, 0, 0, tiled=True)  3.66 us
  transfers between devices with their start and end apart: 7, of which 5 were waited for; matrix products, arithmetic and copies ran while one was open for 2% of the time, Pallas kernels for 0%

profile of v2, /device:TPU:1, one launch (start us, length us, event | category | flops | bytes accessed | tf_op | source)
XLA Modules:
  0.0 140.2 jit_solution(15836699734633239813)
XLA Ops:
  0.6 4.0 %collective-permute-start = (bf16[128,512]{1,0:T(8,128)(2,1)}, bf16[128,512]{1,0:T(8,128)(2,1)S(1)}, u32[]{:S(2)}, u32[]{:S(2)}) collective-permute-start(bf16[128,512]{1,0:T(8,128)(2,1)} %bitcast.26), channel_id=1, source_target_pairs={{0,1},{1,2},{2,3},{3,4},{4,5},{5,6},{6,7},{7,8},{8,9},{9,10},{10,1... | collective-permute-start | bytes 393224 | tf_op jit(solution)/shard_map/ppermute | solution.py:56
  4.6 1.3 collective-permute-start.1
  6.5 0.7 compare_select_fusion.dst_ref
  7.2 0.0 collective-permute-done
  7.3 3.3 %collective-permute-done.1 = bf16[128,512]{1,0:T(8,128)(2,1)S(1)} collective-permute-done((bf16[128,512]{1,0:T(8,128)(2,1)}, bf16[128,512]{1,0:T(8,128)(2,1)S(1)}, u32[]{:S(2)}, u32[]{:S(2)}) %collective-permute-start.1) | collective-permute-done | bytes 131104 | tf_op jit(solution)/shard_map/ppermute | solution.py:56
  10.5 0.9 pad_maximum_fusion.mid_ref
  11.5 6.0 %collective-permute-start.2 = (bf16[384,512]{1,0:T(8,128)(2,1)S(1)}, bf16[384,512]{1,0:T(8,128)(2,1)S(1)}, u32[]{:S(2)}, u32[]{:S(2)}) collective-permute-start(bf16[384,512]{1,0:T(8,128)(2,1)S(1)} %pad_maximum_fusion.mid_ref), channel_id=1, source_target_pairs={{0,16},{16,32},{32,48},{48,64},{64,80},{80,96},{96,112},{112,128},... | collective-permute-start | bytes 1179656 | tf_op jit(solution)/shard_map/ppermute | solution.py:56
  17.4 2.6 %collective-permute-start.3 = (bf16[384,512]{1,0:T(8,128)(2,1)S(1)}, bf16[384,512]{1,0:T(8,128)(2,1)S(1)}, u32[]{:S(2)}, u32[]{:S(2)}) collective-permute-start(bf16[384,512]{1,0:T(8,128)(2,1)S(1)} %pad_maximum_fusion.mid_ref), channel_id=1, source_target_pairs={{16,0},{32,16},{48,32},{64,48},{80,64},{96,80},{112,96},{128,112},... | collective-permute-start | bytes 1179656 | tf_op jit(solution)/shard_map/ppermute | solution.py:56
  20.1 0.7 subtract_bitcast_fusion.band_ref
  20.7 0.7 add_bitcast_fusion.src_ref
  21.4 0.7 collective-permute-done.2.low_ref
  22.1 4.4 %collective-permute-done.3.high_ref = bf16[384,512]{1,0:T(8,128)(2,1)S(1)} collective-permute-done((bf16[384,512]{1,0:T(8,128)(2,1)S(1)}, bf16[384,512]{1,0:T(8,128)(2,1)S(1)}, u32[]{:S(2)}, u32[]{:S(2)}) %collective-permute-start.3) | collective-permute-done | bytes 393248 | tf_op jit(solution)/shard_map/ppermute | solution.py:56
  26.5 0.0 copy-start
  26.5 1.0 copy-done
  27.6 0.0 copy-start.2
  27.6 1.0 copy-done.2
  28.6 0.0 copy-start.3
  28.6 1.0 copy-done.3
  29.7 0.0 copy-start.4
  29.7 1.0 copy-done.4
  30.7 0.0 copy-start.5
  30.7 0.9 copy-done.5
  31.6 0.0 copy-start.6
  31.6 0.9 copy-done.6
  32.5 0.0 copy-start.7
  32.5 0.8 copy-done.7
  33.3 8.9 %block_round.1 = (bf16[128,512]{1,0:T(8,128)(2,1)}, bf16[4,512,512]{2,1,0:T(8,128)(2,1)S(1)}, f32[32,512]{1,0:T(8,128)S(1)}) custom-call(bf16[384,512]{1,0:T(8,128)(2,1)S(1)} %collective-permute-done.2.low_ref, bf16[384,512]{1,0:T(8,128)(2,1)S(1)} %pad_maximum_fusion.mid_ref, bf16[384,512]{1,0:T(8,128)(2,1)S(1)} %collective-permute-done.3.high_ref, ...), custom_call_target="tpu_custom_call" | custom-call | tf_op jit(solution)/shard_map/block_round/pallas_call | solution.py:172
  42.2 5.1 %all_to_all.45 = bf16[2,1024,512]{2,1,0:T(8,128)(2,1)S(1)} all-to-all(bf16[2,1024,512]{2,1,0:T(8,128)(2,1)S(1)} %bitcast.25), channel_id=1, replica_groups=mesh['x_hi'=2,'z_hi'=4,'z_lo'=2,'core'=2,'y_hi'=4,'y_lo'=2,'x_lo'=2] {'c..., dimensions={0} | all-to-all | bytes 4194304 | tf_op jit(solution)/shard_map/all_to_all | solution.py:23
  47.3 1.1 reduce_sum.33
  48.3 25.7 %all_to_all.46 = bf16[16,64,512]{2,1,0:T(8,128)(2,1)S(1)} all-to-all(bf16[16,64,512]{2,1,0:T(8,128)(2,1)S(1)} %bitcast.33), channel_id=1, replica_groups=mesh['x_hi'=2,'z_hi'=4,'z_lo'=2,'core'=2,'y_hi'=4,'y_lo'=2,'x_lo'=2] {'x..., dimensions={0} | all-to-all | bytes 2097152 | tf_op jit(solution)/shard_map/all_to_all | solution.py:23
  74.0 0.1 reduce_sum.34
  74.2 0.0 copy-start.1
  74.2 22.7 %all_to_all.47 = bf16[16,16,128]{2,1,0:T(8,128)(2,1)S(1)} all-to-all(bf16[16,16,128]{2,1,0:T(8,128)(2,1)S(1)} %bitcast.36), channel_id=1, replica_groups=mesh['x_hi'=2,'z_hi'=4,'z_lo'=2,'core'=2,'y_hi'=4,'y_lo'=2,'x_lo'=2] {'z..., dimensions={0} | all-to-all | bytes 131072 | tf_op jit(solution)/shard_map/all_to_all | solution.py:23
  97.0 13.9 %all_to_all.48 = bf16[16,16,128]{2,1,0:T(8,128)(2,1)S(1)} all-to-all(bf16[16,16,128]{2,1,0:T(8,128)(2,1)S(1)} %broadcast_in_dim.26), channel_id=1, replica_groups=mesh['x_hi'=2,'z_hi'=4,'z_lo'=2,'core'=2,'y_hi'=4,'y_lo'=2,'x_lo'=2] {'z..., dimensions={0} | all-to-all | bytes 131072 | tf_op jit(solution)/shard_map/all_to_all | solution.py:23
  110.9 1.1 broadcast_in_dim.28
  112.0 3.7 %all-to-all-start.4 = ((bf16[16,64,512]{2,1,0:T(8,128)(2,1)}), bf16[16,64,512]{2,1,0:T(8,128)(2,1)S(1)}, u32[]{:S(2)}, u32[]{:S(2)}) async-start(bf16[16,64,512]{2,1,0:T(8,128)(2,1)} %broadcast_in_dim.28), calls=%async_computation.4 | async-start | bytes 2097152 | tf_op jit(solution)/shard_map/all_to_all | solution.py:23
  115.7 3.1 %collective-permute-start.4 = (f32[2,512]{1,0:T(2,128)S(1)}, f32[2,512]{1,0:T(2,128)S(1)}, u32[]{:S(2)}, u32[]{:S(2)}) collective-permute-start(f32[2,512]{1,0:T(2,128)S(1)} %get-tuple-element.9), channel_id=1, source_target_pairs={{0,1},{1,2},{2,3},{3,4},{4,5},{5,6},{6,7},{7,8},{8,9},{9,10},{10,1... | collective-permute-start | bytes 12296 | tf_op jit(solution)/shard_map/ppermute | solution.py:245
  118.9 1.3 collective-permute-start.5
  120.2 0.0 collective-permute-done.4
  120.2 7.0 %collective-permute-done.5 = f32[2,512]{1,0:T(2,128)S(1)} collective-permute-done((f32[2,512]{1,0:T(2,128)S(1)}, f32[2,512]{1,0:T(2,128)S(1)}, u32[]{:S(2)}, u32[]{:S(2)}) %collective-permute-start.5) | collective-permute-done | bytes 4128 | tf_op jit(solution)/shard_map/ppermute | solution.py:246
  127.2 0.0 copy-done.1
  127.2 0.8 convolution_convert_fusion
  128.0 0.4 all-to-all-done.4
  128.4 0.1 broadcast_in_dim.30
  128.5 10.3 %all_to_all.49 = bf16[2,1024,512]{2,1,0:T(8,128)(2,1)S(1)} all-to-all(bf16[2,1024,512]{2,1,0:T(8,128)(2,1)S(1)} %broadcast_in_dim.30), channel_id=1, replica_groups=mesh['x_hi'=2,'z_hi'=4,'z_lo'=2,'core'=2,'y_hi'=4,'y_lo'=2,'x_lo'=2] {'c..., dimensions={0} | all-to-all | bytes 4194304 | tf_op jit(solution)/shard_map/all_to_all | solution.py:23
  138.9 1.3 copy.24
  (7 shorter events, 0.1 us)
Async XLA Ops:
  0.6 6.6 %collective-permute-start = (bf16[128,512]{1,0:T(8,128)(2,1)}, bf16[128,512]{1,0:T(8,128)(2,1)S(1)}, u32[]{:S(2)}, u32[]{:S(2)}) collective-permute-start(bf16[128,512]{1,0:T(8,128)(2,1)} %bitcast.26), channel_id=1, source_target_pairs={{0,1},{1,2},{2,3},{3,4},{4,5},{5,6},{6,7},{7,8},{8,9},{9,10},{10,1... | collective-permute-start | bytes 393224 | tf_op jit(solution)/shard_map/ppermute | solution.py:56
  4.6 5.9 %collective-permute-start.1 = (bf16[128,512]{1,0:T(8,128)(2,1)}, bf16[128,512]{1,0:T(8,128)(2,1)S(1)}, u32[]{:S(2)}, u32[]{:S(2)}) collective-permute-start(bf16[128,512]{1,0:T(8,128)(2,1)} %bitcast.27), channel_id=1, source_target_pairs={{1,0},{2,1},{3,2},{4,3},{5,4},{6,5},{7,6},{8,7},{9,8},{10,9},{11,1... | collective-permute-start | bytes 393224 | tf_op jit(solution)/shard_map/ppermute | solution.py:56
  11.5 10.7 %collective-permute-start.2 = (bf16[384,512]{1,0:T(8,128)(2,1)S(1)}, bf16[384,512]{1,0:T(8,128)(2,1)S(1)}, u32[]{:S(2)}, u32[]{:S(2)}) collective-permute-start(bf16[384,512]{1,0:T(8,128)(2,1)S(1)} %pad_maximum_fusion.mid_ref), channel_id=1, source_target_pairs={{0,16},{16,32},{32,48},{48,64},{64,80},{80,96},{96,112},{112,128},... | collective-permute-start | bytes 1179656 | tf_op jit(solution)/shard_map/ppermute | solution.py:56
  17.4 9.1 %collective-permute-start.3 = (bf16[384,512]{1,0:T(8,128)(2,1)S(1)}, bf16[384,512]{1,0:T(8,128)(2,1)S(1)}, u32[]{:S(2)}, u32[]{:S(2)}) collective-permute-start(bf16[384,512]{1,0:T(8,128)(2,1)S(1)} %pad_maximum_fusion.mid_ref), channel_id=1, source_target_pairs={{16,0},{32,16},{48,32},{64,48},{80,64},{96,80},{112,96},{128,112},... | collective-permute-start | bytes 1179656 | tf_op jit(solution)/shard_map/ppermute | solution.py:56
  26.5 1.0 copy-start
  27.6 1.0 copy-start.2
  28.6 1.0 copy-start.3
  29.7 1.0 copy-start.4
  30.7 0.9 copy-start.5
  31.6 0.9 copy-start.6
  32.5 0.8 copy-start.7
  74.2 53.0 %copy-start.1 = (bf16[512,512]{1,0:T(8,128)(2,1)S(1)}, bf16[512,512]{1,0:T(8,128)(2,1)}, u32[]{:S(2)}) copy-start(bf16[512,512]{1,0:T(8,128)(2,1)} %w_top_ref.1) | copy-start | bytes 1572868
  112.0 16.4 %all-to-all-start.4 = ((bf16[16,64,512]{2,1,0:T(8,128)(2,1)}), bf16[16,64,512]{2,1,0:T(8,128)(2,1)S(1)}, u32[]{:S(2)}, u32[]{:S(2)}) async-start(bf16[16,64,512]{2,1,0:T(8,128)(2,1)} %broadcast_in_dim.28), calls=%async_computation.4 | async-start | bytes 2097152 | tf_op jit(solution)/shard_map/all_to_all | solution.py:23
  115.7 4.4 %collective-permute-start.4 = (f32[2,512]{1,0:T(2,128)S(1)}, f32[2,512]{1,0:T(2,128)S(1)}, u32[]{:S(2)}, u32[]{:S(2)}) collective-permute-start(f32[2,512]{1,0:T(2,128)S(1)} %get-tuple-element.9), channel_id=1, source_target_pairs={{0,1},{1,2},{2,3},{3,4},{4,5},{5,6},{6,7},{7,8},{8,9},{9,10},{10,1... | collective-permute-start | bytes 12296 | tf_op jit(solution)/shard_map/ppermute | solution.py:245
  118.9 8.3 %collective-permute-start.5 = (f32[2,512]{1,0:T(2,128)S(1)}, f32[2,512]{1,0:T(2,128)S(1)}, u32[]{:S(2)}, u32[]{:S(2)}) collective-permute-start(f32[2,512]{1,0:T(2,128)S(1)} %get-tuple-element.10), channel_id=1, source_target_pairs={{1,0},{2,1},{3,2},{4,3},{5,4},{6,5},{7,6},{8,7},{9,8},{10,9},{11,1... | collective-permute-start | bytes 12296 | tf_op jit(solution)/shard_map/ppermute | solution.py:246

commit v3 on v2

--- a/solution.py
+++ b/solution.py
@@ -112,14 +112,29 @@
     act_slope,
     msg_slope,
     dst_cols,
+    w_src,
+    w_dst,
+    w_msg,
+    w_top,
+    nodes_own,
+    top_own,
+    cot_own,
+    arrived,
 ):
+    held = (w_src, w_dst, w_msg, w_top, nodes_own, top_own, cot_own)
+    sources = (w_src_ref, w_dst_ref, w_msg_ref, w_top_ref, nodes_ref, top_ref, cot_ref)
+    copies = [
+        pltpu.make_async_copy(source, target, arrived.at[place])
+        for place, (source, target) in enumerate(zip(sources, held))
+    ]
+    for place in (4, 0, 1, 2, 3, 5, 6):
+        copies[place].start()
     slots = src_ref.shape[-1]
-    block, features = nodes_ref.shape
+    block, features = nodes_own.shape
     third = low_ref.shape[0]
     ext[0:third, :] = low_ref[...]
     ext[third : 2 * third, :] = mid_ref[...]
     ext[2 * third :, :] = high_ref[...]
-    nodes = nodes_ref[...]
     src_col = column(src_ref[...])
     dst_col = column(dst_ref[...])
     dst_rows = one_hot_rows(dst_ref[...], block)
@@ -128,25 +143,31 @@
         span = slice(start, start + CHUNK)
         gathered = mm(one_hot_cols(src_col[span], ext.shape[0]), ext[...]).astype(BF16)
         picked[span, :] = gathered
+        if start == 0:
+            for place in (4, 0, 1, 2):
+                copies[place].wait()
+            nodes = nodes_own[...]
         at_dst = one_hot_cols(dst_col[span], block)
         dst_cols[span, :] = at_dst
         local = mm(at_dst, nodes).astype(BF16)
-        pre_act = mm(gathered, w_src_ref[...]) + mm(local, w_dst_ref[...])
+        pre_act = mm(gathered, w_src[...]) + mm(local, w_dst[...])
         value, slope = silu_parts(pre_act)
         act_slope[span, :] = slope
         hid = value.astype(BF16)
         hidden[span, :] = hid
-        value, slope = silu_parts(mm(hid, w_msg_ref[...]))
+        value, slope = silu_parts(mm(hid, w_msg[...]))
         msg_slope[span, :] = slope
         inflow = inflow + mm(dst_rows[:, span], value.astype(BF16))
-    top_count = top_ref.shape[0]
-    top_nodes = top_ref[...]
-    top_table = mm(top_nodes, w_top_ref[...]).astype(BF16)
+    for place in (3, 5, 6):
+        copies[place].wait()
+    top_count = top_own.shape[0]
+    top_nodes = top_own[...]
+    top_table = mm(top_nodes, w_top[...]).astype(BF16)
     band_col = column(band_ref[...])
     node_pre = inflow + mm(one_hot_cols(band_col, top_count), top_table)
     value, slope = silu_parts(node_pre)
     updated_ref[...] = (nodes.astype(F32) + value).astype(BF16)
-    node_grad = (cot_ref[...].astype(F32) * slope).astype(BF16)
+    node_grad = (cot_own[...].astype(F32) * slope).astype(BF16)
     window = mm(one_hot_rows(band_ref[...], top_count), node_grad)
     window_ref[...] = window
     grads_ref[3] = mm_rows(top_nodes, window.astype(BF16)).astype(BF16)
@@ -156,7 +177,7 @@
         msg_grad = mm(dst_cols[span, :], node_grad)
         grad = (msg_grad * msg_slope[span, :]).astype(BF16)
         pre_grad[span, :] = grad
-        grad = (mm_cols(grad, w_msg_ref[...]) * act_slope[span, :]).astype(BF16)
+        grad = (mm_cols(grad, w_msg[...]) * act_slope[span, :]).astype(BF16)
         act_grad[span, :] = grad
         dst_grad = dst_grad + mm(dst_rows[:, span], grad)
     grads_ref[0] = mm_rows(picked[...], act_grad[...]).astype(BF16)
@@ -169,6 +190,8 @@
     slots = args[10].shape[-1]
     block, features = nodes.shape
     ext_rows = 3 * args[0].shape[0]
+    hbm = pltpu.MemorySpace.HBM
+    stay = [pltpu.with_memory_space_constraint(array, hbm) for array in args[3:10]]
     return pl.pallas_call(
         block_kernel,
         out_shape=(
@@ -185,10 +208,21 @@
             pltpu.VMEM((slots, features), F32),
             pltpu.VMEM((slots, features), F32),
             pltpu.VMEM((slots, block), BF16),
+            pltpu.VMEM((features, features), BF16),
+            pltpu.VMEM((features, features), BF16),
+            pltpu.VMEM((features, features), BF16),
+            pltpu.VMEM((features, features), BF16),
+            pltpu.VMEM((block, features), BF16),
+            pltpu.VMEM(top_nodes.shape, BF16),
+            pltpu.VMEM((block, features), BF16),
+            pltpu.SemaphoreType.DMA((7,)),
         ],
+        in_specs=[pl.BlockSpec(memory_space=pltpu.MemorySpace.VMEM)] * 3
+        + [pl.BlockSpec(memory_space=pltpu.MemorySpace.HBM)] * 7
+        + [pl.BlockSpec(memory_space=pltpu.MemorySpace.VMEM)] * 3,
         compiler_params=pltpu.CompilerParams(vmem_limit_bytes=48 << 20),
         name="block_round",
-    )(*args)
+    )(*args[:3], *stay, *args[10:])
 
 
 def shards(

time: 141 us -> 136 us (0.965)
  local copies, waits for them, and re-layouts: 9.34 us -> 2.61 us
  Pallas kernels: 8.92 us -> 10.6 us
    unnamed x17 -> x3, local copies, waits for them, and re-layouts: 8.05 us -> 1.32 us
    pallas_call x1, Pallas kernels: 8.92 us -> 10.6 us  [block_round(): pl.pallas_call(block_kernel, out_shape=(jax.ShapeDtypeStruct((block, feat...]
where the time goes in v3:
time: 136 us; the launch traced here: 135 us
  blocking collectives  77.7 us (57%)
  starting transfers between devices  21.9 us (16%)
  waiting for transfers between devices  15.7 us (12%)
  Pallas kernels  10.6 us (8%)
  other arithmetic  4.25 us (3%)
  local copies, waits for them, and re-layouts  2.61 us (2%)
  between operations  1.45 us (1%)
    all_to_all x5, blocking collectives, exchange(): return lax.all_to_all(part, axes, 0, 0, tiled=True)  77.7 us
    pallas_call x1, Pallas kernels, block_round(): pl.pallas_call(block_kernel, out_shape=(jax.ShapeDtypeStruct((block, feat...  10.6 us
    ppermute x2, starting transfers between devices, both_ways(): lax.ppermute(block, axis, forward)  9.94 us
    ppermute x2, waiting for transfers between devices, both_ways(): lax.ppermute(block, axis, backward)  7.66 us
    ppermute x1, waiting for transfers between devices, shards(): from_right = lax.ppermute(triple[:owner_rows], LON, backward)  6.97 us
    ppermute x2, starting transfers between devices, both_ways(): lax.ppermute(block, axis, backward)  3.9 us
    all_to_all x1, starting transfers between devices, exchange(): return lax.all_to_all(part, axes, 0, 0, tiled=True)  3.66 us
    ppermute x1, starting transfers between devices, shards(): from_left = lax.ppermute(triple[2 * owner_rows:], LON, forward)  3.14 us
  transfers between devices with their start and end apart: 7, of which 5 were waited for; matrix products, arithmetic and copies ran while one was open for 2% of the time, Pallas kernels for 0%

profile of v3, /device:TPU:1, one launch (start us, length us, event | category | flops | bytes accessed | tf_op | source)
XLA Modules:
  0.0 135.1 jit_solution(7613843472858819111)
XLA Ops:
  0.6 4.0 %collective-permute-start = (bf16[128,512]{1,0:T(8,128)(2,1)}, bf16[128,512]{1,0:T(8,128)(2,1)S(1)}, u32[]{:S(2)}, u32[]{:S(2)}) collective-permute-start(bf16[128,512]{1,0:T(8,128)(2,1)} %bitcast.29), channel_id=1, source_target_pairs={{0,1},{1,2},{2,3},{3,4},{4,5},{5,6},{6,7},{7,8},{8,9},{9,10},{10,1... | collective-permute-start | bytes 393224 | tf_op jit(solution)/shard_map/ppermute | solution.py:56
  4.6 1.3 collective-permute-start.1
  6.5 0.7 compare_select_fusion.dst_ref
  7.2 0.0 collective-permute-done
  7.3 3.3 %collective-permute-done.1 = bf16[128,512]{1,0:T(8,128)(2,1)S(1)} collective-permute-done((bf16[128,512]{1,0:T(8,128)(2,1)}, bf16[128,512]{1,0:T(8,128)(2,1)S(1)}, u32[]{:S(2)}, u32[]{:S(2)}) %collective-permute-start.1) | collective-permute-done | bytes 131104 | tf_op jit(solution)/shard_map/ppermute | solution.py:56
  10.5 0.9 pad_maximum_fusion.mid_ref
  11.5 6.0 %collective-permute-start.2 = (bf16[384,512]{1,0:T(8,128)(2,1)S(1)}, bf16[384,512]{1,0:T(8,128)(2,1)S(1)}, u32[]{:S(2)}, u32[]{:S(2)}) collective-permute-start(bf16[384,512]{1,0:T(8,128)(2,1)S(1)} %pad_maximum_fusion.mid_ref), channel_id=1, source_target_pairs={{0,16},{16,32},{32,48},{48,64},{64,80},{80,96},{96,112},{112,128},... | collective-permute-start | bytes 1179656 | tf_op jit(solution)/shard_map/ppermute | solution.py:56
  17.4 2.6 %collective-permute-start.3 = (bf16[384,512]{1,0:T(8,128)(2,1)S(1)}, bf16[384,512]{1,0:T(8,128)(2,1)S(1)}, u32[]{:S(2)}, u32[]{:S(2)}) collective-permute-start(bf16[384,512]{1,0:T(8,128)(2,1)S(1)} %pad_maximum_fusion.mid_ref), channel_id=1, source_target_pairs={{16,0},{32,16},{48,32},{64,48},{80,64},{96,80},{112,96},{128,112},... | collective-permute-start | bytes 1179656 | tf_op jit(solution)/shard_map/ppermute | solution.py:56
  20.1 0.7 subtract_bitcast_fusion.band_ref
  20.7 0.7 add_bitcast_fusion.src_ref
  21.4 0.7 collective-permute-done.2.low_ref
  22.1 4.4 %collective-permute-done.3.high_ref = bf16[384,512]{1,0:T(8,128)(2,1)S(1)} collective-permute-done((bf16[384,512]{1,0:T(8,128)(2,1)S(1)}, bf16[384,512]{1,0:T(8,128)(2,1)S(1)}, u32[]{:S(2)}, u32[]{:S(2)}) %collective-permute-start.3) | collective-permute-done | bytes 393248 | tf_op jit(solution)/shard_map/ppermute | solution.py:56
  26.5 10.6 %block_round.1 = (bf16[128,512]{1,0:T(8,128)(2,1)}, bf16[4,512,512]{2,1,0:T(8,128)(2,1)S(1)}, f32[32,512]{1,0:T(8,128)S(1)}) custom-call(bf16[384,512]{1,0:T(8,128)(2,1)S(1)} %collective-permute-done.2.low_ref, bf16[384,512]{1,0:T(8,128)(2,1)S(1)} %pad_maximum_fusion.mid_ref, bf16[384,512]{1,0:T(8,128)(2,1)S(1)} %collective-permute-done.3.high_ref, ...), custom_call_target="tpu_custom_call" | custom-call | tf_op jit(solution)/shard_map/block_round/pallas_call | solution.py:195
  37.1 5.1 %all_to_all.45 = bf16[2,1024,512]{2,1,0:T(8,128)(2,1)S(1)} all-to-all(bf16[2,1024,512]{2,1,0:T(8,128)(2,1)S(1)} %bitcast.25), channel_id=1, replica_groups=mesh['x_hi'=2,'z_hi'=4,'z_lo'=2,'core'=2,'y_hi'=4,'y_lo'=2,'x_lo'=2] {'c..., dimensions={0} | all-to-all | bytes 4194304 | tf_op jit(solution)/shard_map/all_to_all | solution.py:23
  42.2 1.1 reduce_sum.33
  43.3 25.7 %all_to_all.46 = bf16[16,64,512]{2,1,0:T(8,128)(2,1)S(1)} all-to-all(bf16[16,64,512]{2,1,0:T(8,128)(2,1)S(1)} %bitcast.28), channel_id=1, replica_groups=mesh['x_hi'=2,'z_hi'=4,'z_lo'=2,'core'=2,'y_hi'=4,'y_lo'=2,'x_lo'=2] {'x..., dimensions={0} | all-to-all | bytes 2097152 | tf_op jit(solution)/shard_map/all_to_all | solution.py:23
  69.0 0.1 reduce_sum.34
  69.1 0.0 copy-start
  69.2 22.7 %all_to_all.47 = bf16[16,16,128]{2,1,0:T(8,128)(2,1)S(1)} all-to-all(bf16[16,16,128]{2,1,0:T(8,128)(2,1)S(1)} %bitcast.35), channel_id=1, replica_groups=mesh['x_hi'=2,'z_hi'=4,'z_lo'=2,'core'=2,'y_hi'=4,'y_lo'=2,'x_lo'=2] {'z..., dimensions={0} | all-to-all | bytes 131072 | tf_op jit(solution)/shard_map/all_to_all | solution.py:23
  91.9 13.9 %all_to_all.48 = bf16[16,16,128]{2,1,0:T(8,128)(2,1)S(1)} all-to-all(bf16[16,16,128]{2,1,0:T(8,128)(2,1)S(1)} %broadcast_in_dim.26), channel_id=1, replica_groups=mesh['x_hi'=2,'z_hi'=4,'z_lo'=2,'core'=2,'y_hi'=4,'y_lo'=2,'x_lo'=2] {'z..., dimensions={0} | all-to-all | bytes 131072 | tf_op jit(solution)/shard_map/all_to_all | solution.py:23
  105.9 1.1 broadcast_in_dim.28
  106.9 3.7 %all-to-all-start.4 = ((bf16[16,64,512]{2,1,0:T(8,128)(2,1)}), bf16[16,64,512]{2,1,0:T(8,128)(2,1)S(1)}, u32[]{:S(2)}, u32[]{:S(2)}) async-start(bf16[16,64,512]{2,1,0:T(8,128)(2,1)} %broadcast_in_dim.28), calls=%async_computation.4 | async-start | bytes 2097152 | tf_op jit(solution)/shard_map/all_to_all | solution.py:23
  110.6 3.1 %collective-permute-start.4 = (f32[2,512]{1,0:T(2,128)S(1)}, f32[2,512]{1,0:T(2,128)S(1)}, u32[]{:S(2)}, u32[]{:S(2)}) collective-permute-start(f32[2,512]{1,0:T(2,128)S(1)} %get-tuple-element.9), channel_id=1, source_target_pairs={{0,1},{1,2},{2,3},{3,4},{4,5},{5,6},{6,7},{7,8},{8,9},{9,10},{10,1... | collective-permute-start | bytes 12296 | tf_op jit(solution)/shard_map/ppermute | solution.py:279
  113.8 1.3 collective-permute-start.5
  115.1 0.0 collective-permute-done.4
  115.1 7.0 %collective-permute-done.5 = f32[2,512]{1,0:T(2,128)S(1)} collective-permute-done((f32[2,512]{1,0:T(2,128)S(1)}, f32[2,512]{1,0:T(2,128)S(1)}, u32[]{:S(2)}, u32[]{:S(2)}) %collective-permute-start.5) | collective-permute-done | bytes 4128 | tf_op jit(solution)/shard_map/ppermute | solution.py:280
  122.1 0.0 copy-done
  122.1 0.8 convolution_convert_fusion
  122.9 0.4 all-to-all-done.4
  123.3 0.1 broadcast_in_dim.30
  123.4 10.3 %all_to_all.49 = bf16[2,1024,512]{2,1,0:T(8,128)(2,1)S(1)} all-to-all(bf16[2,1024,512]{2,1,0:T(8,128)(2,1)S(1)} %broadcast_in_dim.30), channel_id=1, replica_groups=mesh['x_hi'=2,'z_hi'=4,'z_lo'=2,'core'=2,'y_hi'=4,'y_lo'=2,'x_lo'=2] {'c..., dimensions={0} | all-to-all | bytes 4194304 | tf_op jit(solution)/shard_map/all_to_all | solution.py:23
  133.8 1.3 copy.24
  (7 shorter events, 0.1 us)
Async XLA Ops:
  0.6 6.6 %collective-permute-start = (bf16[128,512]{1,0:T(8,128)(2,1)}, bf16[128,512]{1,0:T(8,128)(2,1)S(1)}, u32[]{:S(2)}, u32[]{:S(2)}) collective-permute-start(bf16[128,512]{1,0:T(8,128)(2,1)} %bitcast.29), channel_id=1, source_target_pairs={{0,1},{1,2},{2,3},{3,4},{4,5},{5,6},{6,7},{7,8},{8,9},{9,10},{10,1... | collective-permute-start | bytes 393224 | tf_op jit(solution)/shard_map/ppermute | solution.py:56
  4.6 5.9 %collective-permute-start.1 = (bf16[128,512]{1,0:T(8,128)(2,1)}, bf16[128,512]{1,0:T(8,128)(2,1)S(1)}, u32[]{:S(2)}, u32[]{:S(2)}) collective-permute-start(bf16[128,512]{1,0:T(8,128)(2,1)} %bitcast.30), channel_id=1, source_target_pairs={{1,0},{2,1},{3,2},{4,3},{5,4},{6,5},{7,6},{8,7},{9,8},{10,9},{11,1... | collective-permute-start | bytes 393224 | tf_op jit(solution)/shard_map/ppermute | solution.py:56
  11.5 10.7 %collective-permute-start.2 = (bf16[384,512]{1,0:T(8,128)(2,1)S(1)}, bf16[384,512]{1,0:T(8,128)(2,1)S(1)}, u32[]{:S(2)}, u32[]{:S(2)}) collective-permute-start(bf16[384,512]{1,0:T(8,128)(2,1)S(1)} %pad_maximum_fusion.mid_ref), channel_id=1, source_target_pairs={{0,16},{16,32},{32,48},{48,64},{64,80},{80,96},{96,112},{112,128},... | collective-permute-start | bytes 1179656 | tf_op jit(solution)/shard_map/ppermute | solution.py:56
  17.4 9.1 %collective-permute-start.3 = (bf16[384,512]{1,0:T(8,128)(2,1)S(1)}, bf16[384,512]{1,0:T(8,128)(2,1)S(1)}, u32[]{:S(2)}, u32[]{:S(2)}) collective-permute-start(bf16[384,512]{1,0:T(8,128)(2,1)S(1)} %pad_maximum_fusion.mid_ref), channel_id=1, source_target_pairs={{16,0},{32,16},{48,32},{64,48},{80,64},{96,80},{112,96},{128,112},... | collective-permute-start | bytes 1179656 | tf_op jit(solution)/shard_map/ppermute | solution.py:56
  69.1 53.0 %copy-start = (bf16[512,512]{1,0:T(8,128)(2,1)S(1)}, bf16[512,512]{1,0:T(8,128)(2,1)}, u32[]{:S(2)}) copy-start(bf16[512,512]{1,0:T(8,128)(2,1)} %w_top_ref.1) | copy-start | bytes 1572868
  106.9 16.4 %all-to-all-start.4 = ((bf16[16,64,512]{2,1,0:T(8,128)(2,1)}), bf16[16,64,512]{2,1,0:T(8,128)(2,1)S(1)}, u32[]{:S(2)}, u32[]{:S(2)}) async-start(bf16[16,64,512]{2,1,0:T(8,128)(2,1)} %broadcast_in_dim.28), calls=%async_computation.4 | async-start | bytes 2097152 | tf_op jit(solution)/shard_map/all_to_all | solution.py:23
  110.6 4.4 %collective-permute-start.4 = (f32[2,512]{1,0:T(2,128)S(1)}, f32[2,512]{1,0:T(2,128)S(1)}, u32[]{:S(2)}, u32[]{:S(2)}) collective-permute-start(f32[2,512]{1,0:T(2,128)S(1)} %get-tuple-element.9), channel_id=1, source_target_pairs={{0,1},{1,2},{2,3},{3,4},{4,5},{5,6},{6,7},{7,8},{8,9},{9,10},{10,1... | collective-permute-start | bytes 12296 | tf_op jit(solution)/shard_map/ppermute | solution.py:279
  113.8 8.3 %collective-permute-start.5 = (f32[2,512]{1,0:T(2,128)S(1)}, f32[2,512]{1,0:T(2,128)S(1)}, u32[]{:S(2)}, u32[]{:S(2)}) collective-permute-start(f32[2,512]{1,0:T(2,128)S(1)} %get-tuple-element.10), channel_id=1, source_target_pairs={{1,0},{2,1},{3,2},{4,3},{5,4},{6,5},{7,6},{8,7},{9,8},{10,9},{11,1... | collective-permute-start | bytes 12296 | tf_op jit(solution)/shard_map/ppermute | solution.py:280

commit v4 on v3

--- a/solution.py
+++ b/solution.py
@@ -10,10 +10,9 @@
 
 LAT = ("x_hi", "z_hi", "z_lo", "core")
 LON = ("y_hi", "y_lo", "x_lo")
-NEAR = ("x_hi", "z_lo", "y_lo", "x_lo")
-FAR = ("z_hi", "y_hi")
-CORE = ("core",)
-LANES = 128
+RING_X = ("x_hi", "x_lo")
+RING_Y = ("y_hi", "y_lo")
+RING_Z = ("z_hi", "z_lo")
 CHUNK = 256
 BF16 = jnp.bfloat16
 F32 = jnp.float32
@@ -35,18 +34,40 @@
     return exchange(copies.reshape(-1, part.shape[-1]), axes)
 
 
-def all_sum(part, scale):
-    features = part.shape[-1]
-    tiles = features // LANES
-    part = reduce_stage(part, CORE).astype(BF16)
-    part = reduce_stage(part, NEAR).astype(BF16)
-    rows = part.shape[0]
-    part = part.reshape(rows, tiles, LANES).transpose(1, 0, 2).reshape(-1, LANES)
-    part = (reduce_stage(part, FAR) * scale).astype(BF16)
-    part = gather_stage(part, FAR)
-    part = part.reshape(tiles, rows, LANES).transpose(1, 0, 2).reshape(rows, features)
-    part = gather_stage(part, NEAR)
-    return gather_stage(part, CORE)
+def swap_cores(part):
+    return lax.ppermute(part, "core", [(0, 1), (1, 0)])
+
+
+def reduce_all(keep, send, scale):
+    part = (keep.astype(F32) + swap_cores(send).astype(F32)).astype(BF16)
+    part = reduce_stage(part, RING_X).astype(BF16)
+    part = reduce_stage(part, RING_Y).astype(BF16)
+    every = gather_stage(part, RING_Z).reshape((-1,) + part.shape)
+    part = (jnp.sum(every.astype(F32), axis=0) * scale).astype(BF16)
+    return gather_stage(part, RING_Y)
+
+
+def place_kernel(mine_ref, other_ref, core_ref, out_ref, placed):
+    core = core_ref[0]
+    first = pltpu.make_async_copy(mine_ref, out_ref.at[core], placed.at[0])
+    second = pltpu.make_async_copy(other_ref, out_ref.at[1 - core], placed.at[1])
+    first.start()
+    second.start()
+    first.wait()
+    second.wait()
+
+
+def both_halves(mine):
+    other = swap_cores(mine)
+    vmem = pl.BlockSpec(memory_space=pltpu.MemorySpace.VMEM)
+    return pl.pallas_call(
+        place_kernel,
+        out_shape=jax.ShapeDtypeStruct((2,) + mine.shape, mine.dtype),
+        in_specs=[vmem, vmem, pl.BlockSpec(memory_space=pltpu.MemorySpace.SMEM)],
+        out_specs=pl.BlockSpec(memory_space=pltpu.MemorySpace.HBM),
+        scratch_shapes=[pltpu.SemaphoreType.DMA((2,))],
+        name="both_halves",
+    )(mine, other, lax.axis_index("core").reshape(1))
 
 
 def both_ways(block, axis):
@@ -101,8 +122,10 @@
     src_ref,
     dst_ref,
     band_ref,
+    core_ref,
     updated_ref,
-    grads_ref,
+    keep_ref,
+    send_ref,
     window_ref,
     ext,
     picked,
@@ -121,6 +144,17 @@
     cot_own,
     arrived,
 ):
+    core = core_ref[0]
+
+    def emit(place, grad):
+        @pl.when(core == place // 2)
+        def _():
+            keep_ref[place % 2] = grad
+
+        @pl.when(core != place // 2)
+        def _():
+            send_ref[place % 2] = grad
+
     held = (w_src, w_dst, w_msg, w_top, nodes_own, top_own, cot_own)
     sources = (w_src_ref, w_dst_ref, w_msg_ref, w_top_ref, nodes_ref, top_ref, cot_ref)
     copies = [
@@ -170,7 +204,7 @@
     node_grad = (cot_own[...].astype(F32) * slope).astype(BF16)
     window = mm(one_hot_rows(band_ref[...], top_count), node_grad)
     window_ref[...] = window
-    grads_ref[3] = mm_rows(top_nodes, window.astype(BF16)).astype(BF16)
+    emit(3, mm_rows(top_nodes, window.astype(BF16)).astype(BF16))
     dst_grad = jnp.zeros((block, features), F32)
     for start in range(0, slots, CHUNK):
         span = slice(start, start + CHUNK)
@@ -180,9 +214,9 @@
         grad = (mm_cols(grad, w_msg[...]) * act_slope[span, :]).astype(BF16)
         act_grad[span, :] = grad
         dst_grad = dst_grad + mm(dst_rows[:, span], grad)
-    grads_ref[0] = mm_rows(picked[...], act_grad[...]).astype(BF16)
-    grads_ref[1] = mm_rows(nodes, dst_grad.astype(BF16)).astype(BF16)
-    grads_ref[2] = mm_rows(hidden[...], pre_grad[...]).astype(BF16)
+    emit(0, mm_rows(picked[...], act_grad[...]).astype(BF16))
+    emit(1, mm_rows(nodes, dst_grad.astype(BF16)).astype(BF16))
+    emit(2, mm_rows(hidden[...], pre_grad[...]).astype(BF16))
 
 
 def block_round(*args):
@@ -196,7 +230,8 @@
         block_kernel,
         out_shape=(
             jax.ShapeDtypeStruct((block, features), BF16),
-            jax.ShapeDtypeStruct((4, features, features), BF16),
+            jax.ShapeDtypeStruct((2, features, features), BF16),
+            jax.ShapeDtypeStruct((2, features, features), BF16),
             jax.ShapeDtypeStruct((top_nodes.shape[0], features), F32),
         ),
         scratch_shapes=[
@@ -219,7 +254,8 @@
         ],
         in_specs=[pl.BlockSpec(memory_space=pltpu.MemorySpace.VMEM)] * 3
         + [pl.BlockSpec(memory_space=pltpu.MemorySpace.HBM)] * 7
-        + [pl.BlockSpec(memory_space=pltpu.MemorySpace.VMEM)] * 3,
+        + [pl.BlockSpec(memory_space=pltpu.MemorySpace.VMEM)] * 3
+        + [pl.BlockSpec(memory_space=pltpu.MemorySpace.SMEM)],
         compiler_params=pltpu.CompilerParams(vmem_limit_bytes=48 << 20),
         name="block_round",
     )(*args[:3], *stay, *args[10:])
@@ -253,7 +289,7 @@
     live_slot = lax.broadcasted_iota(jnp.int32, (1, slots), 1) < edge_count
     dst_idx = jnp.where(live_slot, dst_node.reshape(1, slots), block_size)
     band_ids = parent.reshape(1, block_size) - band_start
-    updated, grads, window = block_round(
+    updated, keep, send, window = block_round(
         low,
         mid,
         high,
@@ -267,10 +303,13 @@
         src_idx,
         dst_idx,
         band_ids,
+        lax.axis_index("core").reshape(1),
     )
     nodes_total = block_size * lax.axis_size(LAT) * lax.axis_size(LON)
     grad_scale = 8.0 / math.sqrt(nodes_total)
-    weight_grads = all_sum(grads.reshape(-1, features), grad_scale)
+    quarter = reduce_all(keep.reshape(-1, features), send.reshape(-1, features), grad_scale)
+    window, quarter = lax.optimization_barrier((window, quarter))
+    mine = gather_stage(quarter, RING_X)
     padded = jnp.pad(window, ((owner_rows, owner_rows), (0, 0)))
     triple = lax.dynamic_slice_in_dim(padded, lon_index * owner_rows, 3 * owner_rows, 0)
     count = lax.axis_size(LON)
@@ -278,6 +317,8 @@
     backward = [(target, source) for source, target in forward]
     from_left = lax.ppermute(triple[2 * owner_rows :], LON, forward)
     from_right = lax.ppermute(triple[:owner_rows], LON, backward)
+    mine, from_left, from_right = lax.optimization_barrier((mine, from_left, from_right))
+    weight_grads = both_halves(mine)
     table_grad = (triple[owner_rows : 2 * owner_rows] + from_left + from_right).astype(BF16)
     d_top = lax.dot_general(
         table_grad, w_top, (((1,), (1,)), ((), ())), preferred_element_type=F32

time: 136 us -> 143 us (1.051)
  starting transfers between devices: 21.9 us -> 34.8 us
  blocking collectives: 77.7 us -> 69.7 us
  Pallas kernels: 10.6 us -> 14.8 us
    ppermute x0 -> x2, starting transfers between devices: none -> 10.6 us  [swap_cores(): return lax.ppermute(part, 'core', [(0, 1), (1, 0)])]
    all_to_all x5 -> x4, blocking collectives: 77.7 us -> 69.7 us  [exchange(): return lax.all_to_all(part, axes, 0, 0, tiled=True)]
    ppermute x2, waiting for transfers between devices: 7.66 us -> 0.24 us  [both_ways(): lax.ppermute(block, axis, backward)]
    ppermute x2, waiting for transfers between devices: 0.71 us -> 5.71 us  [both_ways(): lax.ppermute(block, axis, forward)]
    ppermute x2, starting transfers between devices: 3.9 us -> 8.88 us  [both_ways(): lax.ppermute(block, axis, backward)]
    ppermute x1, waiting for transfers between devices: 6.97 us -> 2.91 us  [shards(): from_right = lax.ppermute(triple[:owner_rows], LON, backward)]
    ppermute x0 -> x2, waiting for transfers between devices: none -> 4.04 us  [swap_cores(): return lax.ppermute(part, 'core', [(0, 1), (1, 0)])]
    ppermute x2, starting transfers between devices: 9.94 us -> 6.51 us  [both_ways(): lax.ppermute(block, axis, forward)]
  transfers between devices with their start and end apart: 7 -> 9, of which waited for: 5 -> 7; matrix products, arithmetic and copies ran while one was open for 2% -> 2% of each run, Pallas kernels for 0% -> 0%
where the time goes in v4:
time: 143 us; the launch traced here: 142 us
  blocking collectives  69.7 us (49%)
  starting transfers between devices  34.8 us (24%)
  Pallas kernels  14.8 us (10%)
  waiting for transfers between devices  14.4 us (10%)
  other arithmetic  3.68 us (3%)
  local copies, waits for them, and re-layouts  2.16 us (2%)
  between operations  1.45 us (1%)
    all_to_all x4, blocking collectives, exchange(): return lax.all_to_all(part, axes, 0, 0, tiled=True)  69.7 us
    pallas_call x1, Pallas kernels, block_round(): pl.pallas_call(block_kernel, out_shape=(jax.ShapeDtypeStruct((block, feat...  11.9 us
    ppermute x2, starting transfers between devices, swap_cores(): return lax.ppermute(part, 'core', [(0, 1), (1, 0)])  10.6 us
    ppermute x2, starting transfers between devices, both_ways(): lax.ppermute(block, axis, backward)  8.88 us
    ppermute x2, starting transfers between devices, both_ways(): lax.ppermute(block, axis, forward)  6.51 us
    ppermute x2, waiting for transfers between devices, both_ways(): lax.ppermute(block, axis, forward)  5.71 us
    ppermute x2, waiting for transfers between devices, swap_cores(): return lax.ppermute(part, 'core', [(0, 1), (1, 0)])  4.04 us
    ppermute x1, starting transfers between devices, shards(): from_left = lax.ppermute(triple[2 * owner_rows:], LON, forward)  3.99 us
  transfers between devices with their start and end apart: 9, of which 7 were waited for; matrix products, arithmetic and copies ran while one was open for 2% of the time, Pallas kernels for 0%

profile of v4, /device:TPU:1, one launch (start us, length us, event | category | flops | bytes accessed | tf_op | source)
XLA Modules:
  0.0 141.8 jit_solution(11900955887707138173)
XLA Ops:
  0.6 1.3 collective-permute-start.1
  1.9 4.6 %collective-permute-start = (bf16[128,512]{1,0:T(8,128)(2,1)}, bf16[128,512]{1,0:T(8,128)(2,1)S(1)}, u32[]{:S(2)}, u32[]{:S(2)}) collective-permute-start(bf16[128,512]{1,0:T(8,128)(2,1)} %bitcast.30), channel_id=1, source_target_pairs={{0,1},{1,2},{2,3},{3,4},{4,5},{5,6},{6,7},{7,8},{8,9},{9,10},{10,1... | collective-permute-start | bytes 393224 | tf_op jit(solution)/shard_map/ppermute | solution.py:77
  7.2 0.7 compare_select_fusion.dst_ref
  7.9 0.0 collective-permute-done.1
  7.9 2.6 %collective-permute-done = bf16[128,512]{1,0:T(8,128)(2,1)S(1)} collective-permute-done((bf16[128,512]{1,0:T(8,128)(2,1)}, bf16[128,512]{1,0:T(8,128)(2,1)S(1)}, u32[]{:S(2)}, u32[]{:S(2)}) %collective-permute-start) | collective-permute-done | bytes 131104 | tf_op jit(solution)/shard_map/ppermute | solution.py:77
  10.5 0.9 pad_maximum_fusion.mid_ref
  11.4 7.6 %collective-permute-start.3 = (bf16[384,512]{1,0:T(8,128)(2,1)S(1)}, bf16[384,512]{1,0:T(8,128)(2,1)S(1)}, u32[]{:S(2)}, u32[]{:S(2)}) collective-permute-start(bf16[384,512]{1,0:T(8,128)(2,1)S(1)} %pad_maximum_fusion.mid_ref), channel_id=1, source_target_pairs={{16,0},{32,16},{48,32},{64,48},{80,64},{96,80},{112,96},{128,112},... | collective-permute-start | bytes 1179656 | tf_op jit(solution)/shard_map/ppermute | solution.py:77
  19.0 1.9 %collective-permute-start.2 = (bf16[384,512]{1,0:T(8,128)(2,1)S(1)}, bf16[384,512]{1,0:T(8,128)(2,1)S(1)}, u32[]{:S(2)}, u32[]{:S(2)}) collective-permute-start(bf16[384,512]{1,0:T(8,128)(2,1)S(1)} %pad_maximum_fusion.mid_ref), channel_id=1, source_target_pairs={{0,16},{16,32},{32,48},{48,64},{64,80},{80,96},{96,112},{112,128},... | collective-permute-start | bytes 1179656 | tf_op jit(solution)/shard_map/ppermute | solution.py:77
  21.0 0.7 subtract_bitcast_fusion.band_ref
  21.6 0.7 add_bitcast_fusion.src_ref
  22.3 0.2 collective-permute-done.3.high_ref
  22.6 3.1 %collective-permute-done.2.low_ref = bf16[384,512]{1,0:T(8,128)(2,1)S(1)} collective-permute-done((bf16[384,512]{1,0:T(8,128)(2,1)S(1)}, bf16[384,512]{1,0:T(8,128)(2,1)S(1)}, u32[]{:S(2)}, u32[]{:S(2)}) %collective-permute-start.2) | collective-permute-done | bytes 393248 | tf_op jit(solution)/shard_map/ppermute | solution.py:77
  25.7 11.9 %block_round.1 = (bf16[128,512]{1,0:T(8,128)(2,1)}, bf16[2,512,512]{2,1,0:T(8,128)(2,1)S(1)}, bf16[2,512,512]{2,1,0:T(8,128)(2,1)S(1)}, f32[32,512]{1,0:T(8,128)S(1)}) custom-call(bf16[384,512]{1,0:T(8,128)(2,1)S(1)} %collective-permute-done.2.low_ref, bf16[384,512]{1,0:T(8,128)(2,1)S(1)} %pad_maximum_fusion.mid_ref, ...), custom_call_target="tpu_custom_call" | custom-call | tf_op jit(solution)/shard_map/block_round/pallas_call | solution.py:229
  37.6 1.9 %collective-permute-start.4 = (bf16[1024,512]{1,0:T(8,128)(2,1)S(1)}, bf16[1024,512]{1,0:T(8,128)(2,1)S(1)}, u32[]{:S(2)}, u32[]{:S(2)}) collective-permute-start(bf16[1024,512]{1,0:T(8,128)(2,1)S(1)} %bitcast.22), channel_id=1, source_target_pairs={{0,16},{16,0},{1,17},{17,1},{2,18},{18,2},{3,19},{19,3},{4,20},{20... | collective-permute-start | bytes 3145736 | tf_op jit(solution)/shard_map/ppermute | solution.py:38
  39.5 2.6 %collective-permute-done.4 = bf16[1024,512]{1,0:T(8,128)(2,1)S(1)} collective-permute-done((bf16[1024,512]{1,0:T(8,128)(2,1)S(1)}, bf16[1024,512]{1,0:T(8,128)(2,1)S(1)}, u32[]{:S(2)}, u32[]{:S(2)}) %collective-permute-start.4) | collective-permute-done | bytes 1048608 | tf_op jit(solution)/shard_map/ppermute | solution.py:38
  42.1 0.4 fusion
  42.5 30.0 %all_to_all.42 = bf16[4,256,512]{2,1,0:T(8,128)(2,1)S(1)} all-to-all(bf16[4,256,512]{2,1,0:T(8,128)(2,1)S(1)} %bitcast.25), channel_id=1, replica_groups=mesh['x_hi'=2,'z_hi'=4,'z_lo'=2,'core'=2,'y_hi'=4,'y_lo'=2,'x_lo'=2] {'x..., dimensions={0} | all-to-all | bytes 2097152 | tf_op jit(solution)/shard_map/all_to_all | solution.py:22
  72.5 0.2 reduce_sum.33
  72.7 15.9 %all_to_all.43 = bf16[8,32,512]{2,1,0:T(8,128)(2,1)S(1)} all-to-all(bf16[8,32,512]{2,1,0:T(8,128)(2,1)S(1)} %bitcast.27), channel_id=1, replica_groups=mesh['x_hi'=2,'z_hi'=4,'z_lo'=2,'core'=2,'y_hi'=4,'y_lo'=2,'x_lo'=2] {'y..., dimensions={0} | all-to-all | bytes 524288 | tf_op jit(solution)/shard_map/all_to_all | solution.py:22
  88.7 11.9 %all_to_all.44 = bf16[8,32,512]{2,1,0:T(8,128)(2,1)S(1)} all-to-all(bf16[8,32,512]{2,1,0:T(8,128)(2,1)S(1)} %broadcast_in_dim.11), channel_id=1, replica_groups=mesh['x_hi'=2,'z_hi'=4,'z_lo'=2,'core'=2,'y_hi'=4,'y_lo'=2,'x_lo'=2] {'z..., dimensions={0} | all-to-all | bytes 524288 | tf_op jit(solution)/shard_map/all_to_all | solution.py:22
  100.7 0.0 copy-start.1
  100.7 12.0 %all_to_all.45 = bf16[8,32,512]{2,1,0:T(8,128)(2,1)S(1)} all-to-all(bf16[8,32,512]{2,1,0:T(8,128)(2,1)S(1)} %broadcast_in_dim.12), channel_id=1, replica_groups=mesh['x_hi'=2,'z_hi'=4,'z_lo'=2,'core'=2,'y_hi'=4,'y_lo'=2,'x_lo'=2] {'y..., dimensions={0} | all-to-all | bytes 524288 | tf_op jit(solution)/shard_map/all_to_all | solution.py:22
  112.6 1.1 broadcast_in_dim.13
  113.7 3.5 %all-to-all-start.4 = ((bf16[4,256,512]{2,1,0:T(8,128)(2,1)}), bf16[4,256,512]{2,1,0:T(8,128)(2,1)S(1)}, u32[]{:S(2)}, u32[]{:S(2)}) async-start(bf16[4,256,512]{2,1,0:T(8,128)(2,1)} %broadcast_in_dim.13), calls=%async_computation.4 | async-start | bytes 2097152 | tf_op jit(solution)/shard_map/all_to_all | solution.py:22
  117.3 1.3 collective-permute-start.6
  118.6 4.0 %collective-permute-start.5 = (f32[2,512]{1,0:T(2,128)S(1)}, f32[2,512]{1,0:T(2,128)S(1)}, u32[]{:S(2)}, u32[]{:S(2)}) collective-permute-start(f32[2,512]{1,0:T(2,128)S(1)} %get-tuple-element.22), channel_id=1, source_target_pairs={{0,1},{1,2},{2,3},{3,4},{4,5},{5,6},{6,7},{7,8},{8,9},{9,10},{10,1... | collective-permute-start | bytes 12296 | tf_op jit(solution)/shard_map/ppermute | solution.py:318
  122.5 2.9 %collective-permute-done.6 = f32[2,512]{1,0:T(2,128)S(1)} collective-permute-done((f32[2,512]{1,0:T(2,128)S(1)}, f32[2,512]{1,0:T(2,128)S(1)}, u32[]{:S(2)}, u32[]{:S(2)}) %collective-permute-start.6) | collective-permute-done | bytes 4128 | tf_op jit(solution)/shard_map/ppermute | solution.py:319
  125.5 0.0 collective-permute-done.5
  125.5 1.5 %all-to-all-done.4 = bf16[4,256,512]{2,1,0:T(8,128)(2,1)S(1)} async-done(((bf16[4,256,512]{2,1,0:T(8,128)(2,1)}), bf16[4,256,512]{2,1,0:T(8,128)(2,1)S(1)}, u32[]{:S(2)}, u32[]{:S(2)}) %all-to-all-start.4) | async-done | bytes 1048608 | tf_op jit(solution)/shard_map/all_to_all | solution.py:22
  127.0 0.0 copy-start
  127.0 8.7 %collective-permute-start.7 = (bf16[1024,512]{1,0:T(8,128)(2,1)S(1)}, bf16[1024,512]{1,0:T(8,128)(2,1)S(1)}, u32[]{:S(2)}, u32[]{:S(2)}) collective-permute-start(bf16[1024,512]{1,0:T(8,128)(2,1)S(1)} %bitcast.23), channel_id=1, source_target_pairs={{0,16},{16,0},{1,17},{17,1},{2,18},{18,2},{3,19},{19,3},{4,20},{20... | collective-permute-start | bytes 3145736 | tf_op jit(solution)/shard_map/ppermute | solution.py:38
  135.7 0.0 copy-done.1
  135.7 0.8 convolution_convert_fusion
  136.5 1.4 collective-permute-done.7.other_ref
  137.9 0.0 copy-done
  137.9 0.0 copy-start.2
  137.9 1.0 copy-done.2
  139.0 2.9 %both_halves.1 = bf16[2,1024,512]{2,1,0:T(8,128)(2,1)} custom-call(bf16[1024,512]{1,0:T(8,128)(2,1)} %bitcast.24, bf16[1024,512]{1,0:T(8,128)(2,1)} %copy-done.2, s32[1]{0:T(128)} %bitcast.6.core_ref), custom_call_target="tpu_custom_call" | custom-call | tf_op jit(solution)/shard_map/both_halves/pallas_call | solution.py:63
  (6 shorter events, 0.1 us)
Async XLA Ops:
  0.6 7.2 %collective-permute-start.1 = (bf16[128,512]{1,0:T(8,128)(2,1)}, bf16[128,512]{1,0:T(8,128)(2,1)S(1)}, u32[]{:S(2)}, u32[]{:S(2)}) collective-permute-start(bf16[128,512]{1,0:T(8,128)(2,1)} %bitcast.29), channel_id=1, source_target_pairs={{1,0},{2,1},{3,2},{4,3},{5,4},{6,5},{7,6},{8,7},{9,8},{10,9},{11,1... | collective-permute-start | bytes 393224 | tf_op jit(solution)/shard_map/ppermute | solution.py:77
  1.9 8.6 %collective-permute-start = (bf16[128,512]{1,0:T(8,128)(2,1)}, bf16[128,512]{1,0:T(8,128)(2,1)S(1)}, u32[]{:S(2)}, u32[]{:S(2)}) collective-permute-start(bf16[128,512]{1,0:T(8,128)(2,1)} %bitcast.30), channel_id=1, source_target_pairs={{0,1},{1,2},{2,3},{3,4},{4,5},{5,6},{6,7},{7,8},{8,9},{9,10},{10,1... | collective-permute-start | bytes 393224 | tf_op jit(solution)/shard_map/ppermute | solution.py:77
  11.4 11.1 %collective-permute-start.3 = (bf16[384,512]{1,0:T(8,128)(2,1)S(1)}, bf16[384,512]{1,0:T(8,128)(2,1)S(1)}, u32[]{:S(2)}, u32[]{:S(2)}) collective-permute-start(bf16[384,512]{1,0:T(8,128)(2,1)S(1)} %pad_maximum_fusion.mid_ref), channel_id=1, source_target_pairs={{16,0},{32,16},{48,32},{64,48},{80,64},{96,80},{112,96},{128,112},... | collective-permute-start | bytes 1179656 | tf_op jit(solution)/shard_map/ppermute | solution.py:77
  19.0 6.6 %collective-permute-start.2 = (bf16[384,512]{1,0:T(8,128)(2,1)S(1)}, bf16[384,512]{1,0:T(8,128)(2,1)S(1)}, u32[]{:S(2)}, u32[]{:S(2)}) collective-permute-start(bf16[384,512]{1,0:T(8,128)(2,1)S(1)} %pad_maximum_fusion.mid_ref), channel_id=1, source_target_pairs={{0,16},{16,32},{32,48},{48,64},{64,80},{80,96},{96,112},{112,128},... | collective-permute-start | bytes 1179656 | tf_op jit(solution)/shard_map/ppermute | solution.py:77
  37.6 4.6 %collective-permute-start.4 = (bf16[1024,512]{1,0:T(8,128)(2,1)S(1)}, bf16[1024,512]{1,0:T(8,128)(2,1)S(1)}, u32[]{:S(2)}, u32[]{:S(2)}) collective-permute-start(bf16[1024,512]{1,0:T(8,128)(2,1)S(1)} %bitcast.22), channel_id=1, source_target_pairs={{0,16},{16,0},{1,17},{17,1},{2,18},{18,2},{3,19},{19,3},{4,20},{20... | collective-permute-start | bytes 3145736 | tf_op jit(solution)/shard_map/ppermute | solution.py:38
  100.7 35.0 %copy-start.1 = (bf16[512,512]{1,0:T(8,128)(2,1)S(1)}, bf16[512,512]{1,0:T(8,128)(2,1)}, u32[]{:S(2)}) copy-start(bf16[512,512]{1,0:T(8,128)(2,1)} %w_top_ref.1) | copy-start | bytes 1572868
  113.7 13.3 %all-to-all-start.4 = ((bf16[4,256,512]{2,1,0:T(8,128)(2,1)}), bf16[4,256,512]{2,1,0:T(8,128)(2,1)S(1)}, u32[]{:S(2)}, u32[]{:S(2)}) async-start(bf16[4,256,512]{2,1,0:T(8,128)(2,1)} %broadcast_in_dim.13), calls=%async_computation.4 | async-start | bytes 2097152 | tf_op jit(solution)/shard_map/all_to_all | solution.py:22
  117.3 8.2 %collective-permute-start.6 = (f32[2,512]{1,0:T(2,128)S(1)}, f32[2,512]{1,0:T(2,128)S(1)}, u32[]{:S(2)}, u32[]{:S(2)}) collective-permute-start(f32[2,512]{1,0:T(2,128)S(1)} %get-tuple-element.21), channel_id=1, source_target_pairs={{1,0},{2,1},{3,2},{4,3},{5,4},{6,5},{7,6},{8,7},{9,8},{10,9},{11,1... | collective-permute-start | bytes 12296 | tf_op jit(solution)/shard_map/ppermute | solution.py:319
  118.6 6.9 %collective-permute-start.5 = (f32[2,512]{1,0:T(2,128)S(1)}, f32[2,512]{1,0:T(2,128)S(1)}, u32[]{:S(2)}, u32[]{:S(2)}) collective-permute-start(f32[2,512]{1,0:T(2,128)S(1)} %get-tuple-element.22), channel_id=1, source_target_pairs={{0,1},{1,2},{2,3},{3,4},{4,5},{5,6},{6,7},{7,8},{8,9},{9,10},{10,1... | collective-permute-start | bytes 12296 | tf_op jit(solution)/shard_map/ppermute | solution.py:318
  127.0 11.0 %copy-start = (bf16[4,256,512]{2,1,0:T(8,128)(2,1)}, bf16[4,256,512]{2,1,0:T(8,128)(2,1)S(1)}, u32[]{:S(2)}) copy-start(bf16[4,256,512]{2,1,0:T(8,128)(2,1)S(1)} %all-to-all-done.4) | copy-start | bytes 3145732
  127.0 11.0 %collective-permute-start.7 = (bf16[1024,512]{1,0:T(8,128)(2,1)S(1)}, bf16[1024,512]{1,0:T(8,128)(2,1)S(1)}, u32[]{:S(2)}, u32[]{:S(2)}) collective-permute-start(bf16[1024,512]{1,0:T(8,128)(2,1)S(1)} %bitcast.23), channel_id=1, source_target_pairs={{0,16},{16,0},{1,17},{17,1},{2,18},{18,2},{3,19},{19,3},{4,20},{20... | collective-permute-start | bytes 3145736 | tf_op jit(solution)/shard_map/ppermute | solution.py:38
  137.9 1.0 copy-start.2

commit v5 on v3

--- a/solution.py
+++ b/solution.py
@@ -10,10 +10,10 @@
 
 LAT = ("x_hi", "z_hi", "z_lo", "core")
 LON = ("y_hi", "y_lo", "x_lo")
-NEAR = ("x_hi", "z_lo", "y_lo", "x_lo")
-FAR = ("z_hi", "y_hi")
+RING_X = ("x_hi", "x_lo")
+RING_Y = ("y_hi", "y_lo")
+RING_Z = ("z_hi", "z_lo")
 CORE = ("core",)
-LANES = 128
 CHUNK = 256
 BF16 = jnp.bfloat16
 F32 = jnp.float32
@@ -35,25 +35,20 @@
     return exchange(copies.reshape(-1, part.shape[-1]), axes)
 
 
-def all_sum(part, scale):
-    features = part.shape[-1]
-    tiles = features // LANES
-    part = reduce_stage(part, CORE).astype(BF16)
-    part = reduce_stage(part, NEAR).astype(BF16)
-    rows = part.shape[0]
-    part = part.reshape(rows, tiles, LANES).transpose(1, 0, 2).reshape(-1, LANES)
-    part = (reduce_stage(part, FAR) * scale).astype(BF16)
-    part = gather_stage(part, FAR)
-    part = part.reshape(tiles, rows, LANES).transpose(1, 0, 2).reshape(rows, features)
-    part = gather_stage(part, NEAR)
-    return gather_stage(part, CORE)
-
-
-def both_ways(block, axis):
+def ring_z_sum(part):
+    every = gather_stage(part, RING_Z).reshape((-1,) + part.shape)
+    return jnp.sum(every.astype(F32), axis=0)
+
+
+def inner_swap(block, axis):
     count = lax.axis_size(axis)
-    forward = [(i, i + 1) for i in range(count - 1)]
-    backward = [(target, source) for source, target in forward]
-    return lax.ppermute(block, axis, forward), lax.ppermute(block, axis, backward)
+    return lax.ppermute(block, axis, [(i, i ^ 1) for i in range(count)])
+
+
+def outer_swap(block, axis):
+    count = lax.axis_size(axis)
+    partner = {i: i + 1 if i % 2 else i - 1 for i in range(count)}
+    return lax.ppermute(block, axis, [(i, j) for i, j in partner.items() if 0 <= j < count])
 
 
 def silu_parts(values):
@@ -246,10 +241,16 @@
     lon_index = lax.axis_index(LON)
     band_start = lax.axis_index(LAT) * top_local
     own = nodes.reshape(block_size, features)
-    west, east = both_ways(own, LON)
-    mid = jnp.concatenate([west, own, east], axis=0)
-    low, high = both_ways(mid, LAT)
-    src_idx = (src_code * block_size + src_node).reshape(1, slots)
+    lat_odd, lon_odd = lax.axis_index("core"), lax.axis_index("x_lo")
+    outer = outer_swap(own, LON)
+    inner = inner_swap(own, LON)
+    mid = jnp.concatenate([outer, own, inner], axis=0)
+    low = outer_swap(mid, LAT)
+    high = inner_swap(mid, LAT)
+    src_row, src_col = src_code // 3, src_code % 3
+    src_row = jnp.where(lat_odd == 1, 2 - src_row, src_row)
+    src_col = jnp.where(lon_odd == 1, 2 - src_col, src_col)
+    src_idx = ((src_row * 3 + src_col) * block_size + src_node).reshape(1, slots)
     live_slot = lax.broadcasted_iota(jnp.int32, (1, slots), 1) < edge_count
     dst_idx = jnp.where(live_slot, dst_node.reshape(1, slots), block_size)
     band_ids = parent.reshape(1, block_size) - band_start
@@ -270,15 +271,22 @@
     )
     nodes_total = block_size * lax.axis_size(LAT) * lax.axis_size(LON)
     grad_scale = 8.0 / math.sqrt(nodes_total)
-    weight_grads = all_sum(grads.reshape(-1, features), grad_scale)
+    part = reduce_stage(grads.reshape(-1, features), CORE).astype(BF16)
+    part = reduce_stage(part, RING_X).astype(BF16)
+    part = reduce_stage(part, RING_Y).astype(BF16)
+    window, part = lax.optimization_barrier((window, part))
     padded = jnp.pad(window, ((owner_rows, owner_rows), (0, 0)))
     triple = lax.dynamic_slice_in_dim(padded, lon_index * owner_rows, 3 * owner_rows, 0)
-    count = lax.axis_size(LON)
-    forward = [(i, i + 1) for i in range(count - 1)]
-    backward = [(target, source) for source, target in forward]
-    from_left = lax.ppermute(triple[2 * owner_rows :], LON, forward)
-    from_right = lax.ppermute(triple[:owner_rows], LON, backward)
-    table_grad = (triple[owner_rows : 2 * owner_rows] + from_left + from_right).astype(BF16)
+    left, centre, right = jnp.split(triple, 3)
+    from_inner = inner_swap(jnp.where(lon_odd == 1, left, right), LON)
+    total = ring_z_sum(part)
+    total, from_inner, left, right = lax.optimization_barrier((total, from_inner, left, right))
+    from_outer = outer_swap(jnp.where(lon_odd == 1, right, left), LON)
+    part = gather_stage((total * grad_scale).astype(BF16), RING_Y)
+    part, from_outer = lax.optimization_barrier((part, from_outer))
+    part = gather_stage(part, RING_X)
+    weight_grads = gather_stage(part, CORE)
+    table_grad = (centre + from_inner + from_outer).astype(BF16)
     d_top = lax.dot_general(
         table_grad, w_top, (((1,), (1,)), ((), ())), preferred_element_type=F32
     ).astype(BF16)

time: 136 us -> 140 us (1.029)
  blocking collectives: 77.7 us -> 58.9 us
  waiting for transfers between devices: 15.7 us -> 28.1 us
  starting transfers between devices: 21.9 us -> 31.1 us
    all_to_all x1 -> x3, waiting for transfers between devices: 0.39 us -> 24.6 us  [exchange(): return lax.all_to_all(part, axes, 0, 0, tiled=True)]
    all_to_all x5 -> x4, blocking collectives: 77.7 us -> 58.9 us  [exchange(): return lax.all_to_all(part, axes, 0, 0, tiled=True)]
    ppermute x6, waiting for transfers between devices: 15.4 us -> 3.48 us  [the longest x3 2.11 us: outer_swap(): lax.ppermute(block, axis, [(i, j) for i, j in partner.items() if 0 <= j <...]
    all_to_all x1 -> x3, starting transfers between devices: 3.66 us -> 13.4 us  [exchange(): return lax.all_to_all(part, axes, 0, 0, tiled=True)]
    broadcast_in_dim x4, local copies, waits for them, and re-layouts: 1.23 us -> 2.64 us  [gather_stage(): copies = jnp.broadcast_to(part[None], (count,) + part.shape)]
  transfers between devices with their start and end apart: 7 -> 9, of which waited for: 5 -> 5; matrix products, arithmetic and copies ran while one was open for 2% -> 2% of each run, Pallas kernels for 0% -> 0%
where the time goes in v5:
time: 140 us; the launch traced here: 139 us
  blocking collectives  58.9 us (42%)
  starting transfers between devices  31.1 us (22%)
  waiting for transfers between devices  28.1 us (20%)
  Pallas kernels  10.6 us (8%)
  other arithmetic  4.47 us (3%)
  local copies, waits for them, and re-layouts  3.96 us (3%)
  between operations  1.45 us (1%)
    all_to_all x4, blocking collectives, exchange(): return lax.all_to_all(part, axes, 0, 0, tiled=True)  58.9 us
    all_to_all x3, waiting for transfers between devices, exchange(): return lax.all_to_all(part, axes, 0, 0, tiled=True)  24.6 us
    all_to_all x3, starting transfers between devices, exchange(): return lax.all_to_all(part, axes, 0, 0, tiled=True)  13.4 us
    ppermute x3, starting transfers between devices, inner_swap(): return lax.ppermute(block, axis, [(i, i ^ 1) for i in range(count)])  10.6 us
    pallas_call x1, Pallas kernels, block_round(): pl.pallas_call(block_kernel, out_shape=(jax.ShapeDtypeStruct((block, feat...  10.6 us
    ppermute x3, starting transfers between devices, outer_swap(): lax.ppermute(block, axis, [(i, j) for i, j in partner.items() if 0 <= j <...  7.14 us
  transfers between devices with their start and end apart: 9, of which 5 were waited for; matrix products, arithmetic and copies ran while one was open for 2% of the time, Pallas kernels for 0%

profile of v5, /device:TPU:1, one launch (start us, length us, event | category | flops | bytes accessed | tf_op | source)
XLA Modules:
  0.0 139.4 jit_solution(15799663798239795276)
XLA Ops:
  0.6 0.7 collective-permute-start
  1.3 6.5 %collective-permute-start.1 = (bf16[128,512]{1,0:T(8,128)(2,1)}, bf16[128,512]{1,0:T(8,128)(2,1)S(1)}, u32[]{:S(2)}, u32[]{:S(2)}) collective-permute-start(bf16[128,512]{1,0:T(8,128)(2,1)} %bitcast.25), channel_id=1, source_target_pairs={{0,1},{1,0},{2,3},{3,2},{4,5},{5,4},{6,7},{7,6},{8,9},{9,8},{10,11... | collective-permute-start | bytes 393224 | tf_op jit(solution)/shard_map/ppermute | solution.py:45
  8.4 0.7 compare_select_fusion.dst_ref
  9.1 0.0 collective-permute-done
  9.1 1.4 collective-permute-done.1
  10.5 0.9 pad_maximum_fusion.mid_ref
  11.4 5.8 %collective-permute-start.2 = (bf16[384,512]{1,0:T(8,128)(2,1)S(1)}, bf16[384,512]{1,0:T(8,128)(2,1)S(1)}, u32[]{:S(2)}, u32[]{:S(2)}) collective-permute-start(bf16[384,512]{1,0:T(8,128)(2,1)S(1)} %pad_maximum_fusion.mid_ref), channel_id=1, source_target_pairs={{16,32},{32,16},{48,64},{64,48},{80,96},{96,80},{112,128},{128,112... | collective-permute-start | bytes 1179656 | tf_op jit(solution)/shard_map/ppermute | solution.py:51
  17.2 1.9 %collective-permute-start.3 = (bf16[384,512]{1,0:T(8,128)(2,1)S(1)}, bf16[384,512]{1,0:T(8,128)(2,1)S(1)}, u32[]{:S(2)}, u32[]{:S(2)}) collective-permute-start(bf16[384,512]{1,0:T(8,128)(2,1)S(1)} %pad_maximum_fusion.mid_ref), channel_id=1, source_target_pairs={{0,16},{16,0},{32,48},{48,32},{64,80},{80,64},{96,112},{112,96},{1... | collective-permute-start | bytes 1179656 | tf_op jit(solution)/shard_map/ppermute | solution.py:45
  19.2 0.7 subtract_bitcast_fusion.band_ref
  19.8 0.8 add_bitcast_fusion.src_ref
  20.6 2.1 %collective-permute-done.2.low_ref = bf16[384,512]{1,0:T(8,128)(2,1)S(1)} collective-permute-done((bf16[384,512]{1,0:T(8,128)(2,1)S(1)}, bf16[384,512]{1,0:T(8,128)(2,1)S(1)}, u32[]{:S(2)}, u32[]{:S(2)}) %collective-permute-start.2) | collective-permute-done | bytes 393248 | tf_op jit(solution)/shard_map/ppermute | solution.py:51
  22.7 0.0 collective-permute-done.3.high_ref
  22.7 10.6 %block_round.1 = (bf16[128,512]{1,0:T(8,128)(2,1)}, bf16[4,512,512]{2,1,0:T(8,128)(2,1)S(1)}, f32[32,512]{1,0:T(8,128)S(1)}) custom-call(bf16[384,512]{1,0:T(8,128)(2,1)S(1)} %collective-permute-done.2.low_ref, bf16[384,512]{1,0:T(8,128)(2,1)S(1)} %pad_maximum_fusion.mid_ref, bf16[384,512]{1,0:T(8,128)(2,1)S(1)} %collective-permute-done.3.high_ref, ...), custom_call_target="tpu_custom_call" | custom-call | tf_op jit(solution)/shard_map/block_round/pallas_call | solution.py:190
  33.3 5.1 %all_to_all.54 = bf16[2,1024,512]{2,1,0:T(8,128)(2,1)S(1)} all-to-all(bf16[2,1024,512]{2,1,0:T(8,128)(2,1)S(1)} %bitcast.18), channel_id=1, replica_groups=mesh['x_hi'=2,'z_hi'=4,'z_lo'=2,'core'=2,'y_hi'=4,'y_lo'=2,'x_lo'=2] {'c..., dimensions={0} | all-to-all | bytes 4194304 | tf_op jit(solution)/shard_map/all_to_all | solution.py:23
  38.3 1.1 reduce_sum.45
  39.4 25.2 %all_to_all.55 = bf16[4,256,512]{2,1,0:T(8,128)(2,1)S(1)} all-to-all(bf16[4,256,512]{2,1,0:T(8,128)(2,1)S(1)} %bitcast.21), channel_id=1, replica_groups=mesh['x_hi'=2,'z_hi'=4,'z_lo'=2,'core'=2,'y_hi'=4,'y_lo'=2,'x_lo'=2] {'x..., dimensions={0} | all-to-all | bytes 2097152 | tf_op jit(solution)/shard_map/all_to_all | solution.py:23
  64.6 0.2 reduce_sum.46
  64.9 17.3 %all_to_all.56 = bf16[8,32,512]{2,1,0:T(8,128)(2,1)S(1)} all-to-all(bf16[8,32,512]{2,1,0:T(8,128)(2,1)S(1)} %bitcast.23), channel_id=1, replica_groups=mesh['x_hi'=2,'z_hi'=4,'z_lo'=2,'core'=2,'y_hi'=4,'y_lo'=2,'x_lo'=2] {'y..., dimensions={0} | all-to-all | bytes 524288 | tf_op jit(solution)/shard_map/all_to_all | solution.py:23
  82.2 0.7 broadcast_in_dim.15
  82.9 6.5 %all-to-all-start.3 = ((bf16[8,32,512]{2,1,0:T(8,128)(2,1)}), bf16[8,32,512]{2,1,0:T(8,128)(2,1)S(1)}, u32[]{:S(2)}, u32[]{:S(2)}) async-start(bf16[8,32,512]{2,1,0:T(8,128)(2,1)} %broadcast_in_dim.15), calls=%async_computation.3 | async-start | bytes 524288 | tf_op jit(solution)/shard_map/all_to_all | solution.py:23
  89.4 2.2 %collective-permute-start.4 = (f32[2,512]{1,0:T(2,128)S(1)}, f32[2,512]{1,0:T(2,128)S(1)}, u32[]{:S(2)}, u32[]{:S(2)}) collective-permute-start(f32[2,512]{1,0:T(2,128)S(1)} %get-tuple-element.25), channel_id=1, source_target_pairs={{0,1},{1,0},{2,3},{3,2},{4,5},{5,4},{6,7},{7,6},{8,9},{9,8},{10,11... | collective-permute-start | bytes 12296 | tf_op jit(solution)/shard_map/ppermute | solution.py:45
  91.6 7.2 %all-to-all-done.3 = bf16[8,32,512]{2,1,0:T(8,128)(2,1)S(1)} async-done(((bf16[8,32,512]{2,1,0:T(8,128)(2,1)}), bf16[8,32,512]{2,1,0:T(8,128)(2,1)S(1)}, u32[]{:S(2)}, u32[]{:S(2)}) %all-to-all-start.3) | async-done | bytes 262176 | tf_op jit(solution)/shard_map/all_to_all | solution.py:23
  98.8 0.0 collective-permute-done.4
  98.8 0.0 copy-start
  98.8 0.7 broadcast_in_dim.16
  99.6 3.4 %all-to-all-start.4 = ((bf16[8,32,512]{2,1,0:T(8,128)(2,1)}), bf16[8,32,512]{2,1,0:T(8,128)(2,1)S(1)}, u32[]{:S(2)}, u32[]{:S(2)}) async-start(bf16[8,32,512]{2,1,0:T(8,128)(2,1)} %broadcast_in_dim.16), calls=%async_computation.4 | async-start | bytes 524288 | tf_op jit(solution)/shard_map/all_to_all | solution.py:23
  103.0 0.7 collective-permute-start.5
  103.7 0.0 collective-permute-done.5
  103.7 8.6 %all-to-all-done.4 = bf16[8,32,512]{2,1,0:T(8,128)(2,1)S(1)} async-done(((bf16[8,32,512]{2,1,0:T(8,128)(2,1)}), bf16[8,32,512]{2,1,0:T(8,128)(2,1)S(1)}, u32[]{:S(2)}, u32[]{:S(2)}) %all-to-all-start.4) | async-done | bytes 262176 | tf_op jit(solution)/shard_map/all_to_all | solution.py:23
  112.2 1.1 broadcast_in_dim.17
  113.3 3.5 %all-to-all-start.5 = ((bf16[4,256,512]{2,1,0:T(8,128)(2,1)}), bf16[4,256,512]{2,1,0:T(8,128)(2,1)S(1)}, u32[]{:S(2)}, u32[]{:S(2)}) async-start(bf16[4,256,512]{2,1,0:T(8,128)(2,1)} %broadcast_in_dim.17), calls=%async_computation.5 | async-start | bytes 2097152 | tf_op jit(solution)/shard_map/all_to_all | solution.py:23
  116.8 0.0 copy-done
  116.8 0.8 convolution_convert_fusion
  117.7 8.9 %all-to-all-done.5 = bf16[4,256,512]{2,1,0:T(8,128)(2,1)S(1)} async-done(((bf16[4,256,512]{2,1,0:T(8,128)(2,1)}), bf16[4,256,512]{2,1,0:T(8,128)(2,1)S(1)}, u32[]{:S(2)}, u32[]{:S(2)}) %all-to-all-start.5) | async-done | bytes 1048608 | tf_op jit(solution)/shard_map/all_to_all | solution.py:23
  126.6 0.1 broadcast_in_dim.35
  126.7 11.3 %all_to_all.57 = bf16[2,1024,512]{2,1,0:T(8,128)(2,1)S(1)} all-to-all(bf16[2,1024,512]{2,1,0:T(8,128)(2,1)S(1)} %broadcast_in_dim.35), channel_id=1, replica_groups=mesh['x_hi'=2,'z_hi'=4,'z_lo'=2,'core'=2,'y_hi'=4,'y_lo'=2,'x_lo'=2] {'c..., dimensions={0} | all-to-all | bytes 4194304 | tf_op jit(solution)/shard_map/all_to_all | solution.py:23
  138.0 1.3 copy.17
  (5 shorter events, 0.1 us)
Async XLA Ops:
  0.6 8.5 %collective-permute-start = (bf16[128,512]{1,0:T(8,128)(2,1)}, bf16[128,512]{1,0:T(8,128)(2,1)S(1)}, u32[]{:S(2)}, u32[]{:S(2)}) collective-permute-start(bf16[128,512]{1,0:T(8,128)(2,1)} %bitcast.24), channel_id=1, source_target_pairs={{1,2},{2,1},{3,4},{4,3},{5,6},{6,5},{7,8},{8,7},{9,10},{10,9},{11,... | collective-permute-start | bytes 393224 | tf_op jit(solution)/shard_map/ppermute | solution.py:51
  1.3 9.2 %collective-permute-start.1 = (bf16[128,512]{1,0:T(8,128)(2,1)}, bf16[128,512]{1,0:T(8,128)(2,1)S(1)}, u32[]{:S(2)}, u32[]{:S(2)}) collective-permute-start(bf16[128,512]{1,0:T(8,128)(2,1)} %bitcast.25), channel_id=1, source_target_pairs={{0,1},{1,0},{2,3},{3,2},{4,5},{5,4},{6,7},{7,6},{8,9},{9,8},{10,11... | collective-permute-start | bytes 393224 | tf_op jit(solution)/shard_map/ppermute | solution.py:45
  11.4 11.3 %collective-permute-start.2 = (bf16[384,512]{1,0:T(8,128)(2,1)S(1)}, bf16[384,512]{1,0:T(8,128)(2,1)S(1)}, u32[]{:S(2)}, u32[]{:S(2)}) collective-permute-start(bf16[384,512]{1,0:T(8,128)(2,1)S(1)} %pad_maximum_fusion.mid_ref), channel_id=1, source_target_pairs={{16,32},{32,16},{48,64},{64,48},{80,96},{96,80},{112,128},{128,112... | collective-permute-start | bytes 1179656 | tf_op jit(solution)/shard_map/ppermute | solution.py:51
  17.2 5.4 %collective-permute-start.3 = (bf16[384,512]{1,0:T(8,128)(2,1)S(1)}, bf16[384,512]{1,0:T(8,128)(2,1)S(1)}, u32[]{:S(2)}, u32[]{:S(2)}) collective-permute-start(bf16[384,512]{1,0:T(8,128)(2,1)S(1)} %pad_maximum_fusion.mid_ref), channel_id=1, source_target_pairs={{0,16},{16,0},{32,48},{48,32},{64,80},{80,64},{96,112},{112,96},{1... | collective-permute-start | bytes 1179656 | tf_op jit(solution)/shard_map/ppermute | solution.py:45
  82.9 15.8 %all-to-all-start.3 = ((bf16[8,32,512]{2,1,0:T(8,128)(2,1)}), bf16[8,32,512]{2,1,0:T(8,128)(2,1)S(1)}, u32[]{:S(2)}, u32[]{:S(2)}) async-start(bf16[8,32,512]{2,1,0:T(8,128)(2,1)} %broadcast_in_dim.15), calls=%async_computation.3 | async-start | bytes 524288 | tf_op jit(solution)/shard_map/all_to_all | solution.py:23
  89.4 9.4 %collective-permute-start.4 = (f32[2,512]{1,0:T(2,128)S(1)}, f32[2,512]{1,0:T(2,128)S(1)}, u32[]{:S(2)}, u32[]{:S(2)}) collective-permute-start(f32[2,512]{1,0:T(2,128)S(1)} %get-tuple-element.25), channel_id=1, source_target_pairs={{0,1},{1,0},{2,3},{3,2},{4,5},{5,4},{6,7},{7,6},{8,9},{9,8},{10,11... | collective-permute-start | bytes 12296 | tf_op jit(solution)/shard_map/ppermute | solution.py:45
  98.8 18.0 %copy-start = (bf16[512,512]{1,0:T(8,128)(2,1)S(1)}, bf16[512,512]{1,0:T(8,128)(2,1)}, u32[]{:S(2)}) copy-start(bf16[512,512]{1,0:T(8,128)(2,1)} %w_top_ref.1) | copy-start | bytes 1572868
  99.6 12.7 %all-to-all-start.4 = ((bf16[8,32,512]{2,1,0:T(8,128)(2,1)}), bf16[8,32,512]{2,1,0:T(8,128)(2,1)S(1)}, u32[]{:S(2)}, u32[]{:S(2)}) async-start(bf16[8,32,512]{2,1,0:T(8,128)(2,1)} %broadcast_in_dim.16), calls=%async_computation.4 | async-start | bytes 524288 | tf_op jit(solution)/shard_map/all_to_all | solution.py:23
  103.0 0.7 collective-permute-start.5
  113.3 13.3 %all-to-all-start.5 = ((bf16[4,256,512]{2,1,0:T(8,128)(2,1)}), bf16[4,256,512]{2,1,0:T(8,128)(2,1)S(1)}, u32[]{:S(2)}, u32[]{:S(2)}) async-start(bf16[4,256,512]{2,1,0:T(8,128)(2,1)} %broadcast_in_dim.17), calls=%async_computation.5 | async-start | bytes 2097152 | tf_op jit(solution)/shard_map/all_to_all | solution.py:23

commit v6 on v5

--- a/solution.py
+++ b/solution.py
@@ -10,10 +10,10 @@
 
 LAT = ("x_hi", "z_hi", "z_lo", "core")
 LON = ("y_hi", "y_lo", "x_lo")
-RING_X = ("x_hi", "x_lo")
-RING_Y = ("y_hi", "y_lo")
-RING_Z = ("z_hi", "z_lo")
+NEAR = ("x_hi", "z_lo", "y_lo", "x_lo")
+FAR = ("z_hi", "y_hi")
 CORE = ("core",)
+LANES = 128
 CHUNK = 256
 BF16 = jnp.bfloat16
 F32 = jnp.float32
@@ -35,9 +35,12 @@
     return exchange(copies.reshape(-1, part.shape[-1]), axes)
 
 
-def ring_z_sum(part):
-    every = gather_stage(part, RING_Z).reshape((-1,) + part.shape)
-    return jnp.sum(every.astype(F32), axis=0)
+def far_sum(part, scale):
+    rows, features = part.shape
+    tiles = features // LANES
+    part = part.reshape(rows, tiles, LANES).transpose(1, 0, 2).reshape(-1, LANES)
+    part = gather_stage((reduce_stage(part, FAR) * scale).astype(BF16), FAR)
+    return part.reshape(tiles, rows, LANES).transpose(1, 0, 2).reshape(rows, features)
 
 
 def inner_swap(block, axis):
@@ -272,24 +275,21 @@
     nodes_total = block_size * lax.axis_size(LAT) * lax.axis_size(LON)
     grad_scale = 8.0 / math.sqrt(nodes_total)
     part = reduce_stage(grads.reshape(-1, features), CORE).astype(BF16)
-    part = reduce_stage(part, RING_X).astype(BF16)
-    part = reduce_stage(part, RING_Y).astype(BF16)
     window, part = lax.optimization_barrier((window, part))
     padded = jnp.pad(window, ((owner_rows, owner_rows), (0, 0)))
     triple = lax.dynamic_slice_in_dim(padded, lon_index * owner_rows, 3 * owner_rows, 0)
     left, centre, right = jnp.split(triple, 3)
     from_inner = inner_swap(jnp.where(lon_odd == 1, left, right), LON)
-    total = ring_z_sum(part)
-    total, from_inner, left, right = lax.optimization_barrier((total, from_inner, left, right))
+    part = reduce_stage(part, NEAR).astype(BF16)
+    part, from_inner = lax.optimization_barrier((part, from_inner))
+    part = far_sum(part, grad_scale)
+    part, left, right = lax.optimization_barrier((part, left, right))
     from_outer = outer_swap(jnp.where(lon_odd == 1, right, left), LON)
-    part = gather_stage((total * grad_scale).astype(BF16), RING_Y)
-    part, from_outer = lax.optimization_barrier((part, from_outer))
-    part = gather_stage(part, RING_X)
+    part = gather_stage(part, NEAR)
+    table_grad = (centre + from_inner + from_outer).astype(BF16)
+    d_top = mm_cols(table_grad, w_top).astype(BF16)
+    part, d_top = lax.optimization_barrier((part, d_top))
     weight_grads = gather_stage(part, CORE)
-    table_grad = (centre + from_inner + from_outer).astype(BF16)
-    d_top = lax.dot_general(
-        table_grad, w_top, (((1,), (1,)), ((), ())), preferred_element_type=F32
-    ).astype(BF16)
     return (
         updated.reshape(nodes.shape),
         weight_grads.reshape(4, features, features),

time: 140 us -> 134 us (0.957)
  blocking collectives: 58.9 us -> 52 us
  starting transfers between devices: 31.1 us -> 36.3 us
  waiting for transfers between devices: 28.1 us -> 25 us
    all_to_all x4, blocking collectives: 58.9 us -> 52 us  [exchange(): return lax.all_to_all(part, axes, 0, 0, tiled=True)]
    all_to_all x3 -> x2, starting transfers between devices: 13.4 us -> 17.8 us  [exchange(): return lax.all_to_all(part, axes, 0, 0, tiled=True)]
    ppermute x3, waiting for transfers between devices: 2.11 us -> 0.22 us  [outer_swap(): lax.ppermute(block, axis, [(i, j) for i, j in partner.items() if 0 <= j <...]
    broadcast_in_dim x4 -> x3, local copies, waits for them, and re-layouts: 2.64 us -> 1.22 us  [gather_stage(): copies = jnp.broadcast_to(part[None], (count,) + part.shape)]
    all_to_all x3 -> x2, waiting for transfers between devices: 24.6 us -> 24.3 us  [exchange(): return lax.all_to_all(part, axes, 0, 0, tiled=True)]
  transfers between devices with their start and end apart: 9 -> 8, of which waited for: 5 -> 4; matrix products, arithmetic and copies ran while one was open for 2% -> 2% of each run, Pallas kernels for 0% -> 0%
where the time goes in v6:
time: 134 us
  blocking collectives  52 us (39%)
  starting transfers between devices  36.3 us (27%)
  waiting for transfers between devices  25 us (19%)
  Pallas kernels  10.6 us (8%)
  other arithmetic  4.88 us (4%)
  local copies, waits for them, and re-layouts  2.59 us (2%)
  between operations  1.48 us (1%)
    all_to_all x4, blocking collectives, exchange(): return lax.all_to_all(part, axes, 0, 0, tiled=True)  52 us
    all_to_all x2, waiting for transfers between devices, exchange(): return lax.all_to_all(part, axes, 0, 0, tiled=True)  24.3 us
    all_to_all x2, starting transfers between devices, exchange(): return lax.all_to_all(part, axes, 0, 0, tiled=True)  17.8 us
    ppermute x3, starting transfers between devices, inner_swap(): return lax.ppermute(block, axis, [(i, i ^ 1) for i in range(count)])  11 us
    pallas_call x1, Pallas kernels, block_round(): pl.pallas_call(block_kernel, out_shape=(jax.ShapeDtypeStruct((block, feat...  10.6 us
    ppermute x3, starting transfers between devices, outer_swap(): lax.ppermute(block, axis, [(i, j) for i, j in partner.items() if 0 <= j <...  7.55 us
  transfers between devices with their start and end apart: 8, of which 4 were waited for; matrix products, arithmetic and copies ran while one was open for 2% of the time, Pallas kernels for 0%

profile of v6, /device:TPU:1, one launch (start us, length us, event | category | flops | bytes accessed | tf_op | source)
XLA Modules:
  0.0 133.7 jit_solution(15904404698076826206)
XLA Ops:
  0.6 4.0 %collective-permute-start.1 = (bf16[128,512]{1,0:T(8,128)(2,1)}, bf16[128,512]{1,0:T(8,128)(2,1)S(1)}, u32[]{:S(2)}, u32[]{:S(2)}) collective-permute-start(bf16[128,512]{1,0:T(8,128)(2,1)} %bitcast.28), channel_id=1, source_target_pairs={{0,1},{1,0},{2,3},{3,2},{4,5},{5,4},{6,7},{7,6},{8,9},{9,8},{10,11... | collective-permute-start | bytes 393224 | tf_op jit(solution)/shard_map/ppermute | solution.py:48
  4.6 0.7 collective-permute-start
  5.9 0.7 compare_select_fusion.dst_ref
  6.6 0.5 collective-permute-done.1
  7.1 0.0 collective-permute-done
  7.1 0.9 pad_maximum_fusion.mid_ref
  8.1 6.2 %collective-permute-start.2 = (bf16[384,512]{1,0:T(8,128)(2,1)S(1)}, bf16[384,512]{1,0:T(8,128)(2,1)S(1)}, u32[]{:S(2)}, u32[]{:S(2)}) collective-permute-start(bf16[384,512]{1,0:T(8,128)(2,1)S(1)} %pad_maximum_fusion.mid_ref), channel_id=1, source_target_pairs={{16,32},{32,16},{48,64},{64,48},{80,96},{96,80},{112,128},{128,112... | collective-permute-start | bytes 1179656 | tf_op jit(solution)/shard_map/ppermute | solution.py:54
  14.3 3.8 %collective-permute-start.3 = (bf16[384,512]{1,0:T(8,128)(2,1)S(1)}, bf16[384,512]{1,0:T(8,128)(2,1)S(1)}, u32[]{:S(2)}, u32[]{:S(2)}) collective-permute-start(bf16[384,512]{1,0:T(8,128)(2,1)S(1)} %pad_maximum_fusion.mid_ref), channel_id=1, source_target_pairs={{0,16},{16,0},{32,48},{48,32},{64,80},{80,64},{96,112},{112,96},{1... | collective-permute-start | bytes 1179656 | tf_op jit(solution)/shard_map/ppermute | solution.py:48
  18.1 0.7 subtract_bitcast_fusion.band_ref
  18.8 0.8 add_bitcast_fusion.src_ref
  19.5 0.2 collective-permute-done.2.low_ref
  19.8 0.0 collective-permute-done.3.high_ref
  19.8 10.6 %block_round.1 = (bf16[128,512]{1,0:T(8,128)(2,1)}, bf16[4,512,512]{2,1,0:T(8,128)(2,1)S(1)}, f32[32,512]{1,0:T(8,128)S(1)}) custom-call(bf16[384,512]{1,0:T(8,128)(2,1)S(1)} %collective-permute-done.2.low_ref, bf16[384,512]{1,0:T(8,128)(2,1)S(1)} %pad_maximum_fusion.mid_ref, bf16[384,512]{1,0:T(8,128)(2,1)S(1)} %collective-permute-done.3.high_ref, ...), custom_call_target="tpu_custom_call" | custom-call | tf_op jit(solution)/shard_map/block_round/pallas_call | solution.py:193
  30.3 5.1 %all_to_all.48 = bf16[2,1024,512]{2,1,0:T(8,128)(2,1)S(1)} all-to-all(bf16[2,1024,512]{2,1,0:T(8,128)(2,1)S(1)} %bitcast.25), channel_id=1, replica_groups=mesh['x_hi'=2,'z_hi'=4,'z_lo'=2,'core'=2,'y_hi'=4,'y_lo'=2,'x_lo'=2] {'c..., dimensions={0} | all-to-all | bytes 4194304 | tf_op jit(solution)/shard_map/all_to_all | solution.py:23
  35.4 1.6 %reduce_sum.33 = bf16[1024,512]{1,0:T(8,128)(2,1)} reduce(bf16[2,1024,512]{2,1,0:T(8,128)(2,1)S(1)} %all_to_all.48, bf16[]{:T(256)} %constant.67.clone.1), dimensions={0}, to_apply=%region_0.1 | reduce | flops 524288 | bytes 3145730 | tf_op jit(solution)/shard_map/reduce_sum | solution.py:29
  37.1 14.1 %all-to-all-start.1 = ((bf16[16,64,512]{2,1,0:T(8,128)(2,1)}), bf16[16,64,512]{2,1,0:T(8,128)(2,1)S(1)}, u32[]{:S(2)}, u32[]{:S(2)}) async-start(bf16[16,64,512]{2,1,0:T(8,128)(2,1)} %bitcast.8), calls=%async_computation.1 | async-start | bytes 2097152 | tf_op jit(solution)/shard_map/all_to_all | solution.py:23
  51.2 3.3 %collective-permute-start.4 = (f32[2,512]{1,0:T(2,128)S(1)}, f32[2,512]{1,0:T(2,128)S(1)}, u32[]{:S(2)}, u32[]{:S(2)}) collective-permute-start(f32[2,512]{1,0:T(2,128)S(1)} %get-tuple-element.27), channel_id=1, source_target_pairs={{0,1},{1,0},{2,3},{3,2},{4,5},{5,4},{6,7},{7,6},{8,9},{9,8},{10,11... | collective-permute-start | bytes 12296 | tf_op jit(solution)/shard_map/ppermute | solution.py:48
  54.5 13.1 %all-to-all-done.1 = bf16[16,64,512]{2,1,0:T(8,128)(2,1)S(1)} async-done(((bf16[16,64,512]{2,1,0:T(8,128)(2,1)}), bf16[16,64,512]{2,1,0:T(8,128)(2,1)S(1)}, u32[]{:S(2)}, u32[]{:S(2)}) %all-to-all-start.1) | async-done | bytes 1048608 | tf_op jit(solution)/shard_map/all_to_all | solution.py:23
  67.6 0.1 reduce_sum.34
  67.7 0.0 copy-start
  67.7 0.0 collective-permute-done.4
  67.8 22.5 %all_to_all.49 = bf16[16,16,128]{2,1,0:T(8,128)(2,1)S(1)} all-to-all(bf16[16,16,128]{2,1,0:T(8,128)(2,1)S(1)} %bitcast.34), channel_id=1, replica_groups=mesh['x_hi'=2,'z_hi'=4,'z_lo'=2,'core'=2,'y_hi'=4,'y_lo'=2,'x_lo'=2] {'z..., dimensions={0} | all-to-all | bytes 131072 | tf_op jit(solution)/shard_map/all_to_all | solution.py:23
  90.3 13.9 %all_to_all.50 = bf16[16,16,128]{2,1,0:T(8,128)(2,1)S(1)} all-to-all(bf16[16,16,128]{2,1,0:T(8,128)(2,1)S(1)} %broadcast_in_dim.11), channel_id=1, replica_groups=mesh['x_hi'=2,'z_hi'=4,'z_lo'=2,'core'=2,'y_hi'=4,'y_lo'=2,'x_lo'=2] {'z..., dimensions={0} | all-to-all | bytes 131072 | tf_op jit(solution)/shard_map/all_to_all | solution.py:23
  104.2 1.1 broadcast_in_dim.12
  105.3 3.7 %all-to-all-start.4 = ((bf16[16,64,512]{2,1,0:T(8,128)(2,1)}), bf16[16,64,512]{2,1,0:T(8,128)(2,1)S(1)}, u32[]{:S(2)}, u32[]{:S(2)}) async-start(bf16[16,64,512]{2,1,0:T(8,128)(2,1)} %broadcast_in_dim.12), calls=%async_computation.4 | async-start | bytes 2097152 | tf_op jit(solution)/shard_map/all_to_all | solution.py:23
  108.9 0.7 collective-permute-start.5
  109.6 0.0 collective-permute-done.5
  109.6 0.0 copy-done
  109.6 0.8 convolution_convert_fusion
  110.5 11.2 %all-to-all-done.4 = bf16[16,64,512]{2,1,0:T(8,128)(2,1)S(1)} async-done(((bf16[16,64,512]{2,1,0:T(8,128)(2,1)}), bf16[16,64,512]{2,1,0:T(8,128)(2,1)S(1)}, u32[]{:S(2)}, u32[]{:S(2)}) %all-to-all-start.4) | async-done | bytes 1048608 | tf_op jit(solution)/shard_map/all_to_all | solution.py:23
  121.7 0.1 broadcast_in_dim.13
  121.8 10.5 %all_to_all.51 = bf16[2,1024,512]{2,1,0:T(8,128)(2,1)S(1)} all-to-all(bf16[2,1024,512]{2,1,0:T(8,128)(2,1)S(1)} %broadcast_in_dim.13), channel_id=1, replica_groups=mesh['x_hi'=2,'z_hi'=4,'z_lo'=2,'core'=2,'y_hi'=4,'y_lo'=2,'x_lo'=2] {'c..., dimensions={0} | all-to-all | bytes 4194304 | tf_op jit(solution)/shard_map/all_to_all | solution.py:23
  132.3 1.3 copy.24
  (8 shorter events, 0.1 us)
Async XLA Ops:
  0.6 6.5 %collective-permute-start.1 = (bf16[128,512]{1,0:T(8,128)(2,1)}, bf16[128,512]{1,0:T(8,128)(2,1)S(1)}, u32[]{:S(2)}, u32[]{:S(2)}) collective-permute-start(bf16[128,512]{1,0:T(8,128)(2,1)} %bitcast.28), channel_id=1, source_target_pairs={{0,1},{1,0},{2,3},{3,2},{4,5},{5,4},{6,7},{7,6},{8,9},{9,8},{10,11... | collective-permute-start | bytes 393224 | tf_op jit(solution)/shard_map/ppermute | solution.py:48
  4.6 2.6 %collective-permute-start = (bf16[128,512]{1,0:T(8,128)(2,1)}, bf16[128,512]{1,0:T(8,128)(2,1)S(1)}, u32[]{:S(2)}, u32[]{:S(2)}) collective-permute-start(bf16[128,512]{1,0:T(8,128)(2,1)} %bitcast.29), channel_id=1, source_target_pairs={{1,2},{2,1},{3,4},{4,3},{5,6},{6,5},{7,8},{8,7},{9,10},{10,9},{11,... | collective-permute-start | bytes 393224 | tf_op jit(solution)/shard_map/ppermute | solution.py:54
  8.1 11.7 %collective-permute-start.2 = (bf16[384,512]{1,0:T(8,128)(2,1)S(1)}, bf16[384,512]{1,0:T(8,128)(2,1)S(1)}, u32[]{:S(2)}, u32[]{:S(2)}) collective-permute-start(bf16[384,512]{1,0:T(8,128)(2,1)S(1)} %pad_maximum_fusion.mid_ref), channel_id=1, source_target_pairs={{16,32},{32,16},{48,64},{64,48},{80,96},{96,80},{112,128},{128,112... | collective-permute-start | bytes 1179656 | tf_op jit(solution)/shard_map/ppermute | solution.py:54
  14.3 5.4 %collective-permute-start.3 = (bf16[384,512]{1,0:T(8,128)(2,1)S(1)}, bf16[384,512]{1,0:T(8,128)(2,1)S(1)}, u32[]{:S(2)}, u32[]{:S(2)}) collective-permute-start(bf16[384,512]{1,0:T(8,128)(2,1)S(1)} %pad_maximum_fusion.mid_ref), channel_id=1, source_target_pairs={{0,16},{16,0},{32,48},{48,32},{64,80},{80,64},{96,112},{112,96},{1... | collective-permute-start | bytes 1179656 | tf_op jit(solution)/shard_map/ppermute | solution.py:48
  37.1 30.5 %all-to-all-start.1 = ((bf16[16,64,512]{2,1,0:T(8,128)(2,1)}), bf16[16,64,512]{2,1,0:T(8,128)(2,1)S(1)}, u32[]{:S(2)}, u32[]{:S(2)}) async-start(bf16[16,64,512]{2,1,0:T(8,128)(2,1)} %bitcast.8), calls=%async_computation.1 | async-start | bytes 2097152 | tf_op jit(solution)/shard_map/all_to_all | solution.py:23
  51.2 16.5 %collective-permute-start.4 = (f32[2,512]{1,0:T(2,128)S(1)}, f32[2,512]{1,0:T(2,128)S(1)}, u32[]{:S(2)}, u32[]{:S(2)}) collective-permute-start(f32[2,512]{1,0:T(2,128)S(1)} %get-tuple-element.27), channel_id=1, source_target_pairs={{0,1},{1,0},{2,3},{3,2},{4,5},{5,4},{6,7},{7,6},{8,9},{9,8},{10,11... | collective-permute-start | bytes 12296 | tf_op jit(solution)/shard_map/ppermute | solution.py:48
  67.7 41.9 %copy-start = (bf16[512,512]{1,0:T(8,128)(2,1)S(1)}, bf16[512,512]{1,0:T(8,128)(2,1)}, u32[]{:S(2)}) copy-start(bf16[512,512]{1,0:T(8,128)(2,1)} %w_top_ref.1) | copy-start | bytes 1572868
  105.3 16.4 %all-to-all-start.4 = ((bf16[16,64,512]{2,1,0:T(8,128)(2,1)}), bf16[16,64,512]{2,1,0:T(8,128)(2,1)S(1)}, u32[]{:S(2)}, u32[]{:S(2)}) async-start(bf16[16,64,512]{2,1,0:T(8,128)(2,1)} %broadcast_in_dim.12), calls=%async_computation.4 | async-start | bytes 2097152 | tf_op jit(solution)/shard_map/all_to_all | solution.py:23
  108.9 0.7 collective-permute-start.5

commit v7 on v6

--- a/solution.py
+++ b/solution.py
@@ -1,3 +1,4 @@
+import itertools
 import math
 
 import jax
@@ -10,37 +11,52 @@
 
 LAT = ("x_hi", "z_hi", "z_lo", "core")
 LON = ("y_hi", "y_lo", "x_lo")
-NEAR = ("x_hi", "z_lo", "y_lo", "x_lo")
-FAR = ("z_hi", "y_hi")
-CORE = ("core",)
+AXES = LAT + LON
 LANES = 128
-CHUNK = 256
+CHUNK = 512
 BF16 = jnp.bfloat16
 F32 = jnp.float32
 
 
-def exchange(part, axes):
-    return lax.all_to_all(part, axes, 0, 0, tiled=True)
-
-
-def reduce_stage(part, axes):
-    got = exchange(part, axes)
-    count = lax.axis_size(axes)
-    return jnp.sum(got.reshape(count, -1, got.shape[-1]).astype(F32), axis=0)
-
-
-def gather_stage(part, axes):
-    count = lax.axis_size(axes)
-    copies = jnp.broadcast_to(part[None], (count,) + part.shape)
-    return exchange(copies.reshape(-1, part.shape[-1]), axes)
-
-
-def far_sum(part, scale):
-    rows, features = part.shape
-    tiles = features // LANES
-    part = part.reshape(rows, tiles, LANES).transpose(1, 0, 2).reshape(-1, LANES)
-    part = gather_stage((reduce_stage(part, FAR) * scale).astype(BF16), FAR)
-    return part.reshape(tiles, rows, LANES).transpose(1, 0, 2).reshape(rows, features)
+def member_groups():
+    sizes = [lax.axis_size(name) for name in AXES]
+    groups = ({}, {}, {})
+    for device, place in enumerate(itertools.product(*map(range, sizes))):
+        at = dict(zip(AXES, place))
+        core = at["core"]
+        chip = [2 * at[axis + "_hi"] + at[axis + "_lo"] for axis in "xyz"]
+        counts = [2 * lax.axis_size(axis + "_hi") for axis in "xyz"]
+        moved = [(spot + core) % count for spot, count in zip(chip, counts)]
+        cube = tuple(spot // 2 for spot in moved)
+        corner = tuple(spot % 2 for spot in moved)
+        groups[0].setdefault(tuple(chip), []).append(device)
+        groups[1].setdefault((core,) + cube, []).append((corner, device))
+        groups[2].setdefault((core,) + corner, []).append((cube, device))
+    pairs = list(groups[0].values())
+    near, far = ([[device for _, device in sorted(g)] for g in d.values()] for d in groups[1:])
+    return pairs, near, far
+
+
+def exchange(part, groups):
+    return lax.all_to_all(part, AXES, 0, 0, axis_index_groups=groups, tiled=True)
+
+
+def reduce_stage(part, groups):
+    got = exchange(part, groups)
+    return jnp.sum(got.reshape(len(groups[0]), -1, got.shape[-1]).astype(F32), axis=0)
+
+
+def gather_stage(part, groups):
+    copies = jnp.broadcast_to(part[None], (len(groups[0]),) + part.shape)
+    return exchange(copies.reshape(-1, part.shape[-1]), groups)
+
+
+def lane_tiles(part):
+    return jnp.concatenate(jnp.split(part, part.shape[1] // LANES, axis=1), axis=0)
+
+
+def whole_rows(part, features):
+    return jnp.concatenate(jnp.split(part, features // LANES, axis=0), axis=1)
 
 
 def inner_swap(block, axis):
@@ -56,7 +72,8 @@
 
 def silu_parts(values):
     sigmoid_v = jax.nn.sigmoid(values)
-    return values * sigmoid_v, sigmoid_v * (1.0 + values * (1.0 - sigmoid_v))
+    value = values * sigmoid_v
+    return value, sigmoid_v + value * (1.0 - sigmoid_v)
 
 
 def mm(left, right):
@@ -139,21 +156,23 @@
     inflow = jnp.zeros((block, features), F32)
     for start in range(0, slots, CHUNK):
         span = slice(start, start + CHUNK)
-        gathered = mm(one_hot_cols(src_col[span], ext.shape[0]), ext[...]).astype(BF16)
-        picked[span, :] = gathered
-        if start == 0:
-            for place in (4, 0, 1, 2):
-                copies[place].wait()
-            nodes = nodes_own[...]
-        at_dst = one_hot_cols(dst_col[span], block)
-        dst_cols[span, :] = at_dst
-        local = mm(at_dst, nodes).astype(BF16)
-        pre_act = mm(gathered, w_src[...]) + mm(local, w_dst[...])
+        at_src = one_hot_cols(src_col[span], ext.shape[0])
+        picked[span, :] = mm(at_src, ext[...]).astype(BF16)
+        dst_cols[span, :] = one_hot_cols(dst_col[span], block)
+    for place in (4, 0, 1):
+        copies[place].wait()
+    nodes = nodes_own[...]
+    for start in range(0, slots, CHUNK):
+        span = slice(start, start + CHUNK)
+        local = mm(dst_cols[span, :], nodes).astype(BF16)
+        pre_act = mm(picked[span, :], w_src[...]) + mm(local, w_dst[...])
         value, slope = silu_parts(pre_act)
         act_slope[span, :] = slope
-        hid = value.astype(BF16)
-        hidden[span, :] = hid
-        value, slope = silu_parts(mm(hid, w_msg[...]))
+        hidden[span, :] = value.astype(BF16)
+    copies[2].wait()
+    for start in range(0, slots, CHUNK):
+        span = slice(start, start + CHUNK)
+        value, slope = silu_parts(mm(hidden[span, :], w_msg[...]))
         msg_slope[span, :] = slope
         inflow = inflow + mm(dst_rows[:, span], value.astype(BF16))
     for place in (3, 5, 6):
@@ -274,22 +293,22 @@
     )
     nodes_total = block_size * lax.axis_size(LAT) * lax.axis_size(LON)
     grad_scale = 8.0 / math.sqrt(nodes_total)
-    part = reduce_stage(grads.reshape(-1, features), CORE).astype(BF16)
+    pairs, near, far = member_groups()
+    part = reduce_stage(grads.reshape(-1, features), pairs).astype(BF16)
+    part = reduce_stage(part, near).astype(BF16)
+    part = (reduce_stage(lane_tiles(part), far) * grad_scale).astype(BF16)
     window, part = lax.optimization_barrier((window, part))
     padded = jnp.pad(window, ((owner_rows, owner_rows), (0, 0)))
     triple = lax.dynamic_slice_in_dim(padded, lon_index * owner_rows, 3 * owner_rows, 0)
     left, centre, right = jnp.split(triple, 3)
     from_inner = inner_swap(jnp.where(lon_odd == 1, left, right), LON)
-    part = reduce_stage(part, NEAR).astype(BF16)
-    part, from_inner = lax.optimization_barrier((part, from_inner))
-    part = far_sum(part, grad_scale)
-    part, left, right = lax.optimization_barrier((part, left, right))
     from_outer = outer_swap(jnp.where(lon_odd == 1, right, left), LON)
-    part = gather_stage(part, NEAR)
     table_grad = (centre + from_inner + from_outer).astype(BF16)
     d_top = mm_cols(table_grad, w_top).astype(BF16)
+    part = gather_stage(part, far)
     part, d_top = lax.optimization_barrier((part, d_top))
-    weight_grads = gather_stage(part, CORE)
+    part = gather_stage(whole_rows(part, features), near)
+    weight_grads = gather_stage(part, pairs)
     return (
         updated.reshape(nodes.shape),
         weight_grads.reshape(4, features, features),
@@ -301,7 +320,7 @@
     lat_count, lon_count = mesh.shape["lat"], mesh.shape["lon"]
     fine = Mesh(
         mesh.devices.reshape(2, lat_count // 8, 2, 2, lon_count // 4, 2, 2),
-        LAT + LON,
+        AXES,
     )
     placed = (
         P(LAT, LON, None, None),
@@ -321,6 +340,6 @@
         shards,
         mesh=fine,
         in_specs=placed,
-        out_specs=(P(LAT, LON, None, None), P(), P(LAT + LON, None)),
+        out_specs=(P(LAT, LON, None, None), P(), P(AXES, None)),
         check_vma=False,
     )

time: 134 us -> 129 us (0.963)
  waiting for transfers between devices: 25 us -> 18.2 us
  blocking collectives: 52 us -> 54 us
  Pallas kernels: 10.6 us -> 8.93 us
  starting transfers between devices: 36.3 us -> 37.7 us
    all_to_all x2, waiting for transfers between devices: 24.3 us -> 16.2 us  [exchange(): lax.all_to_all(part, AXES, 0, 0, axis_index_groups=groups, tiled=True)]
    ppermute x3, starting transfers between devices: 11 us -> 15.9 us  [inner_swap(): return lax.ppermute(block, axis, [(i, i ^ 1) for i in range(count)])]
    all_to_all x2, starting transfers between devices: 17.8 us -> 14.3 us  [exchange(): lax.all_to_all(part, AXES, 0, 0, axis_index_groups=groups, tiled=True)]
    all_to_all x4, blocking collectives: 52 us -> 54 us  [exchange(): lax.all_to_all(part, AXES, 0, 0, axis_index_groups=groups, tiled=True)]
    pallas_call x1, Pallas kernels: 10.6 us -> 8.93 us  [block_round(): pl.pallas_call(block_kernel, out_shape=(jax.ShapeDtypeStruct((block, feat...]
  transfers between devices with their start and end apart: 8 -> 8, of which waited for: 4 -> 5; matrix products, arithmetic and copies ran while one was open for 2% -> 2% of each run, Pallas kernels for 0% -> 0%
where the time goes in v7:
time: 129 us; the launch traced here: 128 us
  blocking collectives  54 us (42%)
  starting transfers between devices  37.7 us (29%)
  waiting for transfers between devices  18.2 us (14%)
  Pallas kernels  8.93 us (7%)
  other arithmetic  5.02 us (4%)
  local copies, waits for them, and re-layouts  2.25 us (2%)
  between operations  1.46 us (1%)
    all_to_all x4, blocking collectives, exchange(): lax.all_to_all(part, AXES, 0, 0, axis_index_groups=groups, tiled=True)  54 us
    all_to_all x2, waiting for transfers between devices, exchange(): lax.all_to_all(part, AXES, 0, 0, axis_index_groups=groups, tiled=True)  16.2 us
    ppermute x3, starting transfers between devices, inner_swap(): return lax.ppermute(block, axis, [(i, i ^ 1) for i in range(count)])  15.9 us
    all_to_all x2, starting transfers between devices, exchange(): lax.all_to_all(part, AXES, 0, 0, axis_index_groups=groups, tiled=True)  14.3 us
    pallas_call x1, Pallas kernels, block_round(): pl.pallas_call(block_kernel, out_shape=(jax.ShapeDtypeStruct((block, feat...  8.93 us
    ppermute x3, starting transfers between devices, outer_swap(): lax.ppermute(block, axis, [(i, j) for i, j in partner.items() if 0 <= j <...  7.55 us
  transfers between devices with their start and end apart: 8, of which 5 were waited for; matrix products, arithmetic and copies ran while one was open for 2% of the time, Pallas kernels for 0%

profile of v7, /device:TPU:1, one launch (start us, length us, event | category | flops | bytes accessed | tf_op | source)
XLA Modules:
  0.0 128.5 jit_solution(16956902180657749774)
XLA Ops:
  0.6 4.0 %collective-permute-start.1 = (bf16[128,512]{1,0:T(8,128)(2,1)}, bf16[128,512]{1,0:T(8,128)(2,1)S(1)}, u32[]{:S(2)}, u32[]{:S(2)}) collective-permute-start(bf16[128,512]{1,0:T(8,128)(2,1)} %bitcast.23), channel_id=1, source_target_pairs={{0,1},{1,0},{2,3},{3,2},{4,5},{5,4},{6,7},{7,6},{8,9},{9,8},{10,11... | collective-permute-start | bytes 393224 | tf_op jit(solution)/shard_map/ppermute | solution.py:64
  4.6 0.7 collective-permute-start
  5.9 0.7 compare_select_fusion.dst_ref
  6.6 0.5 collective-permute-done.1
  7.1 0.0 collective-permute-done
  7.1 0.9 pad_maximum_fusion.mid_ref
  8.1 6.2 %collective-permute-start.2 = (bf16[384,512]{1,0:T(8,128)(2,1)S(1)}, bf16[384,512]{1,0:T(8,128)(2,1)S(1)}, u32[]{:S(2)}, u32[]{:S(2)}) collective-permute-start(bf16[384,512]{1,0:T(8,128)(2,1)S(1)} %pad_maximum_fusion.mid_ref), channel_id=1, source_target_pairs={{16,32},{32,16},{48,64},{64,48},{80,96},{96,80},{112,128},{128,112... | collective-permute-start | bytes 1179656 | tf_op jit(solution)/shard_map/ppermute | solution.py:70
  14.3 3.8 %collective-permute-start.3 = (bf16[384,512]{1,0:T(8,128)(2,1)S(1)}, bf16[384,512]{1,0:T(8,128)(2,1)S(1)}, u32[]{:S(2)}, u32[]{:S(2)}) collective-permute-start(bf16[384,512]{1,0:T(8,128)(2,1)S(1)} %pad_maximum_fusion.mid_ref), channel_id=1, source_target_pairs={{0,16},{16,0},{32,48},{48,32},{64,80},{80,64},{96,112},{112,96},{1... | collective-permute-start | bytes 1179656 | tf_op jit(solution)/shard_map/ppermute | solution.py:64
  18.1 0.7 subtract_bitcast_fusion.band_ref
  18.8 0.8 add_bitcast_fusion.src_ref
  19.5 0.2 collective-permute-done.2.low_ref
  19.8 0.0 collective-permute-done.3.high_ref
  19.8 8.9 %block_round.1 = (bf16[128,512]{1,0:T(8,128)(2,1)}, bf16[4,512,512]{2,1,0:T(8,128)(2,1)S(1)}, f32[32,512]{1,0:T(8,128)S(1)}) custom-call(bf16[384,512]{1,0:T(8,128)(2,1)S(1)} %collective-permute-done.2.low_ref, bf16[384,512]{1,0:T(8,128)(2,1)S(1)} %pad_maximum_fusion.mid_ref, bf16[384,512]{1,0:T(8,128)(2,1)S(1)} %collective-permute-done.3.high_ref, ...), custom_call_target="tpu_custom_call" | custom-call | tf_op jit(solution)/shard_map/block_round/pallas_call | solution.py:212
  28.7 5.1 %all_to_all.48 = bf16[2,1024,512]{2,1,0:T(8,128)(2,1)S(1)} all-to-all(bf16[2,1024,512]{2,1,0:T(8,128)(2,1)S(1)} %bitcast.18), channel_id=1, replica_groups={{0,16},{1,17},{2,18},{3,19},{4,20},{5,21},{6,22},{7,23},{8,24},{9,25},{..., dimensions={0} | all-to-all | bytes 4194304 | tf_op jit(solution)/shard_map/all_to_all | solution.py:41
  33.8 1.1 reduce_sum.33
  34.9 0.0 copy-start
  34.9 27.6 %all_to_all.49 = bf16[8,128,512]{2,1,0:T(8,128)(2,1)S(1)} all-to-all(bf16[8,128,512]{2,1,0:T(8,128)(2,1)S(1)} %bitcast.21), channel_id=1, replica_groups={{0,32,2,34,1,33,3,35},{4,36,6,38,5,37,7,39},{8,40,10,42,9,41,11,43},{12..., dimensions={0} | all-to-all | bytes 2097152 | tf_op jit(solution)/shard_map/all_to_all | solution.py:41
  62.4 0.1 reduce_sum.34
  62.6 0.7 pad_maximum_fusion.1
  63.3 10.4 %all-to-all-start.2 = ((bf16[32,16,128]{2,1,0:T(8,128)(2,1)}), bf16[32,16,128]{2,1,0:T(8,128)(2,1)S(1)}, u32[]{:S(2)}, u32[]{:S(2)}) async-start(bf16[32,16,128]{2,1,0:T(8,128)(2,1)} %bitcast.9), calls=%async_computation.2 | async-start | bytes 262144 | tf_op jit(solution)/shard_map/all_to_all | solution.py:41
  73.7 13.6 %all-to-all-done.2 = bf16[32,16,128]{2,1,0:T(8,128)(2,1)S(1)} async-done(((bf16[32,16,128]{2,1,0:T(8,128)(2,1)}), bf16[32,16,128]{2,1,0:T(8,128)(2,1)S(1)}, u32[]{:S(2)}, u32[]{:S(2)}) %all-to-all-start.2) | async-done | bytes 131104 | tf_op jit(solution)/shard_map/all_to_all | solution.py:41
  87.3 0.7 broadcast_in_dim.13
  88.0 3.9 %all-to-all-start.3 = ((bf16[32,16,128]{2,1,0:T(8,128)(2,1)}), bf16[32,16,128]{2,1,0:T(8,128)(2,1)S(1)}, u32[]{:S(2)}, u32[]{:S(2)}) async-start(bf16[32,16,128]{2,1,0:T(8,128)(2,1)} %broadcast_in_dim.13), calls=%async_computation.3 | async-start | bytes 262144 | tf_op jit(solution)/shard_map/all_to_all | solution.py:41
  91.9 0.7 collective-permute-start.5
  92.6 8.1 %collective-permute-start.4 = (f32[2,512]{1,0:T(2,128)S(1)}, f32[2,512]{1,0:T(2,128)S(1)}, u32[]{:S(2)}, u32[]{:S(2)}) collective-permute-start(f32[2,512]{1,0:T(2,128)S(1)} %get-tuple-element.25), channel_id=1, source_target_pairs={{0,1},{1,0},{2,3},{3,2},{4,5},{5,4},{6,7},{7,6},{8,9},{9,8},{10,11... | collective-permute-start | bytes 12296 | tf_op jit(solution)/shard_map/ppermute | solution.py:64
  100.7 0.0 collective-permute-done.5
  100.8 1.3 %collective-permute-done.4 = f32[2,512]{1,0:T(2,128)S(1)} collective-permute-done((f32[2,512]{1,0:T(2,128)S(1)}, f32[2,512]{1,0:T(2,128)S(1)}, u32[]{:S(2)}, u32[]{:S(2)}) %collective-permute-start.4) | collective-permute-done | bytes 4128 | tf_op jit(solution)/shard_map/ppermute | solution.py:64
  102.0 0.0 copy-done
  102.1 0.8 convolution_convert_fusion
  102.9 2.6 %all-to-all-done.3 = bf16[32,16,128]{2,1,0:T(8,128)(2,1)S(1)} async-done(((bf16[32,16,128]{2,1,0:T(8,128)(2,1)}), bf16[32,16,128]{2,1,0:T(8,128)(2,1)S(1)}, u32[]{:S(2)}, u32[]{:S(2)}) %all-to-all-start.3) | async-done | bytes 131104 | tf_op jit(solution)/shard_map/all_to_all | solution.py:41
  105.5 0.1 broadcast_in_dim.26
  105.6 16.0 %all_to_all.50 = bf16[8,128,512]{2,1,0:T(8,128)(2,1)S(1)} all-to-all(bf16[8,128,512]{2,1,0:T(8,128)(2,1)S(1)} %broadcast_in_dim.26), channel_id=1, replica_groups={{0,32,2,34,1,33,3,35},{4,36,6,38,5,37,7,39},{8,40,10,42,9,41,11,43},{12..., dimensions={0} | all-to-all | bytes 2097152 | tf_op jit(solution)/shard_map/all_to_all | solution.py:41
  121.6 0.1 broadcast_in_dim.28
  121.7 5.4 %all_to_all.51 = bf16[2,1024,512]{2,1,0:T(8,128)(2,1)S(1)} all-to-all(bf16[2,1024,512]{2,1,0:T(8,128)(2,1)S(1)} %broadcast_in_dim.28), channel_id=1, replica_groups={{0,16},{1,17},{2,18},{3,19},{4,20},{5,21},{6,22},{7,23},{8,24},{9,25},{..., dimensions={0} | all-to-all | bytes 4194304 | tf_op jit(solution)/shard_map/all_to_all | solution.py:41
  127.2 1.3 %copy.17 = bf16[4,512,512]{2,1,0:T(8,128)(2,1)} copy(bf16[4,512,512]{2,1,0:T(8,128)(2,1)S(1)} %bitcast.19) | data formatting | bytes 4194304
  (6 shorter events, 0.1 us)
Async XLA Ops:
  0.6 6.5 %collective-permute-start.1 = (bf16[128,512]{1,0:T(8,128)(2,1)}, bf16[128,512]{1,0:T(8,128)(2,1)S(1)}, u32[]{:S(2)}, u32[]{:S(2)}) collective-permute-start(bf16[128,512]{1,0:T(8,128)(2,1)} %bitcast.23), channel_id=1, source_target_pairs={{0,1},{1,0},{2,3},{3,2},{4,5},{5,4},{6,7},{7,6},{8,9},{9,8},{10,11... | collective-permute-start | bytes 393224 | tf_op jit(solution)/shard_map/ppermute | solution.py:64
  4.6 2.6 %collective-permute-start = (bf16[128,512]{1,0:T(8,128)(2,1)}, bf16[128,512]{1,0:T(8,128)(2,1)S(1)}, u32[]{:S(2)}, u32[]{:S(2)}) collective-permute-start(bf16[128,512]{1,0:T(8,128)(2,1)} %bitcast.24), channel_id=1, source_target_pairs={{1,2},{2,1},{3,4},{4,3},{5,6},{6,5},{7,8},{8,7},{9,10},{10,9},{11,... | collective-permute-start | bytes 393224 | tf_op jit(solution)/shard_map/ppermute | solution.py:70
  8.1 11.7 %collective-permute-start.2 = (bf16[384,512]{1,0:T(8,128)(2,1)S(1)}, bf16[384,512]{1,0:T(8,128)(2,1)S(1)}, u32[]{:S(2)}, u32[]{:S(2)}) collective-permute-start(bf16[384,512]{1,0:T(8,128)(2,1)S(1)} %pad_maximum_fusion.mid_ref), channel_id=1, source_target_pairs={{16,32},{32,16},{48,64},{64,48},{80,96},{96,80},{112,128},{128,112... | collective-permute-start | bytes 1179656 | tf_op jit(solution)/shard_map/ppermute | solution.py:70
  14.3 5.4 %collective-permute-start.3 = (bf16[384,512]{1,0:T(8,128)(2,1)S(1)}, bf16[384,512]{1,0:T(8,128)(2,1)S(1)}, u32[]{:S(2)}, u32[]{:S(2)}) collective-permute-start(bf16[384,512]{1,0:T(8,128)(2,1)S(1)} %pad_maximum_fusion.mid_ref), channel_id=1, source_target_pairs={{0,16},{16,0},{32,48},{48,32},{64,80},{80,64},{96,112},{112,96},{1... | collective-permute-start | bytes 1179656 | tf_op jit(solution)/shard_map/ppermute | solution.py:64
  34.9 67.2 %copy-start = (bf16[512,512]{1,0:T(8,128)(2,1)S(1)}, bf16[512,512]{1,0:T(8,128)(2,1)}, u32[]{:S(2)}) copy-start(bf16[512,512]{1,0:T(8,128)(2,1)} %w_top_ref.1) | copy-start | bytes 1572868
  63.3 24.0 %all-to-all-start.2 = ((bf16[32,16,128]{2,1,0:T(8,128)(2,1)}), bf16[32,16,128]{2,1,0:T(8,128)(2,1)S(1)}, u32[]{:S(2)}, u32[]{:S(2)}) async-start(bf16[32,16,128]{2,1,0:T(8,128)(2,1)} %bitcast.9), calls=%async_computation.2 | async-start | bytes 262144 | tf_op jit(solution)/shard_map/all_to_all | solution.py:41
  88.0 17.5 %all-to-all-start.3 = ((bf16[32,16,128]{2,1,0:T(8,128)(2,1)}), bf16[32,16,128]{2,1,0:T(8,128)(2,1)S(1)}, u32[]{:S(2)}, u32[]{:S(2)}) async-start(bf16[32,16,128]{2,1,0:T(8,128)(2,1)} %broadcast_in_dim.13), calls=%async_computation.3 | async-start | bytes 262144 | tf_op jit(solution)/shard_map/all_to_all | solution.py:41
  91.9 8.8 %collective-permute-start.5 = (f32[2,512]{1,0:T(2,128)S(1)}, f32[2,512]{1,0:T(2,128)S(1)}, u32[]{:S(2)}, u32[]{:S(2)}) collective-permute-start(f32[2,512]{1,0:T(2,128)S(1)} %get-tuple-element.26), channel_id=1, source_target_pairs={{1,2},{2,1},{3,4},{4,3},{5,6},{6,5},{7,8},{8,7},{9,10},{10,9},{11,... | collective-permute-start | bytes 12296 | tf_op jit(solution)/shard_map/ppermute | solution.py:70
  92.6 9.5 %collective-permute-start.4 = (f32[2,512]{1,0:T(2,128)S(1)}, f32[2,512]{1,0:T(2,128)S(1)}, u32[]{:S(2)}, u32[]{:S(2)}) collective-permute-start(f32[2,512]{1,0:T(2,128)S(1)} %get-tuple-element.25), channel_id=1, source_target_pairs={{0,1},{1,0},{2,3},{3,2},{4,5},{5,4},{6,7},{7,6},{8,9},{9,8},{10,11... | collective-permute-start | bytes 12296 | tf_op jit(solution)/shard_map/ppermute | solution.py:64

commit v8 on v7

--- a/solution.py
+++ b/solution.py
@@ -102,11 +102,8 @@
     return (ids_row == row_ids).astype(F32).astype(BF16)
 
 
-def block_kernel(
-    low_ref,
+def first_kernel(
     mid_ref,
-    high_ref,
-    nodes_ref,
     top_ref,
     cot_ref,
     w_src_ref,
@@ -116,6 +113,103 @@
     src_ref,
     dst_ref,
     band_ref,
+    picked_ref,
+    dst_pre_ref,
+    rows_ref,
+    dst_cols_ref,
+    top_own,
+    cot_own,
+    w_src,
+    w_msg,
+    w_dst,
+    w_top,
+    arrived,
+):
+    moves = (
+        (w_dst_ref, w_dst),
+        (w_top_ref, w_top),
+        (top_ref, top_own),
+        (w_src_ref, w_src),
+        (w_msg_ref, w_msg),
+        (cot_ref, cot_own),
+    )
+    copies = [
+        pltpu.make_async_copy(source, target, arrived.at[place])
+        for place, (source, target) in enumerate(moves)
+    ]
+    for copy in copies:
+        copy.start()
+    slots = src_ref.shape[-1]
+    third = mid_ref.shape[0]
+    block = third // 3
+    nodes = mid_ref[block : 2 * block, :]
+    src_col = column(src_ref[...]) - third
+    dst_col = column(dst_ref[...])
+    for start in range(0, slots, CHUNK):
+        span = slice(start, start + CHUNK)
+        at_src = one_hot_cols(src_col[span], third)
+        picked_ref[span, :] = mm(at_src, mid_ref[...]).astype(BF16)
+        dst_cols_ref[span, :] = one_hot_cols(dst_col[span], block)
+    copies[0].wait()
+    for start in range(0, slots, CHUNK):
+        span = slice(start, start + CHUNK)
+        local = mm(dst_cols_ref[span, :], nodes).astype(BF16)
+        dst_pre_ref[span, :] = mm(local, w_dst[...])
+    copies[1].wait()
+    copies[2].wait()
+    top_table = mm(top_own[...], w_top[...]).astype(BF16)
+    band_col = column(band_ref[...])
+    rows_ref[...] = mm(one_hot_cols(band_col, top_own.shape[0]), top_table)
+    for copy in copies[3:]:
+        copy.wait()
+
+
+def first_round(mid, *args):
+    top_nodes, cot, w_src = args[0], args[1], args[2]
+    slots = args[6].shape[-1]
+    block, features = cot.shape
+    vmem = pl.BlockSpec(memory_space=pltpu.MemorySpace.VMEM)
+    hbm = pltpu.MemorySpace.HBM
+    stay = [pltpu.with_memory_space_constraint(array, hbm) for array in args[:6]]
+    return pl.pallas_call(
+        first_kernel,
+        out_shape=(
+            jax.ShapeDtypeStruct((slots, features), BF16),
+            jax.ShapeDtypeStruct((slots, features), F32),
+            jax.ShapeDtypeStruct((block, features), F32),
+            jax.ShapeDtypeStruct((slots, block), BF16),
+            jax.ShapeDtypeStruct(top_nodes.shape, BF16),
+            jax.ShapeDtypeStruct(cot.shape, BF16),
+            jax.ShapeDtypeStruct(w_src.shape, BF16),
+            jax.ShapeDtypeStruct(w_src.shape, BF16),
+        ),
+        scratch_shapes=[
+            pltpu.VMEM(w_src.shape, BF16),
+            pltpu.VMEM(w_src.shape, BF16),
+            pltpu.SemaphoreType.DMA((6,)),
+        ],
+        in_specs=[vmem] + [pl.BlockSpec(memory_space=hbm)] * 6 + [vmem] * 3,
+        out_specs=(vmem,) * 8,
+        compiler_params=pltpu.CompilerParams(vmem_limit_bytes=32 << 20),
+        name="first_round",
+    )(mid, *stay, *args[6:])
+
+
+def block_kernel(
+    low_ref,
+    mid_ref,
+    high_ref,
+    src_ref,
+    dst_ref,
+    band_ref,
+    picked_ref,
+    dst_pre_ref,
+    rows_ref,
+    dst_cols,
+    top_ref,
+    cot_ref,
+    w_src,
+    w_msg,
     updated_ref,
     grads_ref,
     window_ref,
@@ -126,66 +220,37 @@
     act_grad,
     act_slope,
     msg_slope,
-    dst_cols,
-    w_src,
-    w_dst,
-    w_msg,
-    w_top,
-    nodes_own,
-    top_own,
-    cot_own,
-    arrived,
 ):
-    held = (w_src, w_dst, w_msg, w_top, nodes_own, top_own, cot_own)
-    sources = (w_src_ref, w_dst_ref, w_msg_ref, w_top_ref, nodes_ref, top_ref, cot_ref)
-    copies = [
-        pltpu.make_async_copy(source, target, arrived.at[place])
-        for place, (source, target) in enumerate(zip(sources, held))
-    ]
-    for place in (4, 0, 1, 2, 3, 5, 6):
-        copies[place].start()
     slots = src_ref.shape[-1]
-    block, features = nodes_own.shape
-    third = low_ref.shape[0]
+    third, features = mid_ref.shape
+    block = third // 3
     ext[0:third, :] = low_ref[...]
-    ext[third : 2 * third, :] = mid_ref[...]
-    ext[2 * third :, :] = high_ref[...]
-    src_col = column(src_ref[...])
-    dst_col = column(dst_ref[...])
+    ext[third:, :] = high_ref[...]
+    nodes = mid_ref[block : 2 * block, :]
+    src_row = src_ref[...]
+    src_row = jnp.where(src_row < third, src_row, src_row - third)
+    inside = (src_ref[...] >= third) & (src_ref[...] < 2 * third)
+    src_col = column(jnp.where(inside, -1, src_row))
     dst_rows = one_hot_rows(dst_ref[...], block)
-    inflow = jnp.zeros((block, features), F32)
+    inflow = rows_ref[...]
     for start in range(0, slots, CHUNK):
         span = slice(start, start + CHUNK)
-        at_src = one_hot_cols(src_col[span], ext.shape[0])
-        picked[span, :] = mm(at_src, ext[...]).astype(BF16)
-        dst_cols[span, :] = one_hot_cols(dst_col[span], block)
-    for place in (4, 0, 1):
-        copies[place].wait()
-    nodes = nodes_own[...]
-    for start in range(0, slots, CHUNK):
-        span = slice(start, start + CHUNK)
-        local = mm(dst_cols[span, :], nodes).astype(BF16)
-        pre_act = mm(picked[span, :], w_src[...]) + mm(local, w_dst[...])
+        other = mm(one_hot_cols(src_col[span], 2 * third), ext[...])
+        gathered = (other + picked_ref[span, :].astype(F32)).astype(BF16)
+        picked[span, :] = gathered
+        pre_act = mm(gathered, w_src[...]) + dst_pre_ref[span, :]
         value, slope = silu_parts(pre_act)
         act_slope[span, :] = slope
-        hidden[span, :] = value.astype(BF16)
-    copies[2].wait()
-    for start in range(0, slots, CHUNK):
-        span = slice(start, start + CHUNK)
-        value, slope = silu_parts(mm(hidden[span, :], w_msg[...]))
+        hid = value.astype(BF16)
+        hidden[span, :] = hid
+        value, slope = silu_parts(mm(hid, w_msg[...]))
         msg_slope[span, :] = slope
         inflow = inflow + mm(dst_rows[:, span], value.astype(BF16))
-    for place in (3, 5, 6):
-        copies[place].wait()
-    top_count = top_own.shape[0]
-    top_nodes = top_own[...]
-    top_table = mm(top_nodes, w_top[...]).astype(BF16)
-    band_col = column(band_ref[...])
-    node_pre = inflow + mm(one_hot_cols(band_col, top_count), top_table)
-    value, slope = silu_parts(node_pre)
+    value, slope = silu_parts(inflow)
     updated_ref[...] = (nodes.astype(F32) + value).astype(BF16)
-    node_grad = (cot_own[...].astype(F32) * slope).astype(BF16)
-    window = mm(one_hot_rows(band_ref[...], top_count), node_grad)
+    node_grad = (cot_ref[...].astype(F32) * slope).astype(BF16)
+    top_nodes = top_ref[...]
+    window = mm(one_hot_rows(band_ref[...], top_nodes.shape[0]), node_grad)
     window_ref[...] = window
     grads_ref[3] = mm_rows(top_nodes, window.astype(BF16)).astype(BF16)
     dst_grad = jnp.zeros((block, features), F32)
@@ -202,44 +267,26 @@
     grads_ref[2] = mm_rows(hidden[...], pre_grad[...]).astype(BF16)
 
 
-def block_round(*args):
-    nodes, top_nodes = args[3], args[4]
-    slots = args[10].shape[-1]
-    block, features = nodes.shape
-    ext_rows = 3 * args[0].shape[0]
-    hbm = pltpu.MemorySpace.HBM
-    stay = [pltpu.with_memory_space_constraint(array, hbm) for array in args[3:10]]
+def block_round(low, mid, high, src_idx, *rest):
+    slots = src_idx.shape[-1]
+    third, features = mid.shape
+    top_rows = rest[6].shape[0]
+    vmem = pl.BlockSpec(memory_space=pltpu.MemorySpace.VMEM)
     return pl.pallas_call(
         block_kernel,
         out_shape=(
-            jax.ShapeDtypeStruct((block, features), BF16),
+            jax.ShapeDtypeStruct((third // 3, features), BF16),
             jax.ShapeDtypeStruct((4, features, features), BF16),
-            jax.ShapeDtypeStruct((top_nodes.shape[0], features), F32),
+            jax.ShapeDtypeStruct((top_rows, features), F32),
         ),
-        scratch_shapes=[
-            pltpu.VMEM((ext_rows, features), BF16),
-            pltpu.VMEM((slots, features), BF16),
-            pltpu.VMEM((slots, features), BF16),
-            pltpu.VMEM((slots, features), BF16),
-            pltpu.VMEM((slots, features), BF16),
-            pltpu.VMEM((slots, features), F32),
-            pltpu.VMEM((slots, features), F32),
-            pltpu.VMEM((slots, block), BF16),
-            pltpu.VMEM((features, features), BF16),
-            pltpu.VMEM((features, features), BF16),
-            pltpu.VMEM((features, features), BF16),
-            pltpu.VMEM((features, features), BF16),
-            pltpu.VMEM((block, features), BF16),
-            pltpu.VMEM(top_nodes.shape, BF16),
-            pltpu.VMEM((block, features), BF16),
-            pltpu.SemaphoreType.DMA((7,)),
-        ],
-        in_specs=[pl.BlockSpec(memory_space=pltpu.MemorySpace.VMEM)] * 3
-        + [pl.BlockSpec(memory_space=pltpu.MemorySpace.HBM)] * 7
-        + [pl.BlockSpec(memory_space=pltpu.MemorySpace.VMEM)] * 3,
-        compiler_params=pltpu.CompilerParams(vmem_limit_bytes=48 << 20),
+        scratch_shapes=[pltpu.VMEM((2 * third, features), BF16)]
+        + [pltpu.VMEM((slots, features), BF16)] * 4
+        + [pltpu.VMEM((slots, features), F32)] * 2,
+        in_specs=[vmem] * (4 + len(rest)),
+        out_specs=(vmem,) * 3,
+        compiler_params=pltpu.CompilerParams(vmem_limit_bytes=40 << 20),
         name="block_round",
-    )(*args[:3], *stay, *args[10:])
+    )(low, mid, high, src_idx, *rest)
 
 
 def shards(
@@ -276,11 +323,8 @@
     live_slot = lax.broadcasted_iota(jnp.int32, (1, slots), 1) < edge_count
     dst_idx = jnp.where(live_slot, dst_node.reshape(1, slots), block_size)
     band_ids = parent.reshape(1, block_size) - band_start
-    updated, grads, window = block_round(
-        low,
+    ready = first_round(
         mid,
-        high,
-        own,
         top_nodes,
         cotangent.reshape(block_size, features),
         w_src,
@@ -290,6 +334,9 @@
         src_idx,
         dst_idx,
         band_ids,
+    )
+    updated, grads, window = block_round(
+        low, mid, high, src_idx, dst_idx, band_ids, *ready
     )
     nodes_total = block_size * lax.axis_size(LAT) * lax.axis_size(LON)
     grad_scale = 8.0 / math.sqrt(nodes_total)

time: 129 us -> 126 us (0.977)
  waiting for transfers between devices: 18.2 us -> 22.5 us
  blocking collectives: 54 us -> 50.2 us
  starting transfers between devices: 37.7 us -> 34.3 us
    all_to_all x2, waiting for transfers between devices: 16.2 us -> 20.5 us  [exchange(): lax.all_to_all(part, AXES, 0, 0, axis_index_groups=groups, tiled=True)]
    all_to_all x4, blocking collectives: 54 us -> 50.2 us  [exchange(): lax.all_to_all(part, AXES, 0, 0, axis_index_groups=groups, tiled=True)]
    ppermute x3, starting transfers between devices: 15.9 us -> 12.9 us  [inner_swap(): return lax.ppermute(block, axis, [(i, i ^ 1) for i in range(count)])]
    pallas_call x1 -> x2, Pallas kernels: 8.93 us -> 8.92 us  [the longest x1 6.02 us: block_round(): pl.pallas_call(block_kernel, out_shape=(jax.ShapeDtypeStruct((third // 3,...]
  transfers between devices with their start and end apart: 8 -> 8, of which waited for: 5 -> 4; matrix products, arithmetic and copies ran while one was open for 2% -> 2% of each run, Pallas kernels for 0% -> 2%
where the time goes in v8:
time: 126 us
  blocking collectives  50.2 us (40%)
  starting transfers between devices  34.3 us (27%)
  waiting for transfers between devices  22.5 us (18%)
  Pallas kernels  8.92 us (7%)
  other arithmetic  5.02 us (4%)
  local copies, waits for them, and re-layouts  2.25 us (2%)
  between operations  1.48 us (1%)
    all_to_all x4, blocking collectives, exchange(): lax.all_to_all(part, AXES, 0, 0, axis_index_groups=groups, tiled=True)  50.2 us
    all_to_all x2, waiting for transfers between devices, exchange(): lax.all_to_all(part, AXES, 0, 0, axis_index_groups=groups, tiled=True)  20.5 us
    all_to_all x2, starting transfers between devices, exchange(): lax.all_to_all(part, AXES, 0, 0, axis_index_groups=groups, tiled=True)  14.3 us
    ppermute x3, starting transfers between devices, inner_swap(): return lax.ppermute(block, axis, [(i, i ^ 1) for i in range(count)])  12.9 us
    ppermute x3, starting transfers between devices, outer_swap(): lax.ppermute(block, axis, [(i, j) for i, j in partner.items() if 0 <= j <...  7.14 us
    pallas_call x1, Pallas kernels, block_round(): pl.pallas_call(block_kernel, out_shape=(jax.ShapeDtypeStruct((third // 3,...  6.02 us
    pallas_call x1, Pallas kernels, first_round(): pl.pallas_call(first_kernel, out_shape=(jax.ShapeDtypeStruct((slots, feat...  2.9 us
  transfers between devices with their start and end apart: 8, of which 4 were waited for; matrix products, arithmetic and copies ran while one was open for 2% of the time, Pallas kernels for 2%

profile of v8, /device:TPU:1, one launch (start us, length us, event | category | flops | bytes accessed | tf_op | source)
XLA Modules:
  0.0 125.5 jit_solution(12328239060283643068)
XLA Ops:
  0.6 0.7 collective-permute-start
  1.3 6.5 %collective-permute-start.1 = (bf16[128,512]{1,0:T(8,128)(2,1)}, bf16[128,512]{1,0:T(8,128)(2,1)S(1)}, u32[]{:S(2)}, u32[]{:S(2)}) collective-permute-start(bf16[128,512]{1,0:T(8,128)(2,1)} %bitcast.25), channel_id=1, source_target_pairs={{0,1},{1,0},{2,3},{3,2},{4,5},{5,4},{6,7},{7,6},{8,9},{9,8},{10,11... | collective-permute-start | bytes 393224 | tf_op jit(solution)/shard_map/ppermute | solution.py:64
  8.4 0.7 compare_select_fusion.dst_ref
  9.1 0.0 collective-permute-done
  9.1 1.4 %collective-permute-done.1 = bf16[128,512]{1,0:T(8,128)(2,1)S(1)} collective-permute-done((bf16[128,512]{1,0:T(8,128)(2,1)}, bf16[128,512]{1,0:T(8,128)(2,1)S(1)}, u32[]{:S(2)}, u32[]{:S(2)}) %collective-permute-start.1) | collective-permute-done | bytes 131104 | tf_op jit(solution)/shard_map/ppermute | solution.py:64
  10.5 0.9 pad_maximum_fusion.mid_ref
  11.4 5.8 %collective-permute-start.2 = (bf16[384,512]{1,0:T(8,128)(2,1)S(1)}, bf16[384,512]{1,0:T(8,128)(2,1)S(1)}, u32[]{:S(2)}, u32[]{:S(2)}) collective-permute-start(bf16[384,512]{1,0:T(8,128)(2,1)S(1)} %pad_maximum_fusion.mid_ref), channel_id=1, source_target_pairs={{16,32},{32,16},{48,64},{64,48},{80,96},{96,80},{112,128},{128,112... | collective-permute-start | bytes 1179656 | tf_op jit(solution)/shard_map/ppermute | solution.py:70
  17.2 1.9 %collective-permute-start.3 = (bf16[384,512]{1,0:T(8,128)(2,1)S(1)}, bf16[384,512]{1,0:T(8,128)(2,1)S(1)}, u32[]{:S(2)}, u32[]{:S(2)}) collective-permute-start(bf16[384,512]{1,0:T(8,128)(2,1)S(1)} %pad_maximum_fusion.mid_ref), channel_id=1, source_target_pairs={{0,16},{16,0},{32,48},{48,32},{64,80},{80,64},{96,112},{112,96},{1... | collective-permute-start | bytes 1179656 | tf_op jit(solution)/shard_map/ppermute | solution.py:64
  19.2 0.7 subtract_bitcast_fusion.band_ref
  19.8 0.8 add_bitcast_fusion.src_ref
  20.6 2.9 %first_round.1 = (bf16[1024,512]{1,0:T(8,128)(2,1)S(1)}, f32[1024,512]{1,0:T(8,128)S(1)}, f32[128,512]{1,0:T(8,128)S(1)}, bf16[1024,128]{1,0:T(8,128)(2,1)S(1)},...) custom-call(bf16[384,512]{1,0:T(8,128)(2,1)S(1)} %pad_maximum_fusion, ...), custom_call_target="tpu_custom_call" | custom-call | tf_op jit(solution)/shard_map/first_round/pallas_call | solution.py:174
  23.5 0.0 collective-permute-done.2.low_ref
  23.5 0.0 collective-permute-done.3.high_ref
  23.5 6.0 %block_round.1 = (bf16[128,512]{1,0:T(8,128)(2,1)}, bf16[4,512,512]{2,1,0:T(8,128)(2,1)S(1)}, f32[32,512]{1,0:T(8,128)S(1)}) custom-call(bf16[384,512]{1,0:T(8,128)(2,1)S(1)} %collective-permute-done.2.low_ref, bf16[384,512]{1,0:T(8,128)(2,1)S(1)} %pad_maximum_fusion.mid_ref, bf16[384,512]{1,0:T(8,128)(2,1)S(1)} %collective-permute-done.3.high_ref, ...), custom_call_target="tpu_custom_call" | custom-call | tf_op jit(solution)/shard_map/block_round/pallas_call | solution.py:275
  29.5 5.5 %all_to_all.48 = bf16[2,1024,512]{2,1,0:T(8,128)(2,1)S(1)} all-to-all(bf16[2,1024,512]{2,1,0:T(8,128)(2,1)S(1)} %bitcast.18), channel_id=1, replica_groups={{0,16},{1,17},{2,18},{3,19},{4,20},{5,21},{6,22},{7,23},{8,24},{9,25},{..., dimensions={0} | all-to-all | bytes 4194304 | tf_op jit(solution)/shard_map/all_to_all | solution.py:41
  35.1 1.1 reduce_sum.33
  36.2 0.0 copy-start
  36.2 23.2 %all_to_all.49 = bf16[8,128,512]{2,1,0:T(8,128)(2,1)S(1)} all-to-all(bf16[8,128,512]{2,1,0:T(8,128)(2,1)S(1)} %bitcast.21), channel_id=1, replica_groups={{0,32,2,34,1,33,3,35},{4,36,6,38,5,37,7,39},{8,40,10,42,9,41,11,43},{12..., dimensions={0} | all-to-all | bytes 2097152 | tf_op jit(solution)/shard_map/all_to_all | solution.py:41
  59.4 0.1 reduce_sum.34
  59.6 0.7 pad_maximum_fusion.1
  60.3 10.4 %all-to-all-start.2 = ((bf16[32,16,128]{2,1,0:T(8,128)(2,1)}), bf16[32,16,128]{2,1,0:T(8,128)(2,1)S(1)}, u32[]{:S(2)}, u32[]{:S(2)}) async-start(bf16[32,16,128]{2,1,0:T(8,128)(2,1)} %bitcast.9), calls=%async_computation.2 | async-start | bytes 262144 | tf_op jit(solution)/shard_map/all_to_all | solution.py:41
  70.7 13.6 %all-to-all-done.2 = bf16[32,16,128]{2,1,0:T(8,128)(2,1)S(1)} async-done(((bf16[32,16,128]{2,1,0:T(8,128)(2,1)}), bf16[32,16,128]{2,1,0:T(8,128)(2,1)S(1)}, u32[]{:S(2)}, u32[]{:S(2)}) %all-to-all-start.2) | async-done | bytes 131104 | tf_op jit(solution)/shard_map/all_to_all | solution.py:41
  84.3 0.7 broadcast_in_dim.13
  85.0 3.9 %all-to-all-start.3 = ((bf16[32,16,128]{2,1,0:T(8,128)(2,1)}), bf16[32,16,128]{2,1,0:T(8,128)(2,1)S(1)}, u32[]{:S(2)}, u32[]{:S(2)}) async-start(bf16[32,16,128]{2,1,0:T(8,128)(2,1)} %broadcast_in_dim.13), calls=%async_computation.3 | async-start | bytes 262144 | tf_op jit(solution)/shard_map/all_to_all | solution.py:41
  88.9 4.5 %collective-permute-start.4 = (f32[2,512]{1,0:T(2,128)S(1)}, f32[2,512]{1,0:T(2,128)S(1)}, u32[]{:S(2)}, u32[]{:S(2)}) collective-permute-start(f32[2,512]{1,0:T(2,128)S(1)} %get-tuple-element.41), channel_id=1, source_target_pairs={{0,1},{1,0},{2,3},{3,2},{4,5},{5,4},{6,7},{7,6},{8,9},{9,8},{10,11... | collective-permute-start | bytes 12296 | tf_op jit(solution)/shard_map/ppermute | solution.py:64
  93.5 0.7 collective-permute-start.5
  94.1 0.6 collective-permute-done.4
  94.8 0.0 collective-permute-done.5
  94.8 0.0 copy-done
  94.8 0.8 convolution_convert_fusion
  95.6 6.9 %all-to-all-done.3 = bf16[32,16,128]{2,1,0:T(8,128)(2,1)S(1)} async-done(((bf16[32,16,128]{2,1,0:T(8,128)(2,1)}), bf16[32,16,128]{2,1,0:T(8,128)(2,1)S(1)}, u32[]{:S(2)}, u32[]{:S(2)}) %all-to-all-start.3) | async-done | bytes 131104 | tf_op jit(solution)/shard_map/all_to_all | solution.py:41
  102.6 0.1 broadcast_in_dim.26
  102.7 16.0 %all_to_all.50 = bf16[8,128,512]{2,1,0:T(8,128)(2,1)S(1)} all-to-all(bf16[8,128,512]{2,1,0:T(8,128)(2,1)S(1)} %broadcast_in_dim.26), channel_id=1, replica_groups={{0,32,2,34,1,33,3,35},{4,36,6,38,5,37,7,39},{8,40,10,42,9,41,11,43},{12..., dimensions={0} | all-to-all | bytes 2097152 | tf_op jit(solution)/shard_map/all_to_all | solution.py:41
  118.6 0.1 broadcast_in_dim.28
  118.8 5.4 %all_to_all.51 = bf16[2,1024,512]{2,1,0:T(8,128)(2,1)S(1)} all-to-all(bf16[2,1024,512]{2,1,0:T(8,128)(2,1)S(1)} %broadcast_in_dim.28), channel_id=1, replica_groups={{0,16},{1,17},{2,18},{3,19},{4,20},{5,21},{6,22},{7,23},{8,24},{9,25},{..., dimensions={0} | all-to-all | bytes 4194304 | tf_op jit(solution)/shard_map/all_to_all | solution.py:41
  124.2 1.3 %copy.17 = bf16[4,512,512]{2,1,0:T(8,128)(2,1)} copy(bf16[4,512,512]{2,1,0:T(8,128)(2,1)S(1)} %bitcast.19) | data formatting | bytes 4194304
  (6 shorter events, 0.1 us)
Async XLA Ops:
  0.6 8.5 %collective-permute-start = (bf16[128,512]{1,0:T(8,128)(2,1)}, bf16[128,512]{1,0:T(8,128)(2,1)S(1)}, u32[]{:S(2)}, u32[]{:S(2)}) collective-permute-start(bf16[128,512]{1,0:T(8,128)(2,1)} %bitcast.24), channel_id=1, source_target_pairs={{1,2},{2,1},{3,4},{4,3},{5,6},{6,5},{7,8},{8,7},{9,10},{10,9},{11,... | collective-permute-start | bytes 393224 | tf_op jit(solution)/shard_map/ppermute | solution.py:70
  1.3 9.2 %collective-permute-start.1 = (bf16[128,512]{1,0:T(8,128)(2,1)}, bf16[128,512]{1,0:T(8,128)(2,1)S(1)}, u32[]{:S(2)}, u32[]{:S(2)}) collective-permute-start(bf16[128,512]{1,0:T(8,128)(2,1)} %bitcast.25), channel_id=1, source_target_pairs={{0,1},{1,0},{2,3},{3,2},{4,5},{5,4},{6,7},{7,6},{8,9},{9,8},{10,11... | collective-permute-start | bytes 393224 | tf_op jit(solution)/shard_map/ppermute | solution.py:64
  11.4 12.1 %collective-permute-start.2 = (bf16[384,512]{1,0:T(8,128)(2,1)S(1)}, bf16[384,512]{1,0:T(8,128)(2,1)S(1)}, u32[]{:S(2)}, u32[]{:S(2)}) collective-permute-start(bf16[384,512]{1,0:T(8,128)(2,1)S(1)} %pad_maximum_fusion.mid_ref), channel_id=1, source_target_pairs={{16,32},{32,16},{48,64},{64,48},{80,96},{96,80},{112,128},{128,112... | collective-permute-start | bytes 1179656 | tf_op jit(solution)/shard_map/ppermute | solution.py:70
  17.2 6.3 %collective-permute-start.3 = (bf16[384,512]{1,0:T(8,128)(2,1)S(1)}, bf16[384,512]{1,0:T(8,128)(2,1)S(1)}, u32[]{:S(2)}, u32[]{:S(2)}) collective-permute-start(bf16[384,512]{1,0:T(8,128)(2,1)S(1)} %pad_maximum_fusion.mid_ref), channel_id=1, source_target_pairs={{0,16},{16,0},{32,48},{48,32},{64,80},{80,64},{96,112},{112,96},{1... | collective-permute-start | bytes 1179656 | tf_op jit(solution)/shard_map/ppermute | solution.py:64
  36.2 58.6 %copy-start = (bf16[512,512]{1,0:T(8,128)(2,1)S(1)}, bf16[512,512]{1,0:T(8,128)(2,1)}, u32[]{:S(2)}) copy-start(bf16[512,512]{1,0:T(8,128)(2,1)} %w_top_ref.1) | copy-start | bytes 1572868
  60.3 24.0 %all-to-all-start.2 = ((bf16[32,16,128]{2,1,0:T(8,128)(2,1)}), bf16[32,16,128]{2,1,0:T(8,128)(2,1)S(1)}, u32[]{:S(2)}, u32[]{:S(2)}) async-start(bf16[32,16,128]{2,1,0:T(8,128)(2,1)} %bitcast.9), calls=%async_computation.2 | async-start | bytes 262144 | tf_op jit(solution)/shard_map/all_to_all | solution.py:41
  85.0 17.5 %all-to-all-start.3 = ((bf16[32,16,128]{2,1,0:T(8,128)(2,1)}), bf16[32,16,128]{2,1,0:T(8,128)(2,1)S(1)}, u32[]{:S(2)}, u32[]{:S(2)}) async-start(bf16[32,16,128]{2,1,0:T(8,128)(2,1)} %broadcast_in_dim.13), calls=%async_computation.3 | async-start | bytes 262144 | tf_op jit(solution)/shard_map/all_to_all | solution.py:41
  88.9 5.8 %collective-permute-start.4 = (f32[2,512]{1,0:T(2,128)S(1)}, f32[2,512]{1,0:T(2,128)S(1)}, u32[]{:S(2)}, u32[]{:S(2)}) collective-permute-start(f32[2,512]{1,0:T(2,128)S(1)} %get-tuple-element.41), channel_id=1, source_target_pairs={{0,1},{1,0},{2,3},{3,2},{4,5},{5,4},{6,7},{7,6},{8,9},{9,8},{10,11... | collective-permute-start | bytes 12296 | tf_op jit(solution)/shard_map/ppermute | solution.py:64
  93.5 1.3 %collective-permute-start.5 = (f32[2,512]{1,0:T(2,128)S(1)}, f32[2,512]{1,0:T(2,128)S(1)}, u32[]{:S(2)}, u32[]{:S(2)}) collective-permute-start(f32[2,512]{1,0:T(2,128)S(1)} %get-tuple-element.42), channel_id=1, source_target_pairs={{1,2},{2,1},{3,4},{4,3},{5,6},{6,5},{7,8},{8,7},{9,10},{10,9},{11,... | collective-permute-start | bytes 12296 | tf_op jit(solution)/shard_map/ppermute | solution.py:70

commit v9 on v8

--- a/solution.py
+++ b/solution.py
@@ -12,7 +12,6 @@
 LAT = ("x_hi", "z_hi", "z_lo", "core")
 LON = ("y_hi", "y_lo", "x_lo")
 AXES = LAT + LON
-LANES = 128
 CHUNK = 512
 BF16 = jnp.bfloat16
 F32 = jnp.float32
@@ -20,21 +19,20 @@
 
 def member_groups():
     sizes = [lax.axis_size(name) for name in AXES]
-    groups = ({}, {}, {})
+    counts = [2 * lax.axis_size(axis + "_hi") for axis in "xyz"]
+    groups = ({}, {}, {}, {})
     for device, place in enumerate(itertools.product(*map(range, sizes))):
         at = dict(zip(AXES, place))
         core = at["core"]
-        chip = [2 * at[axis + "_hi"] + at[axis + "_lo"] for axis in "xyz"]
-        counts = [2 * lax.axis_size(axis + "_hi") for axis in "xyz"]
+        chip = tuple(2 * at[axis + "_hi"] + at[axis + "_lo"] for axis in "xyz")
         moved = [(spot + core) % count for spot, count in zip(chip, counts)]
         cube = tuple(spot // 2 for spot in moved)
         corner = tuple(spot % 2 for spot in moved)
-        groups[0].setdefault(tuple(chip), []).append(device)
-        groups[1].setdefault((core,) + cube, []).append((corner, device))
-        groups[2].setdefault((core,) + corner, []).append((cube, device))
-    pairs = list(groups[0].values())
-    near, far = ([[device for _, device in sorted(g)] for g in d.values()] for d in groups[1:])
-    return pairs, near, far
+        keys = (chip, (core, cube), (core, corner, cube[2]), (core, corner, cube[:2]))
+        spots = (core, corner, cube[:2], cube[2])
+        for kind, key, spot in zip(groups, keys, spots):
+            kind.setdefault(key, []).append((spot, device))
+    return [[[device for _, device in sorted(g)] for g in kind.values()] for kind in groups]
 
 
 def exchange(part, groups):
@@ -49,14 +47,6 @@
 def gather_stage(part, groups):
     copies = jnp.broadcast_to(part[None], (len(groups[0]),) + part.shape)
     return exchange(copies.reshape(-1, part.shape[-1]), groups)
-
-
-def lane_tiles(part):
-    return jnp.concatenate(jnp.split(part, part.shape[1] // LANES, axis=1), axis=0)
-
-
-def whole_rows(part, features):
-    return jnp.concatenate(jnp.split(part, features // LANES, axis=0), axis=1)
 
 
 def inner_swap(block, axis):
@@ -340,21 +330,25 @@
     )
     nodes_total = block_size * lax.axis_size(LAT) * lax.axis_size(LON)
     grad_scale = 8.0 / math.sqrt(nodes_total)
-    pairs, near, far = member_groups()
+    pairs, near, flat, tall = member_groups()
     part = reduce_stage(grads.reshape(-1, features), pairs).astype(BF16)
     part = reduce_stage(part, near).astype(BF16)
-    part = (reduce_stage(lane_tiles(part), far) * grad_scale).astype(BF16)
     window, part = lax.optimization_barrier((window, part))
     padded = jnp.pad(window, ((owner_rows, owner_rows), (0, 0)))
     triple = lax.dynamic_slice_in_dim(padded, lon_index * owner_rows, 3 * owner_rows, 0)
     left, centre, right = jnp.split(triple, 3)
     from_inner = inner_swap(jnp.where(lon_odd == 1, left, right), LON)
+    part = reduce_stage(part, flat)
+    part, from_inner = lax.optimization_barrier((part, from_inner))
+    every = gather_stage(part, tall).reshape((-1,) + part.shape)
+    part = (jnp.sum(every, axis=0) * grad_scale).astype(BF16)
+    part, left, right = lax.optimization_barrier((part, left, right))
     from_outer = outer_swap(jnp.where(lon_odd == 1, right, left), LON)
     table_grad = (centre + from_inner + from_outer).astype(BF16)
     d_top = mm_cols(table_grad, w_top).astype(BF16)
-    part = gather_stage(part, far)
+    part = gather_stage(part, flat)
     part, d_top = lax.optimization_barrier((part, d_top))
-    part = gather_stage(whole_rows(part, features), near)
+    part = gather_stage(part, near)
     weight_grads = gather_stage(part, pairs)
     return (
         updated.reshape(nodes.shape),

time: 126 us -> 132 us (1.048)
  blocking collectives: 50.2 us -> 61.5 us
  waiting for transfers between devices: 22.5 us -> 14.4 us
  starting transfers between devices: 34.3 us -> 37.3 us
    all_to_all x4 -> x5, blocking collectives: 50.2 us -> 61.5 us  [exchange(): lax.all_to_all(part, AXES, 0, 0, axis_index_groups=groups, tiled=True)]
    all_to_all x2, waiting for transfers between devices: 20.5 us -> 13 us  [exchange(): lax.all_to_all(part, AXES, 0, 0, axis_index_groups=groups, tiled=True)]
    all_to_all x2, starting transfers between devices: 14.3 us -> 16.9 us  [exchange(): lax.all_to_all(part, AXES, 0, 0, axis_index_groups=groups, tiled=True)]
  transfers between devices with their start and end apart: 8 -> 8, of which waited for: 4 -> 3; matrix products, arithmetic and copies ran while one was open for 2% -> 3% of each run, Pallas kernels for 2% -> 2%
where the time goes in v9:
time: 132 us
  blocking collectives  61.5 us (47%)
  starting transfers between devices  37.3 us (28%)
  waiting for transfers between devices  14.4 us (11%)
  Pallas kernels  8.92 us (7%)
  other arithmetic  5 us (4%)
  local copies, waits for them, and re-layouts  2.22 us (2%)
  between operations  1.47 us (1%)
    all_to_all x5, blocking collectives, exchange(): lax.all_to_all(part, AXES, 0, 0, axis_index_groups=groups, tiled=True)  61.5 us
    all_to_all x2, starting transfers between devices, exchange(): lax.all_to_all(part, AXES, 0, 0, axis_index_groups=groups, tiled=True)  16.9 us
    ppermute x3, starting transfers between devices, inner_swap(): return lax.ppermute(block, axis, [(i, i ^ 1) for i in range(count)])  13.3 us
    all_to_all x2, waiting for transfers between devices, exchange(): lax.all_to_all(part, AXES, 0, 0, axis_index_groups=groups, tiled=True)  13 us
    ppermute x3, starting transfers between devices, outer_swap(): lax.ppermute(block, axis, [(i, j) for i, j in partner.items() if 0 <= j <...  7.14 us
    pallas_call x1, Pallas kernels, block_round(): pl.pallas_call(block_kernel, out_shape=(jax.ShapeDtypeStruct((third // 3,...  6.02 us
    pallas_call x1, Pallas kernels, first_round(): pl.pallas_call(first_kernel, out_shape=(jax.ShapeDtypeStruct((slots, feat...  2.9 us
  transfers between devices with their start and end apart: 8, of which 3 were waited for; matrix products, arithmetic and copies ran while one was open for 3% of the time, Pallas kernels for 2%

profile of v9, /device:TPU:1, one launch (start us, length us, event | category | flops | bytes accessed | tf_op | source)
XLA Modules:
  0.0 131.6 jit_solution(11243451522310692900)
XLA Ops:
  0.6 0.7 collective-permute-start
  1.3 6.5 %collective-permute-start.1 = (bf16[128,512]{1,0:T(8,128)(2,1)}, bf16[128,512]{1,0:T(8,128)(2,1)S(1)}, u32[]{:S(2)}, u32[]{:S(2)}) collective-permute-start(bf16[128,512]{1,0:T(8,128)(2,1)} %bitcast.25), channel_id=1, source_target_pairs={{0,1},{1,0},{2,3},{3,2},{4,5},{5,4},{6,7},{7,6},{8,9},{9,8},{10,11... | collective-permute-start | bytes 393224 | tf_op jit(solution)/shard_map/ppermute | solution.py:54
  8.4 0.7 compare_select_fusion.dst_ref
  9.1 0.0 collective-permute-done
  9.1 1.4 %collective-permute-done.1 = bf16[128,512]{1,0:T(8,128)(2,1)S(1)} collective-permute-done((bf16[128,512]{1,0:T(8,128)(2,1)}, bf16[128,512]{1,0:T(8,128)(2,1)S(1)}, u32[]{:S(2)}, u32[]{:S(2)}) %collective-permute-start.1) | collective-permute-done | bytes 131104 | tf_op jit(solution)/shard_map/ppermute | solution.py:54
  10.5 0.9 pad_maximum_fusion.mid_ref
  11.4 5.8 %collective-permute-start.2 = (bf16[384,512]{1,0:T(8,128)(2,1)S(1)}, bf16[384,512]{1,0:T(8,128)(2,1)S(1)}, u32[]{:S(2)}, u32[]{:S(2)}) collective-permute-start(bf16[384,512]{1,0:T(8,128)(2,1)S(1)} %pad_maximum_fusion.mid_ref), channel_id=1, source_target_pairs={{16,32},{32,16},{48,64},{64,48},{80,96},{96,80},{112,128},{128,112... | collective-permute-start | bytes 1179656 | tf_op jit(solution)/shard_map/ppermute | solution.py:60
  17.2 1.9 %collective-permute-start.3 = (bf16[384,512]{1,0:T(8,128)(2,1)S(1)}, bf16[384,512]{1,0:T(8,128)(2,1)S(1)}, u32[]{:S(2)}, u32[]{:S(2)}) collective-permute-start(bf16[384,512]{1,0:T(8,128)(2,1)S(1)} %pad_maximum_fusion.mid_ref), channel_id=1, source_target_pairs={{0,16},{16,0},{32,48},{48,32},{64,80},{80,64},{96,112},{112,96},{1... | collective-permute-start | bytes 1179656 | tf_op jit(solution)/shard_map/ppermute | solution.py:54
  19.2 0.7 subtract_bitcast_fusion.band_ref
  19.8 0.8 add_bitcast_fusion.src_ref
  20.6 2.9 %first_round.1 = (bf16[1024,512]{1,0:T(8,128)(2,1)S(1)}, f32[1024,512]{1,0:T(8,128)S(1)}, f32[128,512]{1,0:T(8,128)S(1)}, bf16[1024,128]{1,0:T(8,128)(2,1)S(1)},...) custom-call(bf16[384,512]{1,0:T(8,128)(2,1)S(1)} %pad_maximum_fusion, ...), custom_call_target="tpu_custom_call" | custom-call | tf_op jit(solution)/shard_map/first_round/pallas_call | solution.py:164
  23.5 0.0 collective-permute-done.2.low_ref
  23.5 0.0 collective-permute-done.3.high_ref
  23.5 6.0 %block_round.1 = (bf16[128,512]{1,0:T(8,128)(2,1)}, bf16[4,512,512]{2,1,0:T(8,128)(2,1)S(1)}, f32[32,512]{1,0:T(8,128)S(1)}) custom-call(bf16[384,512]{1,0:T(8,128)(2,1)S(1)} %collective-permute-done.2.low_ref, bf16[384,512]{1,0:T(8,128)(2,1)S(1)} %pad_maximum_fusion.mid_ref, bf16[384,512]{1,0:T(8,128)(2,1)S(1)} %collective-permute-done.3.high_ref, ...), custom_call_target="tpu_custom_call" | custom-call | tf_op jit(solution)/shard_map/block_round/pallas_call | solution.py:265
  29.5 5.5 %all_to_all.54 = bf16[2,1024,512]{2,1,0:T(8,128)(2,1)S(1)} all-to-all(bf16[2,1024,512]{2,1,0:T(8,128)(2,1)S(1)} %bitcast.18), channel_id=1, replica_groups={{0,16},{1,17},{2,18},{3,19},{4,20},{5,21},{6,22},{7,23},{8,24},{9,25},{..., dimensions={0} | all-to-all | bytes 4194304 | tf_op jit(solution)/shard_map/all_to_all | solution.py:39
  35.1 1.1 reduce_sum.42
  36.2 0.0 copy-start
  36.2 23.2 %all_to_all.55 = bf16[8,128,512]{2,1,0:T(8,128)(2,1)S(1)} all-to-all(bf16[8,128,512]{2,1,0:T(8,128)(2,1)S(1)} %bitcast.21), channel_id=1, replica_groups={{0,32,2,34,1,33,3,35},{4,36,6,38,5,37,7,39},{8,40,10,42,9,41,11,43},{12..., dimensions={0} | all-to-all | bytes 2097152 | tf_op jit(solution)/shard_map/all_to_all | solution.py:39
  59.4 0.8 reduce_sum.43
  60.2 8.6 %all-to-all-start.2 = ((bf16[8,16,512]{2,1,0:T(8,128)(2,1)}), bf16[8,16,512]{2,1,0:T(8,128)(2,1)S(1)}, u32[]{:S(2)}, u32[]{:S(2)}) async-start(bf16[8,16,512]{2,1,0:T(8,128)(2,1)} %bitcast.9), calls=%async_computation.2 | async-start | bytes 262144 | tf_op jit(solution)/shard_map/all_to_all | solution.py:39
  68.9 4.9 %collective-permute-start.4 = (f32[2,512]{1,0:T(2,128)S(1)}, f32[2,512]{1,0:T(2,128)S(1)}, u32[]{:S(2)}, u32[]{:S(2)}) collective-permute-start(f32[2,512]{1,0:T(2,128)S(1)} %get-tuple-element.43), channel_id=1, source_target_pairs={{0,1},{1,0},{2,3},{3,2},{4,5},{5,4},{6,7},{7,6},{8,9},{9,8},{10,11... | collective-permute-start | bytes 12296 | tf_op jit(solution)/shard_map/ppermute | solution.py:54
  73.8 4.5 %all-to-all-done.2 = bf16[8,16,512]{2,1,0:T(8,128)(2,1)S(1)} async-done(((bf16[8,16,512]{2,1,0:T(8,128)(2,1)}), bf16[8,16,512]{2,1,0:T(8,128)(2,1)S(1)}, u32[]{:S(2)}, u32[]{:S(2)}) %all-to-all-start.2) | async-done | bytes 131104 | tf_op jit(solution)/shard_map/all_to_all | solution.py:39
  78.3 0.0 collective-permute-done.4
  78.3 10.1 %all_to_all.56 = f32[4,16,512]{2,1,0:T(8,128)S(1)} all-to-all(f32[4,16,512]{2,1,0:T(8,128)S(1)} %broadcast_in_dim.15), channel_id=1, replica_groups={{0,64,128,192},{1,65,129,193},{2,66,130,194},{3,67,131,195},{4,68,132,1..., dimensions={0} | all-to-all | bytes 262144 | tf_op jit(solution)/shard_map/all_to_all | solution.py:39
  88.5 0.7 collective-permute-start.5
  89.1 0.7 broadcast_in_dim.16
  89.8 8.3 %all-to-all-start.4 = ((bf16[8,16,512]{2,1,0:T(8,128)(2,1)}), bf16[8,16,512]{2,1,0:T(8,128)(2,1)S(1)}, u32[]{:S(2)}, u32[]{:S(2)}) async-start(bf16[8,16,512]{2,1,0:T(8,128)(2,1)} %broadcast_in_dim.16), calls=%async_computation.4 | async-start | bytes 262144 | tf_op jit(solution)/shard_map/all_to_all | solution.py:39
  98.1 0.0 collective-permute-done.5
  98.1 0.0 copy-done
  98.1 0.8 convolution_convert_fusion
  98.9 8.5 %all-to-all-done.4 = bf16[8,16,512]{2,1,0:T(8,128)(2,1)S(1)} async-done(((bf16[8,16,512]{2,1,0:T(8,128)(2,1)}), bf16[8,16,512]{2,1,0:T(8,128)(2,1)S(1)}, u32[]{:S(2)}, u32[]{:S(2)}) %all-to-all-start.4) | async-done | bytes 131104 | tf_op jit(solution)/shard_map/all_to_all | solution.py:39
  107.4 0.1 broadcast_in_dim.17
  107.5 15.6 %all_to_all.57 = bf16[8,128,512]{2,1,0:T(8,128)(2,1)S(1)} all-to-all(bf16[8,128,512]{2,1,0:T(8,128)(2,1)S(1)} %broadcast_in_dim.17), channel_id=1, replica_groups={{0,32,2,34,1,33,3,35},{4,36,6,38,5,37,7,39},{8,40,10,42,9,41,11,43},{12..., dimensions={0} | all-to-all | bytes 2097152 | tf_op jit(solution)/shard_map/all_to_all | solution.py:39
  123.1 0.1 broadcast_in_dim.35
  123.3 7.0 %all_to_all.58 = bf16[2,1024,512]{2,1,0:T(8,128)(2,1)S(1)} all-to-all(bf16[2,1024,512]{2,1,0:T(8,128)(2,1)S(1)} %broadcast_in_dim.35), channel_id=1, replica_groups={{0,16},{1,17},{2,18},{3,19},{4,20},{5,21},{6,22},{7,23},{8,24},{9,25},{..., dimensions={0} | all-to-all | bytes 4194304 | tf_op jit(solution)/shard_map/all_to_all | solution.py:39
  130.3 1.3 %copy.17 = bf16[4,512,512]{2,1,0:T(8,128)(2,1)} copy(bf16[4,512,512]{2,1,0:T(8,128)(2,1)S(1)} %bitcast.19) | data formatting | bytes 4194304
  (6 shorter events, 0.1 us)
Async XLA Ops:
  0.6 8.5 %collective-permute-start = (bf16[128,512]{1,0:T(8,128)(2,1)}, bf16[128,512]{1,0:T(8,128)(2,1)S(1)}, u32[]{:S(2)}, u32[]{:S(2)}) collective-permute-start(bf16[128,512]{1,0:T(8,128)(2,1)} %bitcast.24), channel_id=1, source_target_pairs={{1,2},{2,1},{3,4},{4,3},{5,6},{6,5},{7,8},{8,7},{9,10},{10,9},{11,... | collective-permute-start | bytes 393224 | tf_op jit(solution)/shard_map/ppermute | solution.py:60
  1.3 9.2 %collective-permute-start.1 = (bf16[128,512]{1,0:T(8,128)(2,1)}, bf16[128,512]{1,0:T(8,128)(2,1)S(1)}, u32[]{:S(2)}, u32[]{:S(2)}) collective-permute-start(bf16[128,512]{1,0:T(8,128)(2,1)} %bitcast.25), channel_id=1, source_target_pairs={{0,1},{1,0},{2,3},{3,2},{4,5},{5,4},{6,7},{7,6},{8,9},{9,8},{10,11... | collective-permute-start | bytes 393224 | tf_op jit(solution)/shard_map/ppermute | solution.py:54
  11.4 12.1 %collective-permute-start.2 = (bf16[384,512]{1,0:T(8,128)(2,1)S(1)}, bf16[384,512]{1,0:T(8,128)(2,1)S(1)}, u32[]{:S(2)}, u32[]{:S(2)}) collective-permute-start(bf16[384,512]{1,0:T(8,128)(2,1)S(1)} %pad_maximum_fusion.mid_ref), channel_id=1, source_target_pairs={{16,32},{32,16},{48,64},{64,48},{80,96},{96,80},{112,128},{128,112... | collective-permute-start | bytes 1179656 | tf_op jit(solution)/shard_map/ppermute | solution.py:60
  17.2 6.3 %collective-permute-start.3 = (bf16[384,512]{1,0:T(8,128)(2,1)S(1)}, bf16[384,512]{1,0:T(8,128)(2,1)S(1)}, u32[]{:S(2)}, u32[]{:S(2)}) collective-permute-start(bf16[384,512]{1,0:T(8,128)(2,1)S(1)} %pad_maximum_fusion.mid_ref), channel_id=1, source_target_pairs={{0,16},{16,0},{32,48},{48,32},{64,80},{80,64},{96,112},{112,96},{1... | collective-permute-start | bytes 1179656 | tf_op jit(solution)/shard_map/ppermute | solution.py:54
  36.2 61.9 %copy-start = (bf16[512,512]{1,0:T(8,128)(2,1)S(1)}, bf16[512,512]{1,0:T(8,128)(2,1)}, u32[]{:S(2)}) copy-start(bf16[512,512]{1,0:T(8,128)(2,1)} %w_top_ref.1) | copy-start | bytes 1572868
  60.2 18.0 %all-to-all-start.2 = ((bf16[8,16,512]{2,1,0:T(8,128)(2,1)}), bf16[8,16,512]{2,1,0:T(8,128)(2,1)S(1)}, u32[]{:S(2)}, u32[]{:S(2)}) async-start(bf16[8,16,512]{2,1,0:T(8,128)(2,1)} %bitcast.9), calls=%async_computation.2 | async-start | bytes 262144 | tf_op jit(solution)/shard_map/all_to_all | solution.py:39
  68.9 9.4 %collective-permute-start.4 = (f32[2,512]{1,0:T(2,128)S(1)}, f32[2,512]{1,0:T(2,128)S(1)}, u32[]{:S(2)}, u32[]{:S(2)}) collective-permute-start(f32[2,512]{1,0:T(2,128)S(1)} %get-tuple-element.43), channel_id=1, source_target_pairs={{0,1},{1,0},{2,3},{3,2},{4,5},{5,4},{6,7},{7,6},{8,9},{9,8},{10,11... | collective-permute-start | bytes 12296 | tf_op jit(solution)/shard_map/ppermute | solution.py:54
  88.5 9.6 %collective-permute-start.5 = (f32[2,512]{1,0:T(2,128)S(1)}, f32[2,512]{1,0:T(2,128)S(1)}, u32[]{:S(2)}, u32[]{:S(2)}) collective-permute-start(f32[2,512]{1,0:T(2,128)S(1)} %broadcast_select_fusion.2), channel_id=1, source_target_pairs={{1,2},{2,1},{3,4},{4,3},{5,6},{6,5},{7,8},{8,7},{9,10},{10,9},{11,... | collective-permute-start | bytes 12296 | tf_op jit(solution)/shard_map/ppermute | solution.py:60
  89.8 17.7 %all-to-all-start.4 = ((bf16[8,16,512]{2,1,0:T(8,128)(2,1)}), bf16[8,16,512]{2,1,0:T(8,128)(2,1)S(1)}, u32[]{:S(2)}, u32[]{:S(2)}) async-start(bf16[8,16,512]{2,1,0:T(8,128)(2,1)} %broadcast_in_dim.16), calls=%async_computation.4 | async-start | bytes 262144 | tf_op jit(solution)/shard_map/all_to_all | solution.py:39

commit v10 on v8

--- a/solution.py
+++ b/solution.py
@@ -46,9 +46,13 @@
     return jnp.sum(got.reshape(len(groups[0]), -1, got.shape[-1]).astype(F32), axis=0)
 
 
+def copies_for(part, groups):
+    copies = jnp.broadcast_to(part[None], (len(groups[0]),) + part.shape)
+    return copies.reshape(-1, part.shape[-1])
+
+
 def gather_stage(part, groups):
-    copies = jnp.broadcast_to(part[None], (len(groups[0]),) + part.shape)
-    return exchange(copies.reshape(-1, part.shape[-1]), groups)
+    return exchange(copies_for(part, groups), groups)
 
 
 def lane_tiles(part):
@@ -343,16 +347,18 @@
     pairs, near, far = member_groups()
     part = reduce_stage(grads.reshape(-1, features), pairs).astype(BF16)
     part = reduce_stage(part, near).astype(BF16)
-    part = (reduce_stage(lane_tiles(part), far) * grad_scale).astype(BF16)
-    window, part = lax.optimization_barrier((window, part))
+    window, part = lax.optimization_barrier((window, lane_tiles(part)))
     padded = jnp.pad(window, ((owner_rows, owner_rows), (0, 0)))
     triple = lax.dynamic_slice_in_dim(padded, lon_index * owner_rows, 3 * owner_rows, 0)
     left, centre, right = jnp.split(triple, 3)
     from_inner = inner_swap(jnp.where(lon_odd == 1, left, right), LON)
+    part = (reduce_stage(part, far) * grad_scale).astype(BF16)
+    part, from_inner = lax.optimization_barrier((part, from_inner))
+    copies, left, right = lax.optimization_barrier((copies_for(part, far), left, right))
     from_outer = outer_swap(jnp.where(lon_odd == 1, right, left), LON)
     table_grad = (centre + from_inner + from_outer).astype(BF16)
     d_top = mm_cols(table_grad, w_top).astype(BF16)
-    part = gather_stage(part, far)
+    part = exchange(copies, far)
     part, d_top = lax.optimization_barrier((part, d_top))
     part = gather_stage(whole_rows(part, features), near)
     weight_grads = gather_stage(part, pairs)

time: 126 us -> 128 us (1.016)
  transfers between devices with their start and end apart: 8 -> 8, of which waited for: 4 -> 3; matrix products, arithmetic and copies ran while one was open for 2% -> 2% of each run, Pallas kernels for 2% -> 2%
where the time goes in v10:
time: 128 us; the launch traced here: 127 us
  blocking collectives  50.8 us (40%)
  starting transfers between devices  34.8 us (27%)
  waiting for transfers between devices  22.9 us (18%)
  Pallas kernels  8.92 us (7%)
  other arithmetic  5.02 us (4%)
  local copies, waits for them, and re-layouts  2.25 us (2%)
  between operations  1.51 us (1%)
    all_to_all x4, blocking collectives, exchange(): lax.all_to_all(part, AXES, 0, 0, axis_index_groups=groups, tiled=True)  50.8 us
    all_to_all x2, waiting for transfers between devices, exchange(): lax.all_to_all(part, AXES, 0, 0, axis_index_groups=groups, tiled=True)  21.5 us
    all_to_all x2, starting transfers between devices, exchange(): lax.all_to_all(part, AXES, 0, 0, axis_index_groups=groups, tiled=True)  15.2 us
    ppermute x3, starting transfers between devices, inner_swap(): return lax.ppermute(block, axis, [(i, i ^ 1) for i in range(count)])  12.4 us
    ppermute x3, starting transfers between devices, outer_swap(): lax.ppermute(block, axis, [(i, j) for i, j in partner.items() if 0 <= j <...  7.14 us
    pallas_call x1, Pallas kernels, block_round(): pl.pallas_call(block_kernel, out_shape=(jax.ShapeDtypeStruct((third // 3,...  6.02 us
    pallas_call x1, Pallas kernels, first_round(): pl.pallas_call(first_kernel, out_shape=(jax.ShapeDtypeStruct((slots, feat...  2.9 us
  transfers between devices with their start and end apart: 8, of which 3 were waited for; matrix products, arithmetic and copies ran while one was open for 2% of the time, Pallas kernels for 2%

profile of v10, /device:TPU:1, one launch (start us, length us, event | category | flops | bytes accessed | tf_op | source)
XLA Modules:
  0.0 127.0 jit_solution(8748488205882610950)
XLA Ops:
  0.6 0.7 collective-permute-start
  1.3 6.5 %collective-permute-start.1 = (bf16[128,512]{1,0:T(8,128)(2,1)}, bf16[128,512]{1,0:T(8,128)(2,1)S(1)}, u32[]{:S(2)}, u32[]{:S(2)}) collective-permute-start(bf16[128,512]{1,0:T(8,128)(2,1)} %bitcast.27), channel_id=1, source_target_pairs={{0,1},{1,0},{2,3},{3,2},{4,5},{5,4},{6,7},{7,6},{8,9},{9,8},{10,11... | collective-permute-start | bytes 393224 | tf_op jit(solution)/shard_map/ppermute | solution.py:68
  8.4 0.7 compare_select_fusion.dst_ref
  9.1 0.0 collective-permute-done
  9.1 1.4 %collective-permute-done.1 = bf16[128,512]{1,0:T(8,128)(2,1)S(1)} collective-permute-done((bf16[128,512]{1,0:T(8,128)(2,1)}, bf16[128,512]{1,0:T(8,128)(2,1)S(1)}, u32[]{:S(2)}, u32[]{:S(2)}) %collective-permute-start.1) | collective-permute-done | bytes 131104 | tf_op jit(solution)/shard_map/ppermute | solution.py:68
  10.5 0.9 pad_maximum_fusion.mid_ref
  11.4 5.8 %collective-permute-start.2 = (bf16[384,512]{1,0:T(8,128)(2,1)S(1)}, bf16[384,512]{1,0:T(8,128)(2,1)S(1)}, u32[]{:S(2)}, u32[]{:S(2)}) collective-permute-start(bf16[384,512]{1,0:T(8,128)(2,1)S(1)} %pad_maximum_fusion.mid_ref), channel_id=1, source_target_pairs={{16,32},{32,16},{48,64},{64,48},{80,96},{96,80},{112,128},{128,112... | collective-permute-start | bytes 1179656 | tf_op jit(solution)/shard_map/ppermute | solution.py:74
  17.2 1.9 %collective-permute-start.3 = (bf16[384,512]{1,0:T(8,128)(2,1)S(1)}, bf16[384,512]{1,0:T(8,128)(2,1)S(1)}, u32[]{:S(2)}, u32[]{:S(2)}) collective-permute-start(bf16[384,512]{1,0:T(8,128)(2,1)S(1)} %pad_maximum_fusion.mid_ref), channel_id=1, source_target_pairs={{0,16},{16,0},{32,48},{48,32},{64,80},{80,64},{96,112},{112,96},{1... | collective-permute-start | bytes 1179656 | tf_op jit(solution)/shard_map/ppermute | solution.py:68
  19.2 0.7 subtract_bitcast_fusion.band_ref
  19.8 0.8 add_bitcast_fusion.src_ref
  20.6 2.9 %first_round.1 = (bf16[1024,512]{1,0:T(8,128)(2,1)S(1)}, f32[1024,512]{1,0:T(8,128)S(1)}, f32[128,512]{1,0:T(8,128)S(1)}, bf16[1024,128]{1,0:T(8,128)(2,1)S(1)},...) custom-call(bf16[384,512]{1,0:T(8,128)(2,1)S(1)} %pad_maximum_fusion, ...), custom_call_target="tpu_custom_call" | custom-call | tf_op jit(solution)/shard_map/first_round/pallas_call | solution.py:178
  23.5 0.0 collective-permute-done.2.low_ref
  23.5 0.0 collective-permute-done.3.high_ref
  23.5 6.0 %block_round.1 = (bf16[128,512]{1,0:T(8,128)(2,1)}, bf16[4,512,512]{2,1,0:T(8,128)(2,1)S(1)}, f32[32,512]{1,0:T(8,128)S(1)}) custom-call(bf16[384,512]{1,0:T(8,128)(2,1)S(1)} %collective-permute-done.2.low_ref, bf16[384,512]{1,0:T(8,128)(2,1)S(1)} %pad_maximum_fusion.mid_ref, bf16[384,512]{1,0:T(8,128)(2,1)S(1)} %collective-permute-done.3.high_ref, ...), custom_call_target="tpu_custom_call" | custom-call | tf_op jit(solution)/shard_map/block_round/pallas_call | solution.py:279
  29.5 5.5 %all_to_all.51 = bf16[2,1024,512]{2,1,0:T(8,128)(2,1)S(1)} all-to-all(bf16[2,1024,512]{2,1,0:T(8,128)(2,1)S(1)} %bitcast.20), channel_id=1, replica_groups={{0,16},{1,17},{2,18},{3,19},{4,20},{5,21},{6,22},{7,23},{8,24},{9,25},{..., dimensions={0} | all-to-all | bytes 4194304 | tf_op jit(solution)/shard_map/all_to_all | solution.py:41
  35.1 1.1 reduce_sum.33
  36.2 0.0 copy-start
  36.2 23.2 %all_to_all.52 = bf16[8,128,512]{2,1,0:T(8,128)(2,1)S(1)} all-to-all(bf16[8,128,512]{2,1,0:T(8,128)(2,1)S(1)} %bitcast.23), channel_id=1, replica_groups={{0,32,2,34,1,33,3,35},{4,36,6,38,5,37,7,39},{8,40,10,42,9,41,11,43},{12..., dimensions={0} | all-to-all | bytes 2097152 | tf_op jit(solution)/shard_map/all_to_all | solution.py:41
  59.4 0.1 reduce_sum.34
  59.6 0.7 pad_maximum_fusion.1
  60.3 10.4 %all-to-all-start.2 = ((bf16[32,16,128]{2,1,0:T(8,128)(2,1)}), bf16[32,16,128]{2,1,0:T(8,128)(2,1)S(1)}, u32[]{:S(2)}, u32[]{:S(2)}) async-start(bf16[32,16,128]{2,1,0:T(8,128)(2,1)} %bitcast.9), calls=%async_computation.2 | async-start | bytes 262144 | tf_op jit(solution)/shard_map/all_to_all | solution.py:41
  70.7 4.0 %collective-permute-start.4 = (f32[2,512]{1,0:T(2,128)S(1)}, f32[2,512]{1,0:T(2,128)S(1)}, u32[]{:S(2)}, u32[]{:S(2)}) collective-permute-start(f32[2,512]{1,0:T(2,128)S(1)} %get-tuple-element.43), channel_id=1, source_target_pairs={{0,1},{1,0},{2,3},{3,2},{4,5},{5,4},{6,7},{7,6},{8,9},{9,8},{10,11... | collective-permute-start | bytes 12296 | tf_op jit(solution)/shard_map/ppermute | solution.py:68
  74.8 9.5 %all-to-all-done.2 = bf16[32,16,128]{2,1,0:T(8,128)(2,1)S(1)} async-done(((bf16[32,16,128]{2,1,0:T(8,128)(2,1)}), bf16[32,16,128]{2,1,0:T(8,128)(2,1)S(1)}, u32[]{:S(2)}, u32[]{:S(2)}) %all-to-all-start.2) | async-done | bytes 131104 | tf_op jit(solution)/shard_map/all_to_all | solution.py:41
  84.3 0.0 collective-permute-done.4
  84.3 0.7 broadcast_in_dim.13
  85.0 4.8 %all-to-all-start.3 = ((bf16[32,16,128]{2,1,0:T(8,128)(2,1)}), bf16[32,16,128]{2,1,0:T(8,128)(2,1)S(1)}, u32[]{:S(2)}, u32[]{:S(2)}) async-start(bf16[32,16,128]{2,1,0:T(8,128)(2,1)} %bitcast.11), calls=%async_computation.3 | async-start | bytes 262144 | tf_op jit(solution)/shard_map/all_to_all | solution.py:41
  89.9 0.7 collective-permute-start.5
  90.5 0.0 collective-permute-done.5
  90.5 0.0 copy-done
  90.6 0.8 convolution_convert_fusion
  91.4 12.0 %all-to-all-done.3 = bf16[32,16,128]{2,1,0:T(8,128)(2,1)S(1)} async-done(((bf16[32,16,128]{2,1,0:T(8,128)(2,1)}), bf16[32,16,128]{2,1,0:T(8,128)(2,1)S(1)}, u32[]{:S(2)}, u32[]{:S(2)}) %all-to-all-start.3) | async-done | bytes 131104 | tf_op jit(solution)/shard_map/all_to_all | solution.py:41
  103.4 0.1 broadcast_in_dim.26
  103.5 15.6 %all_to_all.53 = bf16[8,128,512]{2,1,0:T(8,128)(2,1)S(1)} all-to-all(bf16[8,128,512]{2,1,0:T(8,128)(2,1)S(1)} %broadcast_in_dim.26), channel_id=1, replica_groups={{0,32,2,34,1,33,3,35},{4,36,6,38,5,37,7,39},{8,40,10,42,9,41,11,43},{12..., dimensions={0} | all-to-all | bytes 2097152 | tf_op jit(solution)/shard_map/all_to_all | solution.py:41
  119.2 0.1 broadcast_in_dim.28
  119.3 6.3 %all_to_all.54 = bf16[2,1024,512]{2,1,0:T(8,128)(2,1)S(1)} all-to-all(bf16[2,1024,512]{2,1,0:T(8,128)(2,1)S(1)} %broadcast_in_dim.28), channel_id=1, replica_groups={{0,16},{1,17},{2,18},{3,19},{4,20},{5,21},{6,22},{7,23},{8,24},{9,25},{..., dimensions={0} | all-to-all | bytes 4194304 | tf_op jit(solution)/shard_map/all_to_all | solution.py:41
  125.7 1.3 %copy.17 = bf16[4,512,512]{2,1,0:T(8,128)(2,1)} copy(bf16[4,512,512]{2,1,0:T(8,128)(2,1)S(1)} %bitcast.21) | data formatting | bytes 4194304
  (7 shorter events, 0.1 us)
Async XLA Ops:
  0.6 8.5 %collective-permute-start = (bf16[128,512]{1,0:T(8,128)(2,1)}, bf16[128,512]{1,0:T(8,128)(2,1)S(1)}, u32[]{:S(2)}, u32[]{:S(2)}) collective-permute-start(bf16[128,512]{1,0:T(8,128)(2,1)} %bitcast.26), channel_id=1, source_target_pairs={{1,2},{2,1},{3,4},{4,3},{5,6},{6,5},{7,8},{8,7},{9,10},{10,9},{11,... | collective-permute-start | bytes 393224 | tf_op jit(solution)/shard_map/ppermute | solution.py:74
  1.3 9.2 %collective-permute-start.1 = (bf16[128,512]{1,0:T(8,128)(2,1)}, bf16[128,512]{1,0:T(8,128)(2,1)S(1)}, u32[]{:S(2)}, u32[]{:S(2)}) collective-permute-start(bf16[128,512]{1,0:T(8,128)(2,1)} %bitcast.27), channel_id=1, source_target_pairs={{0,1},{1,0},{2,3},{3,2},{4,5},{5,4},{6,7},{7,6},{8,9},{9,8},{10,11... | collective-permute-start | bytes 393224 | tf_op jit(solution)/shard_map/ppermute | solution.py:68
  11.4 12.1 %collective-permute-start.2 = (bf16[384,512]{1,0:T(8,128)(2,1)S(1)}, bf16[384,512]{1,0:T(8,128)(2,1)S(1)}, u32[]{:S(2)}, u32[]{:S(2)}) collective-permute-start(bf16[384,512]{1,0:T(8,128)(2,1)S(1)} %pad_maximum_fusion.mid_ref), channel_id=1, source_target_pairs={{16,32},{32,16},{48,64},{64,48},{80,96},{96,80},{112,128},{128,112... | collective-permute-start | bytes 1179656 | tf_op jit(solution)/shard_map/ppermute | solution.py:74
  17.2 6.3 %collective-permute-start.3 = (bf16[384,512]{1,0:T(8,128)(2,1)S(1)}, bf16[384,512]{1,0:T(8,128)(2,1)S(1)}, u32[]{:S(2)}, u32[]{:S(2)}) collective-permute-start(bf16[384,512]{1,0:T(8,128)(2,1)S(1)} %pad_maximum_fusion.mid_ref), channel_id=1, source_target_pairs={{0,16},{16,0},{32,48},{48,32},{64,80},{80,64},{96,112},{112,96},{1... | collective-permute-start | bytes 1179656 | tf_op jit(solution)/shard_map/ppermute | solution.py:68
  36.2 54.4 %copy-start = (bf16[512,512]{1,0:T(8,128)(2,1)S(1)}, bf16[512,512]{1,0:T(8,128)(2,1)}, u32[]{:S(2)}) copy-start(bf16[512,512]{1,0:T(8,128)(2,1)} %w_top_ref.1) | copy-start | bytes 1572868
  60.3 24.0 %all-to-all-start.2 = ((bf16[32,16,128]{2,1,0:T(8,128)(2,1)}), bf16[32,16,128]{2,1,0:T(8,128)(2,1)S(1)}, u32[]{:S(2)}, u32[]{:S(2)}) async-start(bf16[32,16,128]{2,1,0:T(8,128)(2,1)} %bitcast.9), calls=%async_computation.2 | async-start | bytes 262144 | tf_op jit(solution)/shard_map/all_to_all | solution.py:41
  70.7 13.6 %collective-permute-start.4 = (f32[2,512]{1,0:T(2,128)S(1)}, f32[2,512]{1,0:T(2,128)S(1)}, u32[]{:S(2)}, u32[]{:S(2)}) collective-permute-start(f32[2,512]{1,0:T(2,128)S(1)} %get-tuple-element.43), channel_id=1, source_target_pairs={{0,1},{1,0},{2,3},{3,2},{4,5},{5,4},{6,7},{7,6},{8,9},{9,8},{10,11... | collective-permute-start | bytes 12296 | tf_op jit(solution)/shard_map/ppermute | solution.py:68
  85.0 18.4 %all-to-all-start.3 = ((bf16[32,16,128]{2,1,0:T(8,128)(2,1)}), bf16[32,16,128]{2,1,0:T(8,128)(2,1)S(1)}, u32[]{:S(2)}, u32[]{:S(2)}) async-start(bf16[32,16,128]{2,1,0:T(8,128)(2,1)} %bitcast.11), calls=%async_computation.3 | async-start | bytes 262144 | tf_op jit(solution)/shard_map/all_to_all | solution.py:41
  89.9 0.7 collective-permute-start.5

commit v11 on v8

--- a/solution.py
+++ b/solution.py
@@ -13,7 +13,7 @@
 LON = ("y_hi", "y_lo", "x_lo")
 AXES = LAT + LON
 LANES = 128
-CHUNK = 512
+CHUNK = 1024
 BF16 = jnp.bfloat16
 F32 = jnp.float32
 

time: 126 us -> 126 us (level)
  no operation moved by 1% of the time
where the time goes in v11:
time: 126 us
  blocking collectives  50.6 us (40%)
  starting transfers between devices  34.3 us (27%)
  waiting for transfers between devices  22.5 us (18%)
  Pallas kernels  8.73 us (7%)
  other arithmetic  5.02 us (4%)
  local copies, waits for them, and re-layouts  2.25 us (2%)
  between operations  1.48 us (1%)
    all_to_all x4, blocking collectives, exchange(): lax.all_to_all(part, AXES, 0, 0, axis_index_groups=groups, tiled=True)  50.6 us
    all_to_all x2, waiting for transfers between devices, exchange(): lax.all_to_all(part, AXES, 0, 0, axis_index_groups=groups, tiled=True)  20.5 us
    all_to_all x2, starting transfers between devices, exchange(): lax.all_to_all(part, AXES, 0, 0, axis_index_groups=groups, tiled=True)  14.3 us
    ppermute x3, starting transfers between devices, inner_swap(): return lax.ppermute(block, axis, [(i, i ^ 1) for i in range(count)])  12.9 us
    ppermute x3, starting transfers between devices, outer_swap(): lax.ppermute(block, axis, [(i, j) for i, j in partner.items() if 0 <= j <...  7.14 us
    pallas_call x1, Pallas kernels, block_round(): pl.pallas_call(block_kernel, out_shape=(jax.ShapeDtypeStruct((third // 3,...  6.26 us
  transfers between devices with their start and end apart: 8, of which 4 were waited for; matrix products, arithmetic and copies ran while one was open for 2% of the time, Pallas kernels for 2%

profile of v11, /device:TPU:1, one launch (start us, length us, event | category | flops | bytes accessed | tf_op | source)
XLA Modules:
  0.0 125.8 jit_solution(7042969743506728524)
XLA Ops:
  0.6 0.7 collective-permute-start
  1.3 6.5 %collective-permute-start.1 = (bf16[128,512]{1,0:T(8,128)(2,1)}, bf16[128,512]{1,0:T(8,128)(2,1)S(1)}, u32[]{:S(2)}, u32[]{:S(2)}) collective-permute-start(bf16[128,512]{1,0:T(8,128)(2,1)} %bitcast.25), channel_id=1, source_target_pairs={{0,1},{1,0},{2,3},{3,2},{4,5},{5,4},{6,7},{7,6},{8,9},{9,8},{10,11... | collective-permute-start | bytes 393224 | tf_op jit(solution)/shard_map/ppermute | solution.py:64
  8.4 0.7 compare_select_fusion.dst_ref
  9.1 0.0 collective-permute-done
  9.1 1.4 %collective-permute-done.1 = bf16[128,512]{1,0:T(8,128)(2,1)S(1)} collective-permute-done((bf16[128,512]{1,0:T(8,128)(2,1)}, bf16[128,512]{1,0:T(8,128)(2,1)S(1)}, u32[]{:S(2)}, u32[]{:S(2)}) %collective-permute-start.1) | collective-permute-done | bytes 131104 | tf_op jit(solution)/shard_map/ppermute | solution.py:64
  10.5 0.9 pad_maximum_fusion.mid_ref
  11.4 5.8 %collective-permute-start.2 = (bf16[384,512]{1,0:T(8,128)(2,1)S(1)}, bf16[384,512]{1,0:T(8,128)(2,1)S(1)}, u32[]{:S(2)}, u32[]{:S(2)}) collective-permute-start(bf16[384,512]{1,0:T(8,128)(2,1)S(1)} %pad_maximum_fusion.mid_ref), channel_id=1, source_target_pairs={{16,32},{32,16},{48,64},{64,48},{80,96},{96,80},{112,128},{128,112... | collective-permute-start | bytes 1179656 | tf_op jit(solution)/shard_map/ppermute | solution.py:70
  17.2 1.9 %collective-permute-start.3 = (bf16[384,512]{1,0:T(8,128)(2,1)S(1)}, bf16[384,512]{1,0:T(8,128)(2,1)S(1)}, u32[]{:S(2)}, u32[]{:S(2)}) collective-permute-start(bf16[384,512]{1,0:T(8,128)(2,1)S(1)} %pad_maximum_fusion.mid_ref), channel_id=1, source_target_pairs={{0,16},{16,0},{32,48},{48,32},{64,80},{80,64},{96,112},{112,96},{1... | collective-permute-start | bytes 1179656 | tf_op jit(solution)/shard_map/ppermute | solution.py:64
  19.2 0.7 subtract_bitcast_fusion.band_ref
  19.8 0.8 add_bitcast_fusion.src_ref
  20.6 2.5 %first_round.1 = (bf16[1024,512]{1,0:T(8,128)(2,1)S(1)}, f32[1024,512]{1,0:T(8,128)S(1)}, f32[128,512]{1,0:T(8,128)S(1)}, bf16[1024,128]{1,0:T(8,128)(2,1)S(1)},...) custom-call(bf16[384,512]{1,0:T(8,128)(2,1)S(1)} %pad_maximum_fusion, ...), custom_call_target="tpu_custom_call" | custom-call | tf_op jit(solution)/shard_map/first_round/pallas_call | solution.py:174
  23.1 0.0 collective-permute-done.2.low_ref
  23.1 0.0 collective-permute-done.3.high_ref
  23.1 6.3 %block_round.1 = (bf16[128,512]{1,0:T(8,128)(2,1)}, bf16[4,512,512]{2,1,0:T(8,128)(2,1)S(1)}, f32[32,512]{1,0:T(8,128)S(1)}) custom-call(bf16[384,512]{1,0:T(8,128)(2,1)S(1)} %collective-permute-done.2.low_ref, bf16[384,512]{1,0:T(8,128)(2,1)S(1)} %pad_maximum_fusion.mid_ref, bf16[384,512]{1,0:T(8,128)(2,1)S(1)} %collective-permute-done.3.high_ref, ...), custom_call_target="tpu_custom_call" | custom-call | tf_op jit(solution)/shard_map/block_round/pallas_call | solution.py:275
  29.4 5.5 %all_to_all.48 = bf16[2,1024,512]{2,1,0:T(8,128)(2,1)S(1)} all-to-all(bf16[2,1024,512]{2,1,0:T(8,128)(2,1)S(1)} %bitcast.18), channel_id=1, replica_groups={{0,16},{1,17},{2,18},{3,19},{4,20},{5,21},{6,22},{7,23},{8,24},{9,25},{..., dimensions={0} | all-to-all | bytes 4194304 | tf_op jit(solution)/shard_map/all_to_all | solution.py:41
  34.9 1.1 reduce_sum.33
  36.0 0.0 copy-start
  36.0 23.7 %all_to_all.49 = bf16[8,128,512]{2,1,0:T(8,128)(2,1)S(1)} all-to-all(bf16[8,128,512]{2,1,0:T(8,128)(2,1)S(1)} %bitcast.21), channel_id=1, replica_groups={{0,32,2,34,1,33,3,35},{4,36,6,38,5,37,7,39},{8,40,10,42,9,41,11,43},{12..., dimensions={0} | all-to-all | bytes 2097152 | tf_op jit(solution)/shard_map/all_to_all | solution.py:41
  59.7 0.1 reduce_sum.34
  59.9 0.7 pad_maximum_fusion.1
  60.5 10.4 %all-to-all-start.2 = ((bf16[32,16,128]{2,1,0:T(8,128)(2,1)}), bf16[32,16,128]{2,1,0:T(8,128)(2,1)S(1)}, u32[]{:S(2)}, u32[]{:S(2)}) async-start(bf16[32,16,128]{2,1,0:T(8,128)(2,1)} %bitcast.9), calls=%async_computation.2 | async-start | bytes 262144 | tf_op jit(solution)/shard_map/all_to_all | solution.py:41
  71.0 13.6 %all-to-all-done.2 = bf16[32,16,128]{2,1,0:T(8,128)(2,1)S(1)} async-done(((bf16[32,16,128]{2,1,0:T(8,128)(2,1)}), bf16[32,16,128]{2,1,0:T(8,128)(2,1)S(1)}, u32[]{:S(2)}, u32[]{:S(2)}) %all-to-all-start.2) | async-done | bytes 131104 | tf_op jit(solution)/shard_map/all_to_all | solution.py:41
  84.6 0.7 broadcast_in_dim.13
  85.3 3.9 %all-to-all-start.3 = ((bf16[32,16,128]{2,1,0:T(8,128)(2,1)}), bf16[32,16,128]{2,1,0:T(8,128)(2,1)S(1)}, u32[]{:S(2)}, u32[]{:S(2)}) async-start(bf16[32,16,128]{2,1,0:T(8,128)(2,1)} %broadcast_in_dim.13), calls=%async_computation.3 | async-start | bytes 262144 | tf_op jit(solution)/shard_map/all_to_all | solution.py:41
  89.2 4.5 %collective-permute-start.4 = (f32[2,512]{1,0:T(2,128)S(1)}, f32[2,512]{1,0:T(2,128)S(1)}, u32[]{:S(2)}, u32[]{:S(2)}) collective-permute-start(f32[2,512]{1,0:T(2,128)S(1)} %get-tuple-element.41), channel_id=1, source_target_pairs={{0,1},{1,0},{2,3},{3,2},{4,5},{5,4},{6,7},{7,6},{8,9},{9,8},{10,11... | collective-permute-start | bytes 12296 | tf_op jit(solution)/shard_map/ppermute | solution.py:64
  93.7 0.7 collective-permute-start.5
  94.4 0.6 collective-permute-done.4
  95.0 0.0 collective-permute-done.5
  95.0 0.0 copy-done
  95.0 0.8 convolution_convert_fusion
  95.8 7.0 %all-to-all-done.3 = bf16[32,16,128]{2,1,0:T(8,128)(2,1)S(1)} async-done(((bf16[32,16,128]{2,1,0:T(8,128)(2,1)}), bf16[32,16,128]{2,1,0:T(8,128)(2,1)S(1)}, u32[]{:S(2)}, u32[]{:S(2)}) %all-to-all-start.3) | async-done | bytes 131104 | tf_op jit(solution)/shard_map/all_to_all | solution.py:41
  102.8 0.1 broadcast_in_dim.26
  102.9 16.0 %all_to_all.50 = bf16[8,128,512]{2,1,0:T(8,128)(2,1)S(1)} all-to-all(bf16[8,128,512]{2,1,0:T(8,128)(2,1)S(1)} %broadcast_in_dim.26), channel_id=1, replica_groups={{0,32,2,34,1,33,3,35},{4,36,6,38,5,37,7,39},{8,40,10,42,9,41,11,43},{12..., dimensions={0} | all-to-all | bytes 2097152 | tf_op jit(solution)/shard_map/all_to_all | solution.py:41
  118.9 0.1 broadcast_in_dim.28
  119.0 5.4 %all_to_all.51 = bf16[2,1024,512]{2,1,0:T(8,128)(2,1)S(1)} all-to-all(bf16[2,1024,512]{2,1,0:T(8,128)(2,1)S(1)} %broadcast_in_dim.28), channel_id=1, replica_groups={{0,16},{1,17},{2,18},{3,19},{4,20},{5,21},{6,22},{7,23},{8,24},{9,25},{..., dimensions={0} | all-to-all | bytes 4194304 | tf_op jit(solution)/shard_map/all_to_all | solution.py:41
  124.5 1.3 %copy.17 = bf16[4,512,512]{2,1,0:T(8,128)(2,1)} copy(bf16[4,512,512]{2,1,0:T(8,128)(2,1)S(1)} %bitcast.19) | data formatting | bytes 4194304
  (6 shorter events, 0.1 us)
Async XLA Ops:
  0.6 8.5 %collective-permute-start = (bf16[128,512]{1,0:T(8,128)(2,1)}, bf16[128,512]{1,0:T(8,128)(2,1)S(1)}, u32[]{:S(2)}, u32[]{:S(2)}) collective-permute-start(bf16[128,512]{1,0:T(8,128)(2,1)} %bitcast.24), channel_id=1, source_target_pairs={{1,2},{2,1},{3,4},{4,3},{5,6},{6,5},{7,8},{8,7},{9,10},{10,9},{11,... | collective-permute-start | bytes 393224 | tf_op jit(solution)/shard_map/ppermute | solution.py:70
  1.3 9.2 %collective-permute-start.1 = (bf16[128,512]{1,0:T(8,128)(2,1)}, bf16[128,512]{1,0:T(8,128)(2,1)S(1)}, u32[]{:S(2)}, u32[]{:S(2)}) collective-permute-start(bf16[128,512]{1,0:T(8,128)(2,1)} %bitcast.25), channel_id=1, source_target_pairs={{0,1},{1,0},{2,3},{3,2},{4,5},{5,4},{6,7},{7,6},{8,9},{9,8},{10,11... | collective-permute-start | bytes 393224 | tf_op jit(solution)/shard_map/ppermute | solution.py:64
  11.4 11.6 %collective-permute-start.2 = (bf16[384,512]{1,0:T(8,128)(2,1)S(1)}, bf16[384,512]{1,0:T(8,128)(2,1)S(1)}, u32[]{:S(2)}, u32[]{:S(2)}) collective-permute-start(bf16[384,512]{1,0:T(8,128)(2,1)S(1)} %pad_maximum_fusion.mid_ref), channel_id=1, source_target_pairs={{16,32},{32,16},{48,64},{64,48},{80,96},{96,80},{112,128},{128,112... | collective-permute-start | bytes 1179656 | tf_op jit(solution)/shard_map/ppermute | solution.py:70
  17.2 5.8 %collective-permute-start.3 = (bf16[384,512]{1,0:T(8,128)(2,1)S(1)}, bf16[384,512]{1,0:T(8,128)(2,1)S(1)}, u32[]{:S(2)}, u32[]{:S(2)}) collective-permute-start(bf16[384,512]{1,0:T(8,128)(2,1)S(1)} %pad_maximum_fusion.mid_ref), channel_id=1, source_target_pairs={{0,16},{16,0},{32,48},{48,32},{64,80},{80,64},{96,112},{112,96},{1... | collective-permute-start | bytes 1179656 | tf_op jit(solution)/shard_map/ppermute | solution.py:64
  36.0 59.0 %copy-start = (bf16[512,512]{1,0:T(8,128)(2,1)S(1)}, bf16[512,512]{1,0:T(8,128)(2,1)}, u32[]{:S(2)}) copy-start(bf16[512,512]{1,0:T(8,128)(2,1)} %w_top_ref.1) | copy-start | bytes 1572868
  60.5 24.0 %all-to-all-start.2 = ((bf16[32,16,128]{2,1,0:T(8,128)(2,1)}), bf16[32,16,128]{2,1,0:T(8,128)(2,1)S(1)}, u32[]{:S(2)}, u32[]{:S(2)}) async-start(bf16[32,16,128]{2,1,0:T(8,128)(2,1)} %bitcast.9), calls=%async_computation.2 | async-start | bytes 262144 | tf_op jit(solution)/shard_map/all_to_all | solution.py:41
  85.3 17.5 %all-to-all-start.3 = ((bf16[32,16,128]{2,1,0:T(8,128)(2,1)}), bf16[32,16,128]{2,1,0:T(8,128)(2,1)S(1)}, u32[]{:S(2)}, u32[]{:S(2)}) async-start(bf16[32,16,128]{2,1,0:T(8,128)(2,1)} %broadcast_in_dim.13), calls=%async_computation.3 | async-start | bytes 262144 | tf_op jit(solution)/shard_map/all_to_all | solution.py:41
  89.2 5.8 %collective-permute-start.4 = (f32[2,512]{1,0:T(2,128)S(1)}, f32[2,512]{1,0:T(2,128)S(1)}, u32[]{:S(2)}, u32[]{:S(2)}) collective-permute-start(f32[2,512]{1,0:T(2,128)S(1)} %get-tuple-element.41), channel_id=1, source_target_pairs={{0,1},{1,0},{2,3},{3,2},{4,5},{5,4},{6,7},{7,6},{8,9},{9,8},{10,11... | collective-permute-start | bytes 12296 | tf_op jit(solution)/shard_map/ppermute | solution.py:64
  93.7 1.3 %collective-permute-start.5 = (f32[2,512]{1,0:T(2,128)S(1)}, f32[2,512]{1,0:T(2,128)S(1)}, u32[]{:S(2)}, u32[]{:S(2)}) collective-permute-start(f32[2,512]{1,0:T(2,128)S(1)} %get-tuple-element.42), channel_id=1, source_target_pairs={{1,2},{2,1},{3,4},{4,3},{5,6},{6,5},{7,8},{8,7},{9,10},{10,9},{11,... | collective-permute-start | bytes 12296 | tf_op jit(solution)/shard_map/ppermute | solution.py:70

commit v12 on v8

--- a/solution.py
+++ b/solution.py
@@ -340,13 +340,17 @@
     )
     nodes_total = block_size * lax.axis_size(LAT) * lax.axis_size(LON)
     grad_scale = 8.0 / math.sqrt(nodes_total)
+    first_row = lon_index * owner_rows
+    grads, first_row = lax.optimization_barrier((grads, first_row))
     pairs, near, far = member_groups()
     part = reduce_stage(grads.reshape(-1, features), pairs).astype(BF16)
     part = reduce_stage(part, near).astype(BF16)
     part = (reduce_stage(lane_tiles(part), far) * grad_scale).astype(BF16)
     window, part = lax.optimization_barrier((window, part))
     padded = jnp.pad(window, ((owner_rows, owner_rows), (0, 0)))
-    triple = lax.dynamic_slice_in_dim(padded, lon_index * owner_rows, 3 * owner_rows, 0)
+    triple = lax.dynamic_slice_in_dim(
+        padded, first_row, 3 * owner_rows, 0, allow_negative_indices=False
+    )
     left, centre, right = jnp.split(triple, 3)
     from_inner = inner_swap(jnp.where(lon_odd == 1, left, right), LON)
     from_outer = outer_swap(jnp.where(lon_odd == 1, right, left), LON)

time: 126 us -> 129 us (1.024)
  waiting for transfers between devices: 22.5 us -> 25.3 us
  starting transfers between devices: 34.3 us -> 32.7 us
  blocking collectives: 50.2 us -> 51.5 us
    ppermute x3, starting transfers between devices: 12.9 us -> 17.1 us  [inner_swap(): return lax.ppermute(block, axis, [(i, i ^ 1) for i in range(count)])]
    ppermute x3, starting transfers between devices: 7.14 us -> 3.25 us  [outer_swap(): lax.ppermute(block, axis, [(i, j) for i, j in partner.items() if 0 <= j <...]
    ppermute x3, waiting for transfers between devices: 0.01 us -> 2.84 us  [outer_swap(): lax.ppermute(block, axis, [(i, j) for i, j in partner.items() if 0 <= j <...]
    all_to_all x2, starting transfers between devices: 14.3 us -> 12.4 us  [exchange(): lax.all_to_all(part, AXES, 0, 0, axis_index_groups=groups, tiled=True)]
    all_to_all x4, blocking collectives: 50.2 us -> 51.5 us  [exchange(): lax.all_to_all(part, AXES, 0, 0, axis_index_groups=groups, tiled=True)]
  transfers between devices with their start and end apart: 8 -> 8, of which waited for: 4 -> 5; matrix products, arithmetic and copies ran while one was open for 2% -> 2% of each run, Pallas kernels for 2% -> 2%
where the time goes in v12:
time: 129 us; the launch traced here: 128 us
  blocking collectives  51.5 us (40%)
  starting transfers between devices  32.7 us (25%)
  waiting for transfers between devices  25.3 us (20%)
  Pallas kernels  8.89 us (7%)
  other arithmetic  5.02 us (4%)
  local copies, waits for them, and re-layouts  2.25 us (2%)
  between operations  1.46 us (1%)
    all_to_all x4, blocking collectives, exchange(): lax.all_to_all(part, AXES, 0, 0, axis_index_groups=groups, tiled=True)  51.5 us
    all_to_all x2, waiting for transfers between devices, exchange(): lax.all_to_all(part, AXES, 0, 0, axis_index_groups=groups, tiled=True)  21.6 us
    ppermute x3, starting transfers between devices, inner_swap(): return lax.ppermute(block, axis, [(i, i ^ 1) for i in range(count)])  17.1 us
    all_to_all x2, starting transfers between devices, exchange(): lax.all_to_all(part, AXES, 0, 0, axis_index_groups=groups, tiled=True)  12.4 us
    pallas_call x1, Pallas kernels, block_round(): pl.pallas_call(block_kernel, out_shape=(jax.ShapeDtypeStruct((third // 3,...  5.99 us
    ppermute x3, starting transfers between devices, outer_swap(): lax.ppermute(block, axis, [(i, j) for i, j in partner.items() if 0 <= j <...  3.25 us
    pallas_call x1, Pallas kernels, first_round(): pl.pallas_call(first_kernel, out_shape=(jax.ShapeDtypeStruct((slots, feat...  2.9 us
    ppermute x3, waiting for transfers between devices, outer_swap(): lax.ppermute(block, axis, [(i, j) for i, j in partner.items() if 0 <= j <...  2.84 us
  transfers between devices with their start and end apart: 8, of which 5 were waited for; matrix products, arithmetic and copies ran while one was open for 2% of the time, Pallas kernels for 2%

profile of v12, /device:TPU:1, one launch (start us, length us, event | category | flops | bytes accessed | tf_op | source)
XLA Modules:
  0.0 128.0 jit_solution(12236296823177535610)
XLA Ops:
  0.6 4.0 %collective-permute-start.1 = (bf16[128,512]{1,0:T(8,128)(2,1)}, bf16[128,512]{1,0:T(8,128)(2,1)S(1)}, u32[]{:S(2)}, u32[]{:S(2)}) collective-permute-start(bf16[128,512]{1,0:T(8,128)(2,1)} %bitcast.24), channel_id=1, source_target_pairs={{0,1},{1,0},{2,3},{3,2},{4,5},{5,4},{6,7},{7,6},{8,9},{9,8},{10,11... | collective-permute-start | bytes 393224 | tf_op jit(solution)/shard_map/ppermute | solution.py:64
  4.6 0.7 collective-permute-start
  5.9 0.7 compare_select_fusion.dst_ref
  6.6 0.5 collective-permute-done.1
  7.1 0.0 collective-permute-done
  7.1 0.9 pad_maximum_fusion.mid_ref
  8.1 9.3 %collective-permute-start.3 = (bf16[384,512]{1,0:T(8,128)(2,1)S(1)}, bf16[384,512]{1,0:T(8,128)(2,1)S(1)}, u32[]{:S(2)}, u32[]{:S(2)}) collective-permute-start(bf16[384,512]{1,0:T(8,128)(2,1)S(1)} %pad_maximum_fusion.mid_ref), channel_id=1, source_target_pairs={{0,16},{16,0},{32,48},{48,32},{64,80},{80,64},{96,112},{112,96},{1... | collective-permute-start | bytes 1179656 | tf_op jit(solution)/shard_map/ppermute | solution.py:64
  17.4 1.9 %collective-permute-start.2 = (bf16[384,512]{1,0:T(8,128)(2,1)S(1)}, bf16[384,512]{1,0:T(8,128)(2,1)S(1)}, u32[]{:S(2)}, u32[]{:S(2)}) collective-permute-start(bf16[384,512]{1,0:T(8,128)(2,1)S(1)} %pad_maximum_fusion.mid_ref), channel_id=1, source_target_pairs={{16,32},{32,16},{48,64},{64,48},{80,96},{96,80},{112,128},{128,112... | collective-permute-start | bytes 1179656 | tf_op jit(solution)/shard_map/ppermute | solution.py:70
  19.4 0.7 subtract_bitcast_fusion.band_ref
  20.0 0.8 add_bitcast_fusion.src_ref
  20.8 2.9 %first_round.1 = (bf16[1024,512]{1,0:T(8,128)(2,1)S(1)}, f32[1024,512]{1,0:T(8,128)S(1)}, f32[128,512]{1,0:T(8,128)S(1)}, bf16[1024,128]{1,0:T(8,128)(2,1)S(1)},...) custom-call(bf16[384,512]{1,0:T(8,128)(2,1)S(1)} %pad_maximum_fusion, ...), custom_call_target="tpu_custom_call" | custom-call | tf_op jit(solution)/shard_map/first_round/pallas_call | solution.py:174
  23.7 0.0 collective-permute-done.3.high_ref
  23.7 2.8 %collective-permute-done.2.low_ref = bf16[384,512]{1,0:T(8,128)(2,1)S(1)} collective-permute-done((bf16[384,512]{1,0:T(8,128)(2,1)S(1)}, bf16[384,512]{1,0:T(8,128)(2,1)S(1)}, u32[]{:S(2)}, u32[]{:S(2)}) %collective-permute-start.2) | collective-permute-done | bytes 393248 | tf_op jit(solution)/shard_map/ppermute | solution.py:70
  26.5 6.0 %block_round.1 = (bf16[128,512]{1,0:T(8,128)(2,1)}, bf16[4,512,512]{2,1,0:T(8,128)(2,1)S(1)}, f32[32,512]{1,0:T(8,128)S(1)}) custom-call(bf16[384,512]{1,0:T(8,128)(2,1)S(1)} %collective-permute-done.2.low_ref, bf16[384,512]{1,0:T(8,128)(2,1)S(1)} %pad_maximum_fusion.mid_ref, bf16[384,512]{1,0:T(8,128)(2,1)S(1)} %collective-permute-done.3.high_ref, ...), custom_call_target="tpu_custom_call" | custom-call | tf_op jit(solution)/shard_map/block_round/pallas_call | solution.py:275
  32.5 5.1 %all_to_all.48 = bf16[2,1024,512]{2,1,0:T(8,128)(2,1)S(1)} all-to-all(bf16[2,1024,512]{2,1,0:T(8,128)(2,1)S(1)} %bitcast.18), channel_id=1, replica_groups={{0,16},{1,17},{2,18},{3,19},{4,20},{5,21},{6,22},{7,23},{8,24},{9,25},{..., dimensions={0} | all-to-all | bytes 4194304 | tf_op jit(solution)/shard_map/all_to_all | solution.py:41
  37.6 1.1 reduce_sum.33
  38.7 0.0 copy-start
  38.7 24.9 %all_to_all.49 = bf16[8,128,512]{2,1,0:T(8,128)(2,1)S(1)} all-to-all(bf16[8,128,512]{2,1,0:T(8,128)(2,1)S(1)} %bitcast.21), channel_id=1, replica_groups={{0,32,2,34,1,33,3,35},{4,36,6,38,5,37,7,39},{8,40,10,42,9,41,11,43},{12..., dimensions={0} | all-to-all | bytes 2097152 | tf_op jit(solution)/shard_map/all_to_all | solution.py:41
  63.6 0.1 reduce_sum.34
  63.7 0.7 pad_maximum_fusion.1
  64.4 8.3 %all-to-all-start.2 = ((bf16[32,16,128]{2,1,0:T(8,128)(2,1)}), bf16[32,16,128]{2,1,0:T(8,128)(2,1)S(1)}, u32[]{:S(2)}, u32[]{:S(2)}) async-start(bf16[32,16,128]{2,1,0:T(8,128)(2,1)} %bitcast.9), calls=%async_computation.2 | async-start | bytes 262144 | tf_op jit(solution)/shard_map/all_to_all | solution.py:41
  72.7 13.6 %all-to-all-done.2 = bf16[32,16,128]{2,1,0:T(8,128)(2,1)S(1)} async-done(((bf16[32,16,128]{2,1,0:T(8,128)(2,1)}), bf16[32,16,128]{2,1,0:T(8,128)(2,1)S(1)}, u32[]{:S(2)}, u32[]{:S(2)}) %all-to-all-start.2) | async-done | bytes 131104 | tf_op jit(solution)/shard_map/all_to_all | solution.py:41
  86.4 0.7 broadcast_in_dim.13
  87.0 4.1 %all-to-all-start.3 = ((bf16[32,16,128]{2,1,0:T(8,128)(2,1)}), bf16[32,16,128]{2,1,0:T(8,128)(2,1)S(1)}, u32[]{:S(2)}, u32[]{:S(2)}) async-start(bf16[32,16,128]{2,1,0:T(8,128)(2,1)} %broadcast_in_dim.13), calls=%async_computation.3 | async-start | bytes 262144 | tf_op jit(solution)/shard_map/all_to_all | solution.py:41
  91.2 3.8 %collective-permute-start.4 = (f32[2,512]{1,0:T(2,128)S(1)}, f32[2,512]{1,0:T(2,128)S(1)}, u32[]{:S(2)}, u32[]{:S(2)}) collective-permute-start(f32[2,512]{1,0:T(2,128)S(1)} %get-tuple-element.45), channel_id=1, source_target_pairs={{0,1},{1,0},{2,3},{3,2},{4,5},{5,4},{6,7},{7,6},{8,9},{9,8},{10,11... | collective-permute-start | bytes 12296 | tf_op jit(solution)/shard_map/ppermute | solution.py:64
  95.0 0.7 collective-permute-start.5
  95.6 0.3 collective-permute-done.4
  96.0 0.0 collective-permute-done.5
  96.0 0.0 copy-done
  96.0 0.8 convolution_convert_fusion
  96.8 8.0 %all-to-all-done.3 = bf16[32,16,128]{2,1,0:T(8,128)(2,1)S(1)} async-done(((bf16[32,16,128]{2,1,0:T(8,128)(2,1)}), bf16[32,16,128]{2,1,0:T(8,128)(2,1)S(1)}, u32[]{:S(2)}, u32[]{:S(2)}) %all-to-all-start.3) | async-done | bytes 131104 | tf_op jit(solution)/shard_map/all_to_all | solution.py:41
  104.8 0.1 broadcast_in_dim.26
  104.9 15.4 %all_to_all.50 = bf16[8,128,512]{2,1,0:T(8,128)(2,1)S(1)} all-to-all(bf16[8,128,512]{2,1,0:T(8,128)(2,1)S(1)} %broadcast_in_dim.26), channel_id=1, replica_groups={{0,32,2,34,1,33,3,35},{4,36,6,38,5,37,7,39},{8,40,10,42,9,41,11,43},{12..., dimensions={0} | all-to-all | bytes 2097152 | tf_op jit(solution)/shard_map/all_to_all | solution.py:41
  120.3 0.1 broadcast_in_dim.28
  120.4 6.2 %all_to_all.51 = bf16[2,1024,512]{2,1,0:T(8,128)(2,1)S(1)} all-to-all(bf16[2,1024,512]{2,1,0:T(8,128)(2,1)S(1)} %broadcast_in_dim.28), channel_id=1, replica_groups={{0,16},{1,17},{2,18},{3,19},{4,20},{5,21},{6,22},{7,23},{8,24},{9,25},{..., dimensions={0} | all-to-all | bytes 4194304 | tf_op jit(solution)/shard_map/all_to_all | solution.py:41
  126.6 1.3 %copy.17 = bf16[4,512,512]{2,1,0:T(8,128)(2,1)} copy(bf16[4,512,512]{2,1,0:T(8,128)(2,1)S(1)} %bitcast.19) | data formatting | bytes 4194304
  (6 shorter events, 0.1 us)
Async XLA Ops:
  0.6 6.5 %collective-permute-start.1 = (bf16[128,512]{1,0:T(8,128)(2,1)}, bf16[128,512]{1,0:T(8,128)(2,1)S(1)}, u32[]{:S(2)}, u32[]{:S(2)}) collective-permute-start(bf16[128,512]{1,0:T(8,128)(2,1)} %bitcast.24), channel_id=1, source_target_pairs={{0,1},{1,0},{2,3},{3,2},{4,5},{5,4},{6,7},{7,6},{8,9},{9,8},{10,11... | collective-permute-start | bytes 393224 | tf_op jit(solution)/shard_map/ppermute | solution.py:64
  4.6 2.6 %collective-permute-start = (bf16[128,512]{1,0:T(8,128)(2,1)}, bf16[128,512]{1,0:T(8,128)(2,1)S(1)}, u32[]{:S(2)}, u32[]{:S(2)}) collective-permute-start(bf16[128,512]{1,0:T(8,128)(2,1)} %bitcast.25), channel_id=1, source_target_pairs={{1,2},{2,1},{3,4},{4,3},{5,6},{6,5},{7,8},{8,7},{9,10},{10,9},{11,... | collective-permute-start | bytes 393224 | tf_op jit(solution)/shard_map/ppermute | solution.py:70
  8.1 15.6 %collective-permute-start.3 = (bf16[384,512]{1,0:T(8,128)(2,1)S(1)}, bf16[384,512]{1,0:T(8,128)(2,1)S(1)}, u32[]{:S(2)}, u32[]{:S(2)}) collective-permute-start(bf16[384,512]{1,0:T(8,128)(2,1)S(1)} %pad_maximum_fusion.mid_ref), channel_id=1, source_target_pairs={{0,16},{16,0},{32,48},{48,32},{64,80},{80,64},{96,112},{112,96},{1... | collective-permute-start | bytes 1179656 | tf_op jit(solution)/shard_map/ppermute | solution.py:64
  17.4 9.1 %collective-permute-start.2 = (bf16[384,512]{1,0:T(8,128)(2,1)S(1)}, bf16[384,512]{1,0:T(8,128)(2,1)S(1)}, u32[]{:S(2)}, u32[]{:S(2)}) collective-permute-start(bf16[384,512]{1,0:T(8,128)(2,1)S(1)} %pad_maximum_fusion.mid_ref), channel_id=1, source_target_pairs={{16,32},{32,16},{48,64},{64,48},{80,96},{96,80},{112,128},{128,112... | collective-permute-start | bytes 1179656 | tf_op jit(solution)/shard_map/ppermute | solution.py:70
  38.7 57.3 %copy-start = (bf16[512,512]{1,0:T(8,128)(2,1)S(1)}, bf16[512,512]{1,0:T(8,128)(2,1)}, u32[]{:S(2)}) copy-start(bf16[512,512]{1,0:T(8,128)(2,1)} %w_top_ref.1) | copy-start | bytes 1572868
  64.4 21.9 %all-to-all-start.2 = ((bf16[32,16,128]{2,1,0:T(8,128)(2,1)}), bf16[32,16,128]{2,1,0:T(8,128)(2,1)S(1)}, u32[]{:S(2)}, u32[]{:S(2)}) async-start(bf16[32,16,128]{2,1,0:T(8,128)(2,1)} %bitcast.9), calls=%async_computation.2 | async-start | bytes 262144 | tf_op jit(solution)/shard_map/all_to_all | solution.py:41
  87.0 17.7 %all-to-all-start.3 = ((bf16[32,16,128]{2,1,0:T(8,128)(2,1)}), bf16[32,16,128]{2,1,0:T(8,128)(2,1)S(1)}, u32[]{:S(2)}, u32[]{:S(2)}) async-start(bf16[32,16,128]{2,1,0:T(8,128)(2,1)} %broadcast_in_dim.13), calls=%async_computation.3 | async-start | bytes 262144 | tf_op jit(solution)/shard_map/all_to_all | solution.py:41
  91.2 4.7 %collective-permute-start.4 = (f32[2,512]{1,0:T(2,128)S(1)}, f32[2,512]{1,0:T(2,128)S(1)}, u32[]{:S(2)}, u32[]{:S(2)}) collective-permute-start(f32[2,512]{1,0:T(2,128)S(1)} %get-tuple-element.45), channel_id=1, source_target_pairs={{0,1},{1,0},{2,3},{3,2},{4,5},{5,4},{6,7},{7,6},{8,9},{9,8},{10,11... | collective-permute-start | bytes 12296 | tf_op jit(solution)/shard_map/ppermute | solution.py:64
  95.0 1.0 collective-permute-start.5

commit v13 on v8

--- a/solution.py
+++ b/solution.py
@@ -340,13 +340,14 @@
     )
     nodes_total = block_size * lax.axis_size(LAT) * lax.axis_size(LON)
     grad_scale = 8.0 / math.sqrt(nodes_total)
+    padded = jnp.pad(window, ((owner_rows, owner_rows), (0, 0)))
+    triple = lax.dynamic_slice_in_dim(padded, lon_index * owner_rows, 3 * owner_rows, 0)
+    grads, triple = lax.optimization_barrier((grads, triple))
     pairs, near, far = member_groups()
     part = reduce_stage(grads.reshape(-1, features), pairs).astype(BF16)
     part = reduce_stage(part, near).astype(BF16)
     part = (reduce_stage(lane_tiles(part), far) * grad_scale).astype(BF16)
-    window, part = lax.optimization_barrier((window, part))
-    padded = jnp.pad(window, ((owner_rows, owner_rows), (0, 0)))
-    triple = lax.dynamic_slice_in_dim(padded, lon_index * owner_rows, 3 * owner_rows, 0)
+    triple, part = lax.optimization_barrier((triple, part))
     left, centre, right = jnp.split(triple, 3)
     from_inner = inner_swap(jnp.where(lon_odd == 1, left, right), LON)
     from_outer = outer_swap(jnp.where(lon_odd == 1, right, left), LON)

time: 126 us -> 128 us (1.016)
  blocking collectives: 50.2 us -> 73.2 us
  waiting for transfers between devices: 22.5 us -> 11.6 us
  starting transfers between devices: 34.3 us -> 24.4 us
    all_to_all x4 -> x5, blocking collectives: 50.2 us -> 73.2 us  [exchange(): lax.all_to_all(part, AXES, 0, 0, axis_index_groups=groups, tiled=True)]
    all_to_all x2 -> x1, waiting for transfers between devices: 20.5 us -> 7.95 us  [exchange(): lax.all_to_all(part, AXES, 0, 0, axis_index_groups=groups, tiled=True)]
    all_to_all x2 -> x1, starting transfers between devices: 14.3 us -> 4.13 us  [exchange(): lax.all_to_all(part, AXES, 0, 0, axis_index_groups=groups, tiled=True)]
    ppermute x3, starting transfers between devices: 12.9 us -> 17.1 us  [inner_swap(): return lax.ppermute(block, axis, [(i, i ^ 1) for i in range(count)])]
    ppermute x3, starting transfers between devices: 7.14 us -> 3.25 us  [outer_swap(): lax.ppermute(block, axis, [(i, j) for i, j in partner.items() if 0 <= j <...]
    ppermute x3, waiting for transfers between devices: 0.01 us -> 2.84 us  [outer_swap(): lax.ppermute(block, axis, [(i, j) for i, j in partner.items() if 0 <= j <...]
  transfers between devices with their start and end apart: 8 -> 7, of which waited for: 4 -> 4; matrix products, arithmetic and copies ran while one was open for 2% -> 2% of each run, Pallas kernels for 2% -> 2%
where the time goes in v13:
time: 128 us; the launch traced here: 127 us
  blocking collectives  73.2 us (57%)
  starting transfers between devices  24.4 us (19%)
  waiting for transfers between devices  11.6 us (9%)
  Pallas kernels  8.89 us (7%)
  other arithmetic  4.35 us (3%)
  local copies, waits for them, and re-layouts  2.27 us (2%)
  between operations  1.47 us (1%)
    all_to_all x5, blocking collectives, exchange(): lax.all_to_all(part, AXES, 0, 0, axis_index_groups=groups, tiled=True)  73.2 us
    ppermute x3, starting transfers between devices, inner_swap(): return lax.ppermute(block, axis, [(i, i ^ 1) for i in range(count)])  17.1 us
    all_to_all x1, waiting for transfers between devices, exchange(): lax.all_to_all(part, AXES, 0, 0, axis_index_groups=groups, tiled=True)  7.95 us
    pallas_call x1, Pallas kernels, block_round(): pl.pallas_call(block_kernel, out_shape=(jax.ShapeDtypeStruct((third // 3,...  5.99 us
    all_to_all x1, starting transfers between devices, exchange(): lax.all_to_all(part, AXES, 0, 0, axis_index_groups=groups, tiled=True)  4.13 us
    ppermute x3, starting transfers between devices, outer_swap(): lax.ppermute(block, axis, [(i, j) for i, j in partner.items() if 0 <= j <...  3.25 us
    pallas_call x1, Pallas kernels, first_round(): pl.pallas_call(first_kernel, out_shape=(jax.ShapeDtypeStruct((slots, feat...  2.9 us
    ppermute x3, waiting for transfers between devices, outer_swap(): lax.ppermute(block, axis, [(i, j) for i, j in partner.items() if 0 <= j <...  2.84 us
  transfers between devices with their start and end apart: 7, of which 4 were waited for; matrix products, arithmetic and copies ran while one was open for 2% of the time, Pallas kernels for 2%

profile of v13, /device:TPU:1, one launch (start us, length us, event | category | flops | bytes accessed | tf_op | source)
XLA Modules:
  0.0 127.1 jit_solution(8121252301086171266)
XLA Ops:
  0.6 4.0 %collective-permute-start.1 = (bf16[128,512]{1,0:T(8,128)(2,1)}, bf16[128,512]{1,0:T(8,128)(2,1)S(1)}, u32[]{:S(2)}, u32[]{:S(2)}) collective-permute-start(bf16[128,512]{1,0:T(8,128)(2,1)} %bitcast.25), channel_id=1, source_target_pairs={{0,1},{1,0},{2,3},{3,2},{4,5},{5,4},{6,7},{7,6},{8,9},{9,8},{10,11... | collective-permute-start | bytes 393224 | tf_op jit(solution)/shard_map/ppermute | solution.py:64
  4.6 0.7 collective-permute-start
  5.9 0.7 compare_select_fusion.dst_ref
  6.6 0.5 collective-permute-done.1
  7.1 0.0 collective-permute-done
  7.1 0.9 pad_maximum_fusion.mid_ref
  8.1 9.3 %collective-permute-start.3 = (bf16[384,512]{1,0:T(8,128)(2,1)S(1)}, bf16[384,512]{1,0:T(8,128)(2,1)S(1)}, u32[]{:S(2)}, u32[]{:S(2)}) collective-permute-start(bf16[384,512]{1,0:T(8,128)(2,1)S(1)} %pad_maximum_fusion.mid_ref), channel_id=1, source_target_pairs={{0,16},{16,0},{32,48},{48,32},{64,80},{80,64},{96,112},{112,96},{1... | collective-permute-start | bytes 1179656 | tf_op jit(solution)/shard_map/ppermute | solution.py:64
  17.4 1.9 %collective-permute-start.2 = (bf16[384,512]{1,0:T(8,128)(2,1)S(1)}, bf16[384,512]{1,0:T(8,128)(2,1)S(1)}, u32[]{:S(2)}, u32[]{:S(2)}) collective-permute-start(bf16[384,512]{1,0:T(8,128)(2,1)S(1)} %pad_maximum_fusion.mid_ref), channel_id=1, source_target_pairs={{16,32},{32,16},{48,64},{64,48},{80,96},{96,80},{112,128},{128,112... | collective-permute-start | bytes 1179656 | tf_op jit(solution)/shard_map/ppermute | solution.py:70
  19.4 0.7 subtract_bitcast_fusion.band_ref
  20.0 0.8 add_bitcast_fusion.src_ref
  20.8 2.9 %first_round.1 = (bf16[1024,512]{1,0:T(8,128)(2,1)S(1)}, f32[1024,512]{1,0:T(8,128)S(1)}, f32[128,512]{1,0:T(8,128)S(1)}, bf16[1024,128]{1,0:T(8,128)(2,1)S(1)},...) custom-call(bf16[384,512]{1,0:T(8,128)(2,1)S(1)} %pad_maximum_fusion, ...), custom_call_target="tpu_custom_call" | custom-call | tf_op jit(solution)/shard_map/first_round/pallas_call | solution.py:174
  23.7 0.0 collective-permute-done.3.high_ref
  23.7 2.8 %collective-permute-done.2.low_ref = bf16[384,512]{1,0:T(8,128)(2,1)S(1)} collective-permute-done((bf16[384,512]{1,0:T(8,128)(2,1)S(1)}, bf16[384,512]{1,0:T(8,128)(2,1)S(1)}, u32[]{:S(2)}, u32[]{:S(2)}) %collective-permute-start.2) | collective-permute-done | bytes 393248 | tf_op jit(solution)/shard_map/ppermute | solution.py:70
  26.5 6.0 %block_round.1 = (bf16[128,512]{1,0:T(8,128)(2,1)}, bf16[4,512,512]{2,1,0:T(8,128)(2,1)S(1)}, f32[32,512]{1,0:T(8,128)S(1)}) custom-call(bf16[384,512]{1,0:T(8,128)(2,1)S(1)} %collective-permute-done.2.low_ref, bf16[384,512]{1,0:T(8,128)(2,1)S(1)} %pad_maximum_fusion.mid_ref, bf16[384,512]{1,0:T(8,128)(2,1)S(1)} %collective-permute-done.3.high_ref, ...), custom_call_target="tpu_custom_call" | custom-call | tf_op jit(solution)/shard_map/block_round/pallas_call | solution.py:275
  32.6 5.1 %all_to_all.48 = bf16[2,1024,512]{2,1,0:T(8,128)(2,1)S(1)} all-to-all(bf16[2,1024,512]{2,1,0:T(8,128)(2,1)S(1)} %bitcast.18), channel_id=1, replica_groups={{0,16},{1,17},{2,18},{3,19},{4,20},{5,21},{6,22},{7,23},{8,24},{9,25},{..., dimensions={0} | all-to-all | bytes 4194304 | tf_op jit(solution)/shard_map/all_to_all | solution.py:41
  37.6 1.1 reduce_sum.33
  38.7 0.0 copy-start
  38.7 24.9 %all_to_all.49 = bf16[8,128,512]{2,1,0:T(8,128)(2,1)S(1)} all-to-all(bf16[8,128,512]{2,1,0:T(8,128)(2,1)S(1)} %bitcast.21), channel_id=1, replica_groups={{0,32,2,34,1,33,3,35},{4,36,6,38,5,37,7,39},{8,40,10,42,9,41,11,43},{12..., dimensions={0} | all-to-all | bytes 2097152 | tf_op jit(solution)/shard_map/all_to_all | solution.py:41
  63.6 0.1 reduce_sum.34
  63.8 21.7 %all_to_all.50 = bf16[32,16,128]{2,1,0:T(8,128)(2,1)S(1)} all-to-all(bf16[32,16,128]{2,1,0:T(8,128)(2,1)S(1)} %bitcast.23), channel_id=1, replica_groups={{0,64,128,192,4,68,132,196,8,72,136,200,12,76,140,204,256,320,384,448,2..., dimensions={0} | all-to-all | bytes 262144 | tf_op jit(solution)/shard_map/all_to_all | solution.py:41
  85.5 0.7 broadcast_in_dim.13
  86.2 4.1 %all-to-all-start.3 = ((bf16[32,16,128]{2,1,0:T(8,128)(2,1)}), bf16[32,16,128]{2,1,0:T(8,128)(2,1)S(1)}, u32[]{:S(2)}, u32[]{:S(2)}) async-start(bf16[32,16,128]{2,1,0:T(8,128)(2,1)} %broadcast_in_dim.13), calls=%async_computation.3 | async-start | bytes 262144 | tf_op jit(solution)/shard_map/all_to_all | solution.py:41
  90.4 3.8 %collective-permute-start.4 = (f32[2,512]{1,0:T(2,128)S(1)}, f32[2,512]{1,0:T(2,128)S(1)}, u32[]{:S(2)}, u32[]{:S(2)}) collective-permute-start(f32[2,512]{1,0:T(2,128)S(1)} %get-tuple-element.45), channel_id=1, source_target_pairs={{0,1},{1,0},{2,3},{3,2},{4,5},{5,4},{6,7},{7,6},{8,9},{9,8},{10,11... | collective-permute-start | bytes 12296 | tf_op jit(solution)/shard_map/ppermute | solution.py:64
  94.1 0.7 collective-permute-start.5
  94.8 0.3 collective-permute-done.4
  95.1 0.0 collective-permute-done.5
  95.1 0.0 copy-done
  95.1 0.8 convolution_convert_fusion
  96.0 8.0 %all-to-all-done.3 = bf16[32,16,128]{2,1,0:T(8,128)(2,1)S(1)} async-done(((bf16[32,16,128]{2,1,0:T(8,128)(2,1)}), bf16[32,16,128]{2,1,0:T(8,128)(2,1)S(1)}, u32[]{:S(2)}, u32[]{:S(2)}) %all-to-all-start.3) | async-done | bytes 131104 | tf_op jit(solution)/shard_map/all_to_all | solution.py:41
  104.0 0.1 broadcast_in_dim.26
  104.0 15.4 %all_to_all.51 = bf16[8,128,512]{2,1,0:T(8,128)(2,1)S(1)} all-to-all(bf16[8,128,512]{2,1,0:T(8,128)(2,1)S(1)} %broadcast_in_dim.26), channel_id=1, replica_groups={{0,32,2,34,1,33,3,35},{4,36,6,38,5,37,7,39},{8,40,10,42,9,41,11,43},{12..., dimensions={0} | all-to-all | bytes 2097152 | tf_op jit(solution)/shard_map/all_to_all | solution.py:41
  119.4 0.1 broadcast_in_dim.28
  119.6 6.2 %all_to_all.52 = bf16[2,1024,512]{2,1,0:T(8,128)(2,1)S(1)} all-to-all(bf16[2,1024,512]{2,1,0:T(8,128)(2,1)S(1)} %broadcast_in_dim.28), channel_id=1, replica_groups={{0,16},{1,17},{2,18},{3,19},{4,20},{5,21},{6,22},{7,23},{8,24},{9,25},{..., dimensions={0} | all-to-all | bytes 4194304 | tf_op jit(solution)/shard_map/all_to_all | solution.py:41
  125.8 1.3 %copy.17 = bf16[4,512,512]{2,1,0:T(8,128)(2,1)} copy(bf16[4,512,512]{2,1,0:T(8,128)(2,1)S(1)} %bitcast.19) | data formatting | bytes 4194304
  (8 shorter events, 0.1 us)
Async XLA Ops:
  0.6 6.5 %collective-permute-start.1 = (bf16[128,512]{1,0:T(8,128)(2,1)}, bf16[128,512]{1,0:T(8,128)(2,1)S(1)}, u32[]{:S(2)}, u32[]{:S(2)}) collective-permute-start(bf16[128,512]{1,0:T(8,128)(2,1)} %bitcast.25), channel_id=1, source_target_pairs={{0,1},{1,0},{2,3},{3,2},{4,5},{5,4},{6,7},{7,6},{8,9},{9,8},{10,11... | collective-permute-start | bytes 393224 | tf_op jit(solution)/shard_map/ppermute | solution.py:64
  4.6 2.6 %collective-permute-start = (bf16[128,512]{1,0:T(8,128)(2,1)}, bf16[128,512]{1,0:T(8,128)(2,1)S(1)}, u32[]{:S(2)}, u32[]{:S(2)}) collective-permute-start(bf16[128,512]{1,0:T(8,128)(2,1)} %bitcast.26), channel_id=1, source_target_pairs={{1,2},{2,1},{3,4},{4,3},{5,6},{6,5},{7,8},{8,7},{9,10},{10,9},{11,... | collective-permute-start | bytes 393224 | tf_op jit(solution)/shard_map/ppermute | solution.py:70
  8.1 15.6 %collective-permute-start.3 = (bf16[384,512]{1,0:T(8,128)(2,1)S(1)}, bf16[384,512]{1,0:T(8,128)(2,1)S(1)}, u32[]{:S(2)}, u32[]{:S(2)}) collective-permute-start(bf16[384,512]{1,0:T(8,128)(2,1)S(1)} %pad_maximum_fusion.mid_ref), channel_id=1, source_target_pairs={{0,16},{16,0},{32,48},{48,32},{64,80},{80,64},{96,112},{112,96},{1... | collective-permute-start | bytes 1179656 | tf_op jit(solution)/shard_map/ppermute | solution.py:64
  17.4 9.1 %collective-permute-start.2 = (bf16[384,512]{1,0:T(8,128)(2,1)S(1)}, bf16[384,512]{1,0:T(8,128)(2,1)S(1)}, u32[]{:S(2)}, u32[]{:S(2)}) collective-permute-start(bf16[384,512]{1,0:T(8,128)(2,1)S(1)} %pad_maximum_fusion.mid_ref), channel_id=1, source_target_pairs={{16,32},{32,16},{48,64},{64,48},{80,96},{96,80},{112,128},{128,112... | collective-permute-start | bytes 1179656 | tf_op jit(solution)/shard_map/ppermute | solution.py:70
  38.7 56.4 %copy-start = (bf16[512,512]{1,0:T(8,128)(2,1)S(1)}, bf16[512,512]{1,0:T(8,128)(2,1)}, u32[]{:S(2)}) copy-start(bf16[512,512]{1,0:T(8,128)(2,1)} %w_top_ref.1) | copy-start | bytes 1572868
  86.2 17.7 %all-to-all-start.3 = ((bf16[32,16,128]{2,1,0:T(8,128)(2,1)}), bf16[32,16,128]{2,1,0:T(8,128)(2,1)S(1)}, u32[]{:S(2)}, u32[]{:S(2)}) async-start(bf16[32,16,128]{2,1,0:T(8,128)(2,1)} %broadcast_in_dim.13), calls=%async_computation.3 | async-start | bytes 262144 | tf_op jit(solution)/shard_map/all_to_all | solution.py:41
  90.4 4.8 %collective-permute-start.4 = (f32[2,512]{1,0:T(2,128)S(1)}, f32[2,512]{1,0:T(2,128)S(1)}, u32[]{:S(2)}, u32[]{:S(2)}) collective-permute-start(f32[2,512]{1,0:T(2,128)S(1)} %get-tuple-element.45), channel_id=1, source_target_pairs={{0,1},{1,0},{2,3},{3,2},{4,5},{5,4},{6,7},{7,6},{8,9},{9,8},{10,11... | collective-permute-start | bytes 12296 | tf_op jit(solution)/shard_map/ppermute | solution.py:64
  94.1 1.0 collective-permute-start.5
